TPU v7x, 1024 devices: a whole 4x8x16 slice. The times are simulated.
1024 devices in a mesh: elem: 32 (over y_lo, x, core), band: 32 (over z, y_hi).
Axes of the slice: x: 4, y: 8 (y_hi: 2, y_lo: 4; y = y_hi * 4 + y_lo), z: 16, core: 2. Of those that a mesh axis runs over, the one named last changes fastest.
Arguments:
- orbitals: float32 [128, 160, 1024], P('elem', 'band'), may hold values from -6 to 6
- rotation: float32 [1024, 1024], P('band'), may hold values from -0.375 to 0.375
- counts: int32 [128], P('elem'), may hold values from 96 to 160, as said below
- hamiltonian: float32 [128, 7, 160, 160], P('elem'), may hold values from -0.1875 to 0.1875
- filter_center: float32 [1], replicated, may hold values from -0.5 to 0.5
- filter_width: float32 [1], replicated, may hold values from 1.5 to 2.5
Outputs:
- filtered: float32 [128, 160, 1024], P('elem', None, 'band')
Inputs may be any that keep to these rules, and one draw needn't show every extreme that they name: `counts`: some element has exactly 96 and some exactly 160 basis functions.
All inputs are finite; a program needn't handle non-finite values.
Results may differ from a plain program's by a relative error of at most 0.0001.
Values sent between devices are 32-bit elements; how exact they have to be, the bound alone decides.
No kernel may reach another device: no remote copies, remote signals or barrier semaphores. Data moves between devices by JAX's collectives and lax.ppermute only.
A program may use at most 32 MiB of HBM per device.

v0:
```python
import jax
import jax.numpy as jnp
from jax import lax
from jax.sharding import PartitionSpec as P

GY = 8


def shifted(shard, axis, by):
    size = lax.axis_size(axis)
    return lax.ppermute(shard, axis, [(i, (i + by) % size) for i in range(size)])


def moved(field, steps):
    return shifted(field, "elem", steps)


def apply_operator(field, hamiltonian, live):
    position = lax.axis_index("elem")
    y_place = position % GY
    z_place = position // GY
    layers = lax.axis_size("elem") // GY
    zero = jnp.float32(0.0)
    y_minus = jnp.where(y_place == 0, moved(field, -(GY - 1)), moved(field, 1))
    y_plus = jnp.where(y_place == GY - 1, moved(field, GY - 1), moved(field, -1))
    z_minus = jnp.where(z_place == 0, zero, moved(field, GY))
    z_plus = jnp.where(z_place == layers - 1, zero, moved(field, -GY))
    others = [
        field,
        jnp.roll(field, 1, axis=0),
        jnp.roll(field, -1, axis=0),
        y_minus,
        y_plus,
        z_minus,
        z_plus,
    ]
    total = jnp.zeros(field.shape, jnp.float32)
    for slot in range(7):
        total = total + jnp.einsum(
            "erc,ecb->erb", hamiltonian[:, slot], others[slot], precision=lax.Precision.HIGHEST
        )
    return jnp.where(live[:, :, None], total, zero)


def shards(orbitals, rotation, counts, hamiltonian, filter_center, filter_width):
    elements, rows_here, bands = orbitals.shape
    basis = hamiltonian.shape[2]
    row_index = lax.axis_index("band") * rows_here + jnp.arange(rows_here, dtype=jnp.int32)
    masked = jnp.where(
        (row_index[None, :] < counts[:, None])[:, :, None], orbitals, jnp.float32(0.0)
    )
    by_columns = lax.all_to_all(masked, "band", split_axis=2, concat_axis=1, tiled=True)
    flat_rows = by_columns.reshape(elements * basis, by_columns.shape[2])
    summed = lax.psum_scatter(
        jnp.einsum("kb,mk->bm", rotation, flat_rows, precision=lax.Precision.HIGHEST),
        "band",
        scatter_dimension=0,
        tiled=True,
    )
    start = jnp.transpose(summed.reshape(summed.shape[0], elements, basis), (1, 2, 0))
    live = jnp.arange(basis, dtype=jnp.int32)[None, :] < counts[:, None]
    center = filter_center[0]
    width = filter_width[0]
    middle = (apply_operator(start, hamiltonian, live) - center * start) / width
    filtered = 2.0 * (apply_operator(middle, hamiltonian, live) - center * middle) / width - start
    return filtered


def solution(mesh):
    return jax.shard_map(
        shards,
        mesh=mesh,
        in_specs=(
            P("elem", "band", None),
            P("band", None),
            P("elem"),
            P("elem", None, None, None),
            P(),
            P(),
        ),
        out_specs=P("elem", None, "band"),
        check_vma=False,
    )
```

profile of v0, /device:TPU:128, one launch (start us, length us, event | category | flops | bytes accessed | tf_op | source)
XLA Modules:
  0.0 822.3 jit_solution(10145293774731951125)
XLA Ops:
  6.5 0.0 copy-start
  6.5 0.0 reduce-scatter.4.cloned.1.call-start
  6.5 0.8 broadcast_compare_fusion
  7.3 1.0 broadcast_select_fusion
  8.3 0.9 copy.61
  9.2 2.3 reshape.62
  11.4 38.2 %all_to_all.15 = f32[32,1,640]{2,1,0:T(1,128)S(1)} all-to-all(f32[32,1,640]{2,1,0:T(1,128)S(1)} %reshape.62), channel_id=1, replica_groups=mesh['elem'=32,'band'=32] {'band'}, dimensions={0} | all-to-all | bytes 163840 | tf_op jit(solution)/shard_map/all_to_all | solution.py:52
  49.7 0.5 broadcast.48
  50.2 0.8 reduce
  51.0 2.6 reshape.63
  53.6 1.1 copy.62
  54.7 0.0 copy-done
  54.8 2.2 convolution_bitcast_fusion
  56.9 0.0 copy-start.1
  57.0 0.0 slice-start
  57.0 2.1 copy.74
  59.1 0.0 reduce-scatter.4.cloned.1.call-update
  60.4 0.0 copy-done.1
  60.4 0.1 iota_compare_fusion
  60.5 687.3 %reduce-scatter.4.cloned.1.call-done = f32[32,640]{1,0:T(8,128)} async-done(((f32[1024,640]{1,0:T(8,128)}), f32[32,640]{1,0:T(8,128)}) %reduce-scatter.4.cloned.1.call-update) | async-done | bytes 81936
  747.8 1.0 copy.75
  748.8 0.2 copy.64
  749.0 2.7 collective-permute-start.5
  751.7 3.1 collective-permute-start.4
  754.9 1.9 collective-permute-start.2
  756.8 7.6 collective-permute-start.3
  764.4 0.0 slice-start.1
  764.4 2.2 collective-permute-start
  766.6 1.8 fusion.36
  768.4 1.8 convolution_add_fusion.5
  770.2 1.8 convolution_add_fusion.4
  772.0 0.0 collective-permute-done.2
  772.0 1.9 collective-permute-start.1
  773.9 0.0 collective-permute-done.3
  774.0 1.8 fusion.26
  775.8 0.0 collective-permute-done.5
  775.8 1.8 fusion.18
  777.6 0.0 collective-permute-done.4
  777.6 1.8 fusion.22
  779.4 0.0 collective-permute-done
  779.4 2.8 collective-permute-done.1
  782.2 1.8 fusion.15
  784.0 1.9 collective-permute-start.11
  785.9 3.9 collective-permute-start.10
  789.9 3.0 collective-permute-start.8
  792.9 5.1 collective-permute-start.9
  798.0 1.8 fusion.34
  799.8 2.6 collective-permute-start.6
  802.4 0.0 slice-done
  802.4 0.0 slice-done.1
  802.4 0.7 convolution_add_fusion.2
  803.2 0.7 convolution_add_fusion.1
  803.9 0.0 collective-permute-done.8
  803.9 2.3 collective-permute-start.7
  806.1 0.0 collective-permute-done.9
  806.2 0.7 fusion.24
  806.9 0.0 collective-permute-done.11
  806.9 0.7 fusion.16
  807.6 0.0 collective-permute-done.10
  807.6 0.7 fusion.20
  808.3 0.0 collective-permute-done.6
  808.3 5.7 collective-permute-done.7
  814.1 1.4 fusion.11
  (7 shorter events, 0.1 us)
Async XLA Ops:
  6.5 48.2 %copy-start = (f32[32,1024]{1,0:T(8,128)S(1)}, f32[32,1024]{1,0:T(8,128)}, u32[]{:S(2)}) copy-start(f32[32,1024]{1,0:T(8,128)} %param.7) | copy-start | bytes 393220
  6.5 741.2 %reduce-scatter.4.cloned.1.call-start = ((), (), s32[]{:S(2)}) async-start(), calls=%async_computation.2 | async-start | bytes 2703360
  56.9 3.5 copy-start.1
  57.0 745.5 %slice-start = ((s8[4587520]{0:T(1024)(128)(4,1)}), s8[393216]{0:T(1024)(128)(4,1)S(1)}, s32[]{:S(2)}) async-start(s8[4587520]{0:T(1024)(128)(4,1)} %bitcast.87), calls=%async_computation.3 | async-start | bytes 786432
  749.0 26.8 %collective-permute-start.5 = (f32[4,160,32]{1,2,0:T(8,128)S(1)}, f32[4,160,32]{1,2,0:T(8,128)S(1)}, u32[]{:S(2)}, u32[]{:S(2)}) collective-permute-start(f32[4,160,32]{1,2,0:T(8,128)S(1)} %bitcast.91), channel_id=1, source_target_pairs={{0,768},{32,800},{64,832},{96,864},{128,896},{160,928},{192,960},{... | collective-permute-start | bytes 245768 | tf_op jit(solution)/shard_map/ppermute | solution.py:11
  751.7 25.9 %collective-permute-start.4 = (f32[4,160,32]{1,2,0:T(8,128)S(1)}, f32[4,160,32]{1,2,0:T(8,128)S(1)}, u32[]{:S(2)}, u32[]{:S(2)}) collective-permute-start(f32[4,160,32]{1,2,0:T(8,128)S(1)} %bitcast.92), channel_id=1, source_target_pairs={{0,256},{32,288},{64,320},{96,352},{128,384},{160,416},{192,448},{... | collective-permute-start | bytes 245768 | tf_op jit(solution)/shard_map/ppermute | solution.py:11
  754.9 17.1 %collective-permute-start.2 = (f32[4,160,32]{1,2,0:T(8,128)S(1)}, f32[4,160,32]{1,2,0:T(8,128)S(1)}, u32[]{:S(2)}, u32[]{:S(2)}) collective-permute-start(f32[4,160,32]{1,2,0:T(8,128)S(1)} %bitcast.93), channel_id=1, source_target_pairs={{0,224},{32,256},{64,288},{96,320},{128,352},{160,384},{192,416},{... | collective-permute-start | bytes 245768 | tf_op jit(solution)/shard_map/ppermute | solution.py:11
  756.8 17.2 %collective-permute-start.3 = (f32[4,160,32]{1,2,0:T(8,128)S(1)}, f32[4,160,32]{1,2,0:T(8,128)S(1)}, u32[]{:S(2)}, u32[]{:S(2)}) collective-permute-start(f32[4,160,32]{1,2,0:T(8,128)S(1)} %bitcast.94), channel_id=1, source_target_pairs={{0,992},{32,0},{64,32},{96,64},{128,96},{160,128},{192,160},{224,1... | collective-permute-start | bytes 245768 | tf_op jit(solution)/shard_map/ppermute | solution.py:11
  764.4 38.1 %slice-start.1 = ((s8[4587520]{0:T(1024)(128)(4,1)}), s8[4194304]{0:T(1024)(128)(4,1)S(1)}, s32[]{:S(2)}) async-start(s8[4587520]{0:T(1024)(128)(4,1)} %bitcast.87), calls=%async_computation.4 | async-start | bytes 8388608
  764.4 15.0 %collective-permute-start = (f32[4,160,32]{1,2,0:T(8,128)S(1)}, f32[4,160,32]{1,2,0:T(8,128)S(1)}, u32[]{:S(2)}, u32[]{:S(2)}) collective-permute-start(f32[4,160,32]{1,2,0:T(8,128)S(1)} %bitcast.97), channel_id=1, source_target_pairs={{0,800},{32,832},{64,864},{96,896},{128,928},{160,960},{192,992},{... | collective-permute-start | bytes 245768 | tf_op jit(solution)/shard_map/ppermute | solution.py:11
  772.0 10.2 %collective-permute-start.1 = (f32[4,160,32]{1,2,0:T(8,128)S(1)}, f32[4,160,32]{1,2,0:T(8,128)S(1)}, u32[]{:S(2)}, u32[]{:S(2)}) collective-permute-start(f32[4,160,32]{1,2,0:T(8,128)S(1)} %bitcast.98), channel_id=1, source_target_pairs={{0,32},{32,64},{64,96},{96,128},{128,160},{160,192},{192,224},{224... | collective-permute-start | bytes 245768 | tf_op jit(solution)/shard_map/ppermute | solution.py:11
  784.0 22.9 %collective-permute-start.11 = (f32[4,160,32]{1,2,0:T(8,128)S(1)}, f32[4,160,32]{1,2,0:T(8,128)S(1)}, u32[]{:S(2)}, u32[]{:S(2)}) collective-permute-start(f32[4,160,32]{1,2,0:T(8,128)S(1)} %fusion.15), channel_id=1, source_target_pairs={{0,768},{32,800},{64,832},{96,864},{128,896},{160,928},{192,960},{... | collective-permute-start | bytes 245768 | tf_op jit(solution)/shard_map/ppermute | solution.py:11
  785.9 21.6 %collective-permute-start.10 = (f32[4,160,32]{1,2,0:T(8,128)S(1)}, f32[4,160,32]{1,2,0:T(8,128)S(1)}, u32[]{:S(2)}, u32[]{:S(2)}) collective-permute-start(f32[4,160,32]{1,2,0:T(8,128)S(1)} %fusion.15), channel_id=1, source_target_pairs={{0,256},{32,288},{64,320},{96,352},{128,384},{160,416},{192,448},{... | collective-permute-start | bytes 245768 | tf_op jit(solution)/shard_map/ppermute | solution.py:11
  789.9 14.0 %collective-permute-start.8 = (f32[4,160,32]{1,2,0:T(8,128)S(1)}, f32[4,160,32]{1,2,0:T(8,128)S(1)}, u32[]{:S(2)}, u32[]{:S(2)}) collective-permute-start(f32[4,160,32]{1,2,0:T(8,128)S(1)} %fusion.15), channel_id=1, source_target_pairs={{0,224},{32,256},{64,288},{96,320},{128,352},{160,384},{192,416},{... | collective-permute-start | bytes 245768 | tf_op jit(solution)/shard_map/ppermute | solution.py:11
  792.9 13.2 %collective-permute-start.9 = (f32[4,160,32]{1,2,0:T(8,128)S(1)}, f32[4,160,32]{1,2,0:T(8,128)S(1)}, u32[]{:S(2)}, u32[]{:S(2)}) collective-permute-start(f32[4,160,32]{1,2,0:T(8,128)S(1)} %fusion.15), channel_id=1, source_target_pairs={{0,992},{32,0},{64,32},{96,64},{128,96},{160,128},{192,160},{224,1... | collective-permute-start | bytes 245768 | tf_op jit(solution)/shard_map/ppermute | solution.py:11
  799.8 8.5 %collective-permute-start.6 = (f32[4,160,32]{1,2,0:T(8,128)S(1)}, f32[4,160,32]{1,2,0:T(8,128)S(1)}, u32[]{:S(2)}, u32[]{:S(2)}) collective-permute-start(f32[4,160,32]{1,2,0:T(8,128)S(1)} %fusion.15), channel_id=1, source_target_pairs={{0,800},{32,832},{64,864},{96,896},{128,928},{160,960},{192,992},{... | collective-permute-start | bytes 245768 | tf_op jit(solution)/shard_map/ppermute | solution.py:11
  803.9 10.2 %collective-permute-start.7 = (f32[4,160,32]{1,2,0:T(8,128)S(1)}, f32[4,160,32]{1,2,0:T(8,128)S(1)}, u32[]{:S(2)}, u32[]{:S(2)}) collective-permute-start(f32[4,160,32]{1,2,0:T(8,128)S(1)} %fusion.15), channel_id=1, source_target_pairs={{0,32},{32,64},{64,96},{96,128},{128,160},{160,192},{192,224},{224... | collective-permute-start | bytes 245768 | tf_op jit(solution)/shard_map/ppermute | solution.py:11
Sparse Core Ops, SparseCore 0:
  59.2 688.5 reduce-scatter.3
where the time goes:
time: 824 us; the launch traced here: 822 us
  waiting for transfers between devices  696 us (84%)
  starting transfers between devices  38.2 us (5%)
  blocking collectives  38.2 us (5%)
  matrix products  21.5 us (3%)
  between operations  15.2 us (2%)
  local copies, waits for them, and re-layouts  10.7 us (1%)
    unnamed x2, waiting for transfers between devices  687 us
    all_to_all x1, blocking collectives, shards(): lax.all_to_all(masked, 'band', split_axis=2, concat_axis=1, tiled=True)  38.2 us
    ppermute x12, starting transfers between devices, shifted(): lax.ppermute(shard, axis, [(i, (i + by) % size) for i in range(size)])  38.2 us
    dot_general x14, matrix products, apply_operator(): jnp.einsum('erc,ecb->erb', hamiltonian[:, slot], others[slot], precision=...  19.3 us
  transfers between devices with their start and end apart: 13, of which 3 were waited for; matrix products, arithmetic and copies ran while one was open for 2% of the time, Pallas kernels for 0%

commit v1 on v0

v1 whole, which is shorter than its diff:
```python
import jax
import jax.numpy as jnp
from jax import lax
from jax.experimental import pallas as pl
from jax.experimental.pallas import tpu as pltpu
from jax.sharding import Mesh
from jax.sharding import PartitionSpec as P

LAYERS, COLUMNS, CORES = 4, 4, 2
FAR, NEAR = 4, 8
ELEMS, ROWS, WIDE = 4, 160, 128
BANDS = 32
PIECE = 5
ELEM = ("layer", "column", "core")
RING = ("column", "core")
NEARS = ("z_lo", "y_hi")
BAND = ("z_hi",) + NEARS
F32, BF16 = jnp.float32, jnp.bfloat16


def call(kernel, out, flops, moved, spaces):
    return pl.pallas_call(
        kernel,
        out_shape=jax.ShapeDtypeStruct(out, F32),
        in_specs=[pl.BlockSpec(memory_space=s) for s in spaces],
        out_specs=pl.BlockSpec(memory_space=pltpu.VMEM),
        compiler_params=pltpu.CompilerParams(vmem_limit_bytes=32 << 20),
        cost_estimate=pl.CostEstimate(flops=flops, bytes_accessed=moved, transcendentals=0),
    )


def split(v):
    high = v.astype(BF16)
    return high, (v - high.astype(F32)).astype(BF16)


def dot3(a, b):
    def dot(x, y):
        return jnp.dot(x, y, preferred_element_type=F32)

    return dot(a[0], b[0]) + (dot(a[0], b[1]) + dot(a[1], b[0]))


def lane_owner(shape):
    return lax.broadcasted_iota(jnp.int32, shape, len(shape) - 1) // BANDS


def by_owner(parts):
    owner = lane_owner(parts[0].shape)
    picked = parts[0]
    for e in range(1, ELEMS):
        picked = jnp.where(owner == e, parts[e], picked)
    return picked


def turned(v, by):
    by = by % ELEMS
    return pltpu.roll(v, by * BANDS, 1) if by else v


def alive(counts_ref):
    owner = lane_owner((ROWS, WIDE))
    row = lax.broadcasted_iota(jnp.int32, (ROWS, WIDE), 0)
    limit = jnp.full((ROWS, WIDE), counts_ref[0], jnp.int32)
    for e in range(1, ELEMS):
        limit = jnp.where(owner == e, counts_ref[e], limit)
    return row < limit


def cut_columns(orbitals_ref, out_ref):
    for i in range(PIECE):
        for near in range(NEAR):
            half, place = divmod(near, ELEMS)
            parts = [
                turned(orbitals_ref[i, :, pl.ds(256 * far + 128 * half, 128)], far - place)
                for far in range(FAR)
            ]
            out_ref[near, pl.ds(ELEMS * i, ELEMS), :] = by_owner(parts)


def pack(rows_ref, rotation_ref, out_ref):
    for e in range(ELEMS):
        for near in range(NEAR):
            for i in range(PIECE):
                out_ref[0, pl.ds(40 * e + PIECE * near + i, 1), :] = rows_ref[near, pl.ds(ELEMS * i + e, 1), :]
    rows = out_ref[0, :ROWS, :]
    for far in range(FAR):
        if far:
            out_ref[far, :ROWS, :] = rows
        out_ref[far, ROWS : ROWS + 32, :] = rotation_ref[:, pl.ds(256 * far, 128)]
        out_ref[far, ROWS + 32 :, :] = rotation_ref[:, pl.ds(256 * far + 128, 128)]


def rotate(packed_ref, out_ref):
    left = jnp.concatenate([packed_ref[far, ROWS : ROWS + 32, :] for far in range(FAR)], axis=0)
    right = jnp.concatenate([packed_ref[far, ROWS + 32 :, :] for far in range(FAR)], axis=0)
    halves = [split(left), split(right)]
    products = []
    for e in range(ELEMS):
        rows = jnp.concatenate([packed_ref[far, 40 * e : 40 * e + 40, :] for far in range(FAR)], axis=0)
        rows = split(rows)
        products.append([dot3(rows, half) for half in halves])
    for near in range(NEAR):
        half, place = divmod(near, ELEMS)
        out_ref[near] = by_owner([turned(products[e][half], e - place) for e in range(ELEMS)])


def add_up(parts_ref, counts_ref, out_ref):
    total = parts_ref[0]
    for near in range(1, NEAR):
        total = total + parts_ref[near]
    out_ref[...] = jnp.where(alive(counts_ref), total, 0.0)


def blocks_times(hamiltonian_ref, slots, fields):
    fields = [split(f) for f in fields]
    totals = []
    for e in range(ELEMS):
        total = None
        for slot, field in zip(slots, fields):
            term = dot3(split(hamiltonian_ref[e, slot]), field)
            total = term if total is None else total + term
        totals.append(total)
    return by_owner(totals)


def own_slots(field_ref, hamiltonian_ref, out_ref):
    field = field_ref[...]
    out_ref[...] = blocks_times(hamiltonian_ref, (0, 1, 2), (field, turned(field, 1), turned(field, -1)))


def first_step(own_ref, a_ref, b_ref, c_ref, d_ref, hamiltonian_ref, start_ref, counts_ref, center_ref, width_ref, out_ref):
    total = own_ref[...] + blocks_times(
        hamiltonian_ref, (3, 4, 5, 6), (a_ref[...], b_ref[...], c_ref[...], d_ref[...])
    )
    total = jnp.where(alive(counts_ref), total, 0.0)
    out_ref[...] = (total - center_ref[0] * start_ref[...]) / width_ref[0]


def second_step(own_ref, a_ref, b_ref, c_ref, d_ref, hamiltonian_ref, middle_ref, start_ref, counts_ref, center_ref, width_ref, out_ref):
    total = own_ref[...] + blocks_times(
        hamiltonian_ref, (3, 4, 5, 6), (a_ref[...], b_ref[...], c_ref[...], d_ref[...])
    )
    total = jnp.where(alive(counts_ref), total, 0.0)
    filtered = 2.0 * (total - center_ref[0] * middle_ref[...]) / width_ref[0] - start_ref[...]
    out_ref[...] = jnp.transpose(filtered)


def neighbours(field):
    ring = COLUMNS * CORES
    return (
        lax.ppermute(field, RING, [(i, (i + 1) % ring) for i in range(ring)]),
        lax.ppermute(field, RING, [(i, (i - 1) % ring) for i in range(ring)]),
        lax.ppermute(field, "layer", [(i, i + 1) for i in range(LAYERS - 1)]),
        lax.ppermute(field, "layer", [(i + 1, i) for i in range(LAYERS - 1)]),
    )


V, S = pltpu.VMEM, pltpu.SMEM
FIELD = ROWS * WIDE * 4
BLOCKS = ELEMS * 7 * ROWS * 256 * 4


def shards(orbitals, rotation, counts, hamiltonian, center, width):
    pieces = jnp.transpose(orbitals, (1, 0, 2))
    cut = call(cut_columns, (NEAR, ELEMS * PIECE, WIDE), 0, 2 * FIELD, (V,))(pieces)
    cut = lax.all_to_all(cut, NEARS, split_axis=0, concat_axis=0, tiled=True)
    packed = call(pack, (FAR, ROWS + 64, WIDE), 0, 6 * FIELD, (V, V))(cut, rotation)
    packed = lax.all_to_all(packed, "z_hi", split_axis=0, concat_axis=0, tiled=True)
    parts = call(rotate, (NEAR, ROWS, WIDE), 6 * 640 * 128 * 256, 13 * FIELD, (V,))(packed)
    parts = lax.all_to_all(parts, NEARS, split_axis=0, concat_axis=0, tiled=True)
    start = call(add_up, (ROWS, WIDE), 0, 9 * FIELD, (V, S))(parts, counts)

    own = call(own_slots, (ROWS, WIDE), 6 * 12 * ROWS * ROWS * WIDE, BLOCKS, (V, V))
    first = call(first_step, (ROWS, WIDE), 6 * 16 * ROWS * ROWS * WIDE, BLOCKS, (V,) * 7 + (S,) * 3)
    second = call(second_step, (WIDE, ROWS), 6 * 16 * ROWS * ROWS * WIDE, BLOCKS, (V,) * 8 + (S,) * 3)
    around = neighbours(start)
    middle = first(own(start, hamiltonian), *around, hamiltonian, start, counts, center, width)
    around = neighbours(middle)
    filtered = second(own(middle, hamiltonian), *around, hamiltonian, middle, start, counts, center, width)
    return jnp.transpose(filtered.reshape(ELEMS, BANDS, ROWS), (0, 2, 1))


def solution(mesh):
    inner = Mesh(
        mesh.devices.reshape(LAYERS, COLUMNS, CORES, FAR, NEAR // 2, 2), ELEM + BAND
    )
    return jax.shard_map(
        shards,
        mesh=inner,
        in_specs=(P(ELEM, BAND, None), P(BAND, None), P(ELEM), P(ELEM, None, None, None), P(), P()),
        out_specs=P(ELEM, None, BAND),
        check_vma=False,
    )
```

time: 824 us -> 123 us (0.15)
  the two profiles are of different devices: /device:TPU:128 before, /device:TPU:8 now
where the time goes in v1:
time: 123 us; the launch traced here: 122 us
  blocking collectives  90.1 us (73%)
  starting transfers between devices  17.6 us (14%)
  Pallas kernels  7.65 us (6%)
  waiting for transfers between devices  2.98 us (2%)
  local copies, waits for them, and re-layouts  2.6 us (2%)
  between operations  1.45 us (1%)
    all_to_all x1, blocking collectives, shards(): lax.all_to_all(packed, 'z_hi', split_axis=0, concat_axis=0, tiled=True)  38.5 us
    all_to_all x1, blocking collectives, shards(): lax.all_to_all(parts, NEARS, split_axis=0, concat_axis=0, tiled=True)  29.1 us
    all_to_all x1, blocking collectives, shards(): cut = lax.all_to_all(cut, NEARS, split_axis=0, concat_axis=0, tiled=True)  22.6 us
    ppermute x2, starting transfers between devices, neighbours(): lax.ppermute(field, 'layer', [(i + 1, i) for i in range(LAYERS - 1)])  6.47 us
    ppermute x2, starting transfers between devices, neighbours(): lax.ppermute(field, RING, [(i, (i - 1) % ring) for i in range(ring)])  5.89 us
    ppermute x2, starting transfers between devices, neighbours(): lax.ppermute(field, 'layer', [(i, i + 1) for i in range(LAYERS - 1)])  5.19 us
    ppermute x2, waiting for transfers between devices, neighbours(): lax.ppermute(field, 'layer', [(i + 1, i) for i in range(LAYERS - 1)])  2.97 us
    unnamed x8, local copies, waits for them, and re-layouts  2.6 us
  transfers between devices with their start and end apart: 8, of which 2 were waited for; matrix products, arithmetic and copies ran while one was open for 0% of the time, Pallas kernels for 1%

profile of v1, /device:TPU:8, one launch (start us, length us, event | category | flops | bytes accessed | tf_op | source)
XLA Modules:
  0.0 122.4 jit_solution(9221063419954708191)
XLA Ops:
  0.0 0.0 copy-start
  0.0 0.0 copy-start.2
  0.0 1.0 copy-done.2
  1.0 0.2 shard_map.64
  1.2 22.6 %all_to_all.15.rows_ref = f32[8,20,128]{2,1,0:T(8,128)S(1)} all-to-all(f32[8,20,128]{2,1,0:T(8,128)S(1)} %shard_map.64), channel_id=1, replica_groups=mesh['layer'=4,'column'=4,'core'=2,'z_hi'=4,'z_lo'=4,'y_hi'=2] {'z_lo','..., dimensions={0} | all-to-all | bytes 163840 | tf_op jit(solution)/shard_map/all_to_all | solution.py:167
  23.8 0.0 copy-start.1
  23.8 0.9 copy-done.1
  24.7 0.1 shard_map.65
  24.8 38.5 %all_to_all.16.packed_ref = f32[4,224,128]{2,1,0:T(8,128)S(1)} all-to-all(f32[4,224,128]{2,1,0:T(8,128)S(1)} %shard_map.65), channel_id=1, replica_groups=mesh['layer'=4,'column'=4,'core'=2,'z_hi'=4,'z_lo'=4,'y_hi'=2] {'z_hi'}, dimensions={0} | all-to-all | bytes 917504 | tf_op jit(solution)/shard_map/all_to_all | solution.py:169
  63.3 0.8 shard_map.66
  64.0 29.1 %all_to_all.17.parts_ref = f32[8,160,128]{2,1,0:T(8,128)S(1)} all-to-all(f32[8,160,128]{2,1,0:T(8,128)S(1)} %shard_map.66), channel_id=1, replica_groups=mesh['layer'=4,'column'=4,'core'=2,'z_hi'=4,'z_lo'=4,'y_hi'=2] {'z_lo','..., dimensions={0} | all-to-all | bytes 1310720 | tf_op jit(solution)/shard_map/all_to_all | solution.py:171
  93.1 0.0 copy-start.3
  93.1 0.7 copy-done.3
  93.8 0.6 shard_map.67.field_ref.start_ref
  94.3 0.0 collective-permute-start
  94.4 2.9 %collective-permute-start.1 = (f32[160,128]{1,0:T(8,128)S(1)}, f32[160,128]{1,0:T(8,128)S(1)}, u32[]{:S(2)}, u32[]{:S(2)}) collective-permute-start(f32[160,128]{1,0:T(8,128)S(1)} %shard_map.67.field_ref.start_ref), channel_id=1, source_target_pairs={{0,224},{32,0},{64,32},{96,64},{128,96},{160,128},{192,160},{224,1... | collective-permute-start | bytes 245768 | tf_op jit(solution)/shard_map/ppermute | solution.py:153
  97.3 2.7 %collective-permute-start.2 = (f32[160,128]{1,0:T(8,128)S(1)}, f32[160,128]{1,0:T(8,128)S(1)}, u32[]{:S(2)}, u32[]{:S(2)}) collective-permute-start(f32[160,128]{1,0:T(8,128)S(1)} %shard_map.67.field_ref.start_ref), channel_id=1, source_target_pairs={{0,256},{256,512},{512,768},{1,257},{257,513},{513,769},{2,258},{2... | collective-permute-start | bytes 245768 | tf_op jit(solution)/shard_map/ppermute | solution.py:154
  100.1 3.1 %collective-permute-start.3 = (f32[160,128]{1,0:T(8,128)S(1)}, f32[160,128]{1,0:T(8,128)S(1)}, u32[]{:S(2)}, u32[]{:S(2)}) collective-permute-start(f32[160,128]{1,0:T(8,128)S(1)} %shard_map.67.field_ref.start_ref), channel_id=1, source_target_pairs={{256,0},{512,256},{768,512},{257,1},{513,257},{769,513},{258,2},{5... | collective-permute-start | bytes 245768 | tf_op jit(solution)/shard_map/ppermute | solution.py:155
  104.5 0.0 copy-done
  104.5 0.9 shard_map.68.own_ref
  105.4 0.0 collective-permute-done.a_ref
  105.4 0.0 collective-permute-done.1.b_ref
  105.4 0.0 collective-permute-done.2.c_ref
  105.4 1.0 collective-permute-done.3.d_ref
  106.4 1.7 %shard_map.69.field_ref.middle_ref = f32[160,128]{1,0:T(8,128)S(1)} custom-call(f32[160,128]{1,0:T(8,128)S(1)} %shard_map.68.own_ref, f32[160,128]{1,0:T(8,128)S(1)} %collective-permute-done.a_ref, f32[160,128]{1,0:T(8,128)S(1)} %collective-permute-done.1.b_ref, f32[160,128]{1,0:T(8,128)S(1)} %collective-permute-done.2.c_ref, ...), custom_call_target="tpu_custom_call" | custom-call | flops 314572800 | bytes 4587520 | tf_op jit(solution)/shard_map/pallas_call | solution.py:178
  108.1 0.0 collective-permute-start.4
  108.2 2.9 %collective-permute-start.5 = (f32[160,128]{1,0:T(8,128)S(1)}, f32[160,128]{1,0:T(8,128)S(1)}, u32[]{:S(2)}, u32[]{:S(2)}) collective-permute-start(f32[160,128]{1,0:T(8,128)S(1)} %shard_map.69.field_ref.middle_ref), channel_id=1, source_target_pairs={{0,224},{32,0},{64,32},{96,64},{128,96},{160,128},{192,160},{224,1... | collective-permute-start | bytes 245768 | tf_op jit(solution)/shard_map/ppermute | solution.py:153
  111.1 2.4 %collective-permute-start.6 = (f32[160,128]{1,0:T(8,128)S(1)}, f32[160,128]{1,0:T(8,128)S(1)}, u32[]{:S(2)}, u32[]{:S(2)}) collective-permute-start(f32[160,128]{1,0:T(8,128)S(1)} %shard_map.69.field_ref.middle_ref), channel_id=1, source_target_pairs={{0,256},{256,512},{512,768},{1,257},{257,513},{513,769},{2,258},{2... | collective-permute-start | bytes 245768 | tf_op jit(solution)/shard_map/ppermute | solution.py:154
  113.6 3.4 %collective-permute-start.7 = (f32[160,128]{1,0:T(8,128)S(1)}, f32[160,128]{1,0:T(8,128)S(1)}, u32[]{:S(2)}, u32[]{:S(2)}) collective-permute-start(f32[160,128]{1,0:T(8,128)S(1)} %shard_map.69.field_ref.middle_ref), channel_id=1, source_target_pairs={{256,0},{512,256},{768,512},{257,1},{513,257},{769,513},{258,2},{5... | collective-permute-start | bytes 245768 | tf_op jit(solution)/shard_map/ppermute | solution.py:155
  116.9 0.9 shard_map.70.own_ref
  117.9 0.0 collective-permute-done.4.a_ref
  117.9 0.0 collective-permute-done.5.b_ref
  117.9 0.0 collective-permute-done.6.c_ref
  117.9 2.0 %collective-permute-done.7.d_ref = f32[160,128]{1,0:T(8,128)S(1)} collective-permute-done((f32[160,128]{1,0:T(8,128)S(1)}, f32[160,128]{1,0:T(8,128)S(1)}, u32[]{:S(2)}, u32[]{:S(2)}) %collective-permute-start.7) | collective-permute-done | bytes 81952 | tf_op jit(solution)/shard_map/ppermute | solution.py:155
  119.9 2.5 %shard_map.71 = f32[128,160]{1,0:T(8,128)} custom-call(f32[160,128]{1,0:T(8,128)S(1)} %shard_map.70.own_ref, f32[160,128]{1,0:T(8,128)S(1)} %collective-permute-done.4.a_ref, f32[160,128]{1,0:T(8,128)S(1)} %collective-permute-done.5.b_ref, f32[160,128]{1,0:T(8,128)S(1)} %collective-permute-done.6.c_ref, f32[160,128]{1,0:T(8,128)S(1)} %collective-permute-done.7.d_ref, ...), custom_call_target="tpu_custom_call" | custom-call | flops 314572800 | bytes 4587520 | tf_op jit(solution)/shard_map/pallas_call | solution.py:180
Async XLA Ops:
  0.0 104.5 %copy-start = (f32[4,7,160,160]{3,2,1,0:T(8,128)S(1)}, f32[4,7,160,160]{3,2,1,0:T(8,128)}, u32[]{:S(2)}) copy-start(f32[4,7,160,160]{3,2,1,0:T(8,128)} %hamiltonian_ref.7) | copy-start | bytes 8601604
  0.0 1.0 copy-start.2
  23.8 0.9 copy-start.1
  93.1 0.7 copy-start.3
  94.3 11.1 %collective-permute-start = (f32[160,128]{1,0:T(8,128)S(1)}, f32[160,128]{1,0:T(8,128)S(1)}, u32[]{:S(2)}, u32[]{:S(2)}) collective-permute-start(f32[160,128]{1,0:T(8,128)S(1)} %shard_map.67.field_ref.start_ref), channel_id=1, source_target_pairs={{0,32},{32,64},{64,96},{96,128},{128,160},{160,192},{192,224},{224... | collective-permute-start | bytes 245768 | tf_op jit(solution)/shard_map/ppermute | solution.py:152
  94.4 11.0 %collective-permute-start.1 = (f32[160,128]{1,0:T(8,128)S(1)}, f32[160,128]{1,0:T(8,128)S(1)}, u32[]{:S(2)}, u32[]{:S(2)}) collective-permute-start(f32[160,128]{1,0:T(8,128)S(1)} %shard_map.67.field_ref.start_ref), channel_id=1, source_target_pairs={{0,224},{32,0},{64,32},{96,64},{128,96},{160,128},{192,160},{224,1... | collective-permute-start | bytes 245768 | tf_op jit(solution)/shard_map/ppermute | solution.py:153
  97.3 8.1 %collective-permute-start.2 = (f32[160,128]{1,0:T(8,128)S(1)}, f32[160,128]{1,0:T(8,128)S(1)}, u32[]{:S(2)}, u32[]{:S(2)}) collective-permute-start(f32[160,128]{1,0:T(8,128)S(1)} %shard_map.67.field_ref.start_ref), channel_id=1, source_target_pairs={{0,256},{256,512},{512,768},{1,257},{257,513},{513,769},{2,258},{2... | collective-permute-start | bytes 245768 | tf_op jit(solution)/shard_map/ppermute | solution.py:154
  100.1 6.3 %collective-permute-start.3 = (f32[160,128]{1,0:T(8,128)S(1)}, f32[160,128]{1,0:T(8,128)S(1)}, u32[]{:S(2)}, u32[]{:S(2)}) collective-permute-start(f32[160,128]{1,0:T(8,128)S(1)} %shard_map.67.field_ref.start_ref), channel_id=1, source_target_pairs={{256,0},{512,256},{768,512},{257,1},{513,257},{769,513},{258,2},{5... | collective-permute-start | bytes 245768 | tf_op jit(solution)/shard_map/ppermute | solution.py:155
  108.1 9.7 %collective-permute-start.4 = (f32[160,128]{1,0:T(8,128)S(1)}, f32[160,128]{1,0:T(8,128)S(1)}, u32[]{:S(2)}, u32[]{:S(2)}) collective-permute-start(f32[160,128]{1,0:T(8,128)S(1)} %shard_map.69.field_ref.middle_ref), channel_id=1, source_target_pairs={{0,32},{32,64},{64,96},{96,128},{128,160},{160,192},{192,224},{224... | collective-permute-start | bytes 245768 | tf_op jit(solution)/shard_map/ppermute | solution.py:152
  108.2 9.7 %collective-permute-start.5 = (f32[160,128]{1,0:T(8,128)S(1)}, f32[160,128]{1,0:T(8,128)S(1)}, u32[]{:S(2)}, u32[]{:S(2)}) collective-permute-start(f32[160,128]{1,0:T(8,128)S(1)} %shard_map.69.field_ref.middle_ref), channel_id=1, source_target_pairs={{0,224},{32,0},{64,32},{96,64},{128,96},{160,128},{192,160},{224,1... | collective-permute-start | bytes 245768 | tf_op jit(solution)/shard_map/ppermute | solution.py:153
  111.1 6.8 %collective-permute-start.6 = (f32[160,128]{1,0:T(8,128)S(1)}, f32[160,128]{1,0:T(8,128)S(1)}, u32[]{:S(2)}, u32[]{:S(2)}) collective-permute-start(f32[160,128]{1,0:T(8,128)S(1)} %shard_map.69.field_ref.middle_ref), channel_id=1, source_target_pairs={{0,256},{256,512},{512,768},{1,257},{257,513},{513,769},{2,258},{2... | collective-permute-start | bytes 245768 | tf_op jit(solution)/shard_map/ppermute | solution.py:154
  113.6 6.3 %collective-permute-start.7 = (f32[160,128]{1,0:T(8,128)S(1)}, f32[160,128]{1,0:T(8,128)S(1)}, u32[]{:S(2)}, u32[]{:S(2)}) collective-permute-start(f32[160,128]{1,0:T(8,128)S(1)} %shard_map.69.field_ref.middle_ref), channel_id=1, source_target_pairs={{256,0},{512,256},{768,512},{257,1},{513,257},{769,513},{258,2},{5... | collective-permute-start | bytes 245768 | tf_op jit(solution)/shard_map/ppermute | solution.py:155

commit v2 on v1

--- a/solution.py
+++ b/solution.py
@@ -19,11 +19,14 @@
 
 
 def call(kernel, out, flops, moved, spaces):
+    several = isinstance(out[0], tuple)
+    shapes = tuple(jax.ShapeDtypeStruct(o, F32) for o in (out if several else (out,)))
+    specs = tuple(pl.BlockSpec(memory_space=pltpu.VMEM) for _ in shapes)
     return pl.pallas_call(
         kernel,
-        out_shape=jax.ShapeDtypeStruct(out, F32),
+        out_shape=shapes if several else shapes[0],
         in_specs=[pl.BlockSpec(memory_space=s) for s in spaces],
-        out_specs=pl.BlockSpec(memory_space=pltpu.VMEM),
+        out_specs=specs if several else specs[0],
         compiler_params=pltpu.CompilerParams(vmem_limit_bytes=32 << 20),
         cost_estimate=pl.CostEstimate(flops=flops, bytes_accessed=moved, transcendentals=0),
     )
@@ -67,7 +70,11 @@
     return row < limit
 
 
-def cut_columns(orbitals_ref, out_ref):
+def cut_columns(orbitals_ref, rotation_ref, counts_ref, out_ref, slices_ref, live_ref):
+    live_ref[...] = jnp.where(alive(counts_ref), 1.0, 0.0)
+    for far in range(FAR):
+        for half in range(2):
+            slices_ref[far, pl.ds(32 * half, 32), :] = rotation_ref[:, pl.ds(256 * far + 128 * half, 128)]
     for i in range(PIECE):
         for near in range(NEAR):
             half, place = divmod(near, ELEMS)
@@ -78,7 +85,7 @@
             out_ref[near, pl.ds(ELEMS * i, ELEMS), :] = by_owner(parts)
 
 
-def pack(rows_ref, rotation_ref, out_ref):
+def pack(rows_ref, slices_ref, out_ref):
     for e in range(ELEMS):
         for near in range(NEAR):
             for i in range(PIECE):
@@ -87,8 +94,7 @@
     for far in range(FAR):
         if far:
             out_ref[far, :ROWS, :] = rows
-        out_ref[far, ROWS : ROWS + 32, :] = rotation_ref[:, pl.ds(256 * far, 128)]
-        out_ref[far, ROWS + 32 :, :] = rotation_ref[:, pl.ds(256 * far + 128, 128)]
+        out_ref[far, ROWS:, :] = slices_ref[far]
 
 
 def rotate(packed_ref, out_ref):
@@ -105,43 +111,50 @@
         out_ref[near] = by_owner([turned(products[e][half], e - place) for e in range(ELEMS)])
 
 
-def add_up(parts_ref, counts_ref, out_ref):
+def add_up(parts_ref, live_ref, out_ref):
     total = parts_ref[0]
     for near in range(1, NEAR):
         total = total + parts_ref[near]
-    out_ref[...] = jnp.where(alive(counts_ref), total, 0.0)
+    out_ref[...] = jnp.where(live_ref[...] > 0.5, total, 0.0)
 
 
 def blocks_times(hamiltonian_ref, slots, fields):
+    def dot(x, y):
+        return jnp.dot(x, y, preferred_element_type=F32)
+
     fields = [split(f) for f in fields]
+    pairs = [jnp.concatenate(f, axis=1) for f in fields]
     totals = []
     for e in range(ELEMS):
-        total = None
-        for slot, field in zip(slots, fields):
-            term = dot3(split(hamiltonian_ref[e, slot]), field)
-            total = term if total is None else total + term
-        totals.append(total)
+        wide = narrow = None
+        for slot, field, pair in zip(slots, fields, pairs):
+            high, low = split(hamiltonian_ref[e, slot])
+            first, second = dot(high, pair), dot(low, field[0])
+            wide = first if wide is None else wide + first
+            narrow = second if narrow is None else narrow + second
+        totals.append(wide[:, :WIDE] + (wide[:, WIDE:] + narrow))
     return by_owner(totals)
 
 
-def own_slots(field_ref, hamiltonian_ref, out_ref):
+def own_and_ring(field_ref, a_ref, b_ref, hamiltonian_ref, out_ref):
     field = field_ref[...]
-    out_ref[...] = blocks_times(hamiltonian_ref, (0, 1, 2), (field, turned(field, 1), turned(field, -1)))
-
-
-def first_step(own_ref, a_ref, b_ref, c_ref, d_ref, hamiltonian_ref, start_ref, counts_ref, center_ref, width_ref, out_ref):
-    total = own_ref[...] + blocks_times(
-        hamiltonian_ref, (3, 4, 5, 6), (a_ref[...], b_ref[...], c_ref[...], d_ref[...])
-    )
-    total = jnp.where(alive(counts_ref), total, 0.0)
+    out_ref[...] = blocks_times(
+        hamiltonian_ref, range(5), (field, turned(field, 1), turned(field, -1), a_ref[...], b_ref[...])
+    )
+
+
+def applied(own_ref, c_ref, d_ref, hamiltonian_ref, live_ref):
+    total = own_ref[...] + blocks_times(hamiltonian_ref, (5, 6), (c_ref[...], d_ref[...]))
+    return jnp.where(live_ref[...] > 0.5, total, 0.0)
+
+
+def first_step(own_ref, c_ref, d_ref, hamiltonian_ref, start_ref, live_ref, center_ref, width_ref, out_ref):
+    total = applied(own_ref, c_ref, d_ref, hamiltonian_ref, live_ref)
     out_ref[...] = (total - center_ref[0] * start_ref[...]) / width_ref[0]
 
 
-def second_step(own_ref, a_ref, b_ref, c_ref, d_ref, hamiltonian_ref, middle_ref, start_ref, counts_ref, center_ref, width_ref, out_ref):
-    total = own_ref[...] + blocks_times(
-        hamiltonian_ref, (3, 4, 5, 6), (a_ref[...], b_ref[...], c_ref[...], d_ref[...])
-    )
-    total = jnp.where(alive(counts_ref), total, 0.0)
+def second_step(own_ref, c_ref, d_ref, hamiltonian_ref, middle_ref, start_ref, live_ref, center_ref, width_ref, out_ref):
+    total = applied(own_ref, c_ref, d_ref, hamiltonian_ref, live_ref)
     filtered = 2.0 * (total - center_ref[0] * middle_ref[...]) / width_ref[0] - start_ref[...]
     out_ref[...] = jnp.transpose(filtered)
 
@@ -163,21 +176,24 @@
 
 def shards(orbitals, rotation, counts, hamiltonian, center, width):
     pieces = jnp.transpose(orbitals, (1, 0, 2))
-    cut = call(cut_columns, (NEAR, ELEMS * PIECE, WIDE), 0, 2 * FIELD, (V,))(pieces)
+    shapes = ((NEAR, ELEMS * PIECE, WIDE), (FAR, 64, WIDE), (ROWS, WIDE))
+    cut, slices, live = call(cut_columns, shapes, 0, 6 * FIELD, (V, V, S))(pieces, rotation, counts)
     cut = lax.all_to_all(cut, NEARS, split_axis=0, concat_axis=0, tiled=True)
-    packed = call(pack, (FAR, ROWS + 64, WIDE), 0, 6 * FIELD, (V, V))(cut, rotation)
+    packed = call(pack, (FAR, ROWS + 64, WIDE), 0, 6 * FIELD, (V, V))(cut, slices)
     packed = lax.all_to_all(packed, "z_hi", split_axis=0, concat_axis=0, tiled=True)
     parts = call(rotate, (NEAR, ROWS, WIDE), 6 * 640 * 128 * 256, 13 * FIELD, (V,))(packed)
     parts = lax.all_to_all(parts, NEARS, split_axis=0, concat_axis=0, tiled=True)
-    start = call(add_up, (ROWS, WIDE), 0, 9 * FIELD, (V, S))(parts, counts)
-
-    own = call(own_slots, (ROWS, WIDE), 6 * 12 * ROWS * ROWS * WIDE, BLOCKS, (V, V))
-    first = call(first_step, (ROWS, WIDE), 6 * 16 * ROWS * ROWS * WIDE, BLOCKS, (V,) * 7 + (S,) * 3)
-    second = call(second_step, (WIDE, ROWS), 6 * 16 * ROWS * ROWS * WIDE, BLOCKS, (V,) * 8 + (S,) * 3)
-    around = neighbours(start)
-    middle = first(own(start, hamiltonian), *around, hamiltonian, start, counts, center, width)
-    around = neighbours(middle)
-    filtered = second(own(middle, hamiltonian), *around, hamiltonian, middle, start, counts, center, width)
+    start = call(add_up, (ROWS, WIDE), 0, 9 * FIELD, (V, V))(parts, live)
+
+    own = call(own_and_ring, (ROWS, WIDE), 6 * 20 * ROWS * ROWS * WIDE, BLOCKS, (V,) * 4)
+    first = call(first_step, (ROWS, WIDE), 6 * 8 * ROWS * ROWS * WIDE, BLOCKS // 3, (V,) * 6 + (S,) * 2)
+    second = call(second_step, (WIDE, ROWS), 6 * 8 * ROWS * ROWS * WIDE, BLOCKS // 3, (V,) * 7 + (S,) * 2)
+    a, b, c, d = neighbours(start)
+    own_part = own(start, a, b, hamiltonian)
+    middle = first(own_part, c, d, hamiltonian, start, live, center, width)
+    a, b, c, d = neighbours(middle)
+    own_part = own(middle, a, b, hamiltonian)
+    filtered = second(own_part, c, d, hamiltonian, middle, start, live, center, width)
     return jnp.transpose(filtered.reshape(ELEMS, BANDS, ROWS), (0, 2, 1))
 
 

time: 123 us -> 120 us (0.976)
  Pallas kernels: 7.65 us -> 5.54 us
    pallas_call x7, Pallas kernels: 6.88 us -> 4.77 us  [the longest x1 1.26 us: shards(): second(own_part, c, d, hamiltonian, middle, start, live, center, width)]
  transfers between devices with their start and end apart: 8 -> 8, of which waited for: 2 -> 2; matrix products, arithmetic and copies ran while one was open for 0% -> 0% of each run, Pallas kernels for 1% -> 2%
where the time goes in v2:
time: 120 us
  blocking collectives  90 us (75%)
  starting transfers between devices  17.6 us (15%)
  Pallas kernels  5.54 us (5%)
  local copies, waits for them, and re-layouts  2.86 us (2%)
  waiting for transfers between devices  2.66 us (2%)
  between operations  1.45 us (1%)
    all_to_all x1, blocking collectives, shards(): lax.all_to_all(packed, 'z_hi', split_axis=0, concat_axis=0, tiled=True)  38.5 us
    all_to_all x1, blocking collectives, shards(): lax.all_to_all(parts, NEARS, split_axis=0, concat_axis=0, tiled=True)  29.1 us
    all_to_all x1, blocking collectives, shards(): cut = lax.all_to_all(cut, NEARS, split_axis=0, concat_axis=0, tiled=True)  22.5 us
    ppermute x2, starting transfers between devices, neighbours(): lax.ppermute(field, 'layer', [(i + 1, i) for i in range(LAYERS - 1)])  6.47 us
    ppermute x2, starting transfers between devices, neighbours(): lax.ppermute(field, RING, [(i, (i - 1) % ring) for i in range(ring)])  5.89 us
    ppermute x2, starting transfers between devices, neighbours(): lax.ppermute(field, 'layer', [(i, i + 1) for i in range(LAYERS - 1)])  5.19 us
    unnamed x8, local copies, waits for them, and re-layouts  2.86 us
    ppermute x2, waiting for transfers between devices, neighbours(): lax.ppermute(field, 'layer', [(i + 1, i) for i in range(LAYERS - 1)])  2.65 us
  transfers between devices with their start and end apart: 8, of which 2 were waited for; matrix products, arithmetic and copies ran while one was open for 0% of the time, Pallas kernels for 2%

profile of v2, /device:TPU:8, one launch (start us, length us, event | category | flops | bytes accessed | tf_op | source)
XLA Modules:
  0.0 120.1 jit_solution(1912137901251371267)
XLA Ops:
  0.0 0.0 copy-start
  0.0 0.0 copy-start.1
  0.0 1.1 copy-done.1
  1.1 0.0 copy-start.2
  1.1 1.1 copy-done.2
  2.2 0.0 copy-start.3
  2.2 0.7 copy-done.3
  2.9 0.7 shard_map.64
  3.6 22.5 %all_to_all.15.rows_ref = f32[8,20,128]{2,1,0:T(8,128)S(1)} all-to-all(f32[8,20,128]{2,1,0:T(8,128)S(1)} %get-tuple-element.8), channel_id=1, replica_groups=mesh['layer'=4,'column'=4,'core'=2,'z_hi'=4,'z_lo'=4,'y_hi'=2] {'z_lo','..., dimensions={0} | all-to-all | bytes 163840 | tf_op jit(solution)/shard_map/all_to_all | solution.py:181
  26.1 0.1 shard_map.65
  26.1 38.5 %all_to_all.16.packed_ref = f32[4,224,128]{2,1,0:T(8,128)S(1)} all-to-all(f32[4,224,128]{2,1,0:T(8,128)S(1)} %shard_map.65), channel_id=1, replica_groups=mesh['layer'=4,'column'=4,'core'=2,'z_hi'=4,'z_lo'=4,'y_hi'=2] {'z_hi'}, dimensions={0} | all-to-all | bytes 917504 | tf_op jit(solution)/shard_map/all_to_all | solution.py:183
  64.6 0.8 shard_map.66
  65.4 29.1 %all_to_all.17.parts_ref = f32[8,160,128]{2,1,0:T(8,128)S(1)} all-to-all(f32[8,160,128]{2,1,0:T(8,128)S(1)} %shard_map.66), channel_id=1, replica_groups=mesh['layer'=4,'column'=4,'core'=2,'z_hi'=4,'z_lo'=4,'y_hi'=2] {'z_lo','..., dimensions={0} | all-to-all | bytes 1310720 | tf_op jit(solution)/shard_map/all_to_all | solution.py:185
  94.5 0.0 collective-permute-start
  94.5 2.9 %collective-permute-start.1 = (f32[160,128]{1,0:T(8,128)S(1)}, f32[160,128]{1,0:T(8,128)S(1)}, u32[]{:S(2)}, u32[]{:S(2)}) collective-permute-start(f32[160,128]{1,0:T(8,128)S(1)} %shard_map.67.field_ref.start_ref), channel_id=1, source_target_pairs={{0,224},{32,0},{64,32},{96,64},{128,96},{160,128},{192,160},{224,1... | collective-permute-start | bytes 245768 | tf_op jit(solution)/shard_map/ppermute | solution.py:166
  97.4 2.7 %collective-permute-start.2 = (f32[160,128]{1,0:T(8,128)S(1)}, f32[160,128]{1,0:T(8,128)S(1)}, u32[]{:S(2)}, u32[]{:S(2)}) collective-permute-start(f32[160,128]{1,0:T(8,128)S(1)} %shard_map.67.field_ref.start_ref), channel_id=1, source_target_pairs={{0,256},{256,512},{512,768},{1,257},{257,513},{513,769},{2,258},{2... | collective-permute-start | bytes 245768 | tf_op jit(solution)/shard_map/ppermute | solution.py:167
  100.2 3.1 %collective-permute-start.3 = (f32[160,128]{1,0:T(8,128)S(1)}, f32[160,128]{1,0:T(8,128)S(1)}, u32[]{:S(2)}, u32[]{:S(2)}) collective-permute-start(f32[160,128]{1,0:T(8,128)S(1)} %shard_map.67.field_ref.start_ref), channel_id=1, source_target_pairs={{256,0},{512,256},{768,512},{257,1},{513,257},{769,513},{258,2},{5... | collective-permute-start | bytes 245768 | tf_op jit(solution)/shard_map/ppermute | solution.py:168
  104.6 0.0 collective-permute-done.a_ref
  104.6 0.0 collective-permute-done.1.b_ref
  104.6 0.0 copy-done
  104.6 1.1 shard_map.68.own_ref
  105.7 0.0 collective-permute-done.2.c_ref
  105.7 0.8 collective-permute-done.3.d_ref
  106.5 0.5 shard_map.69.field_ref.middle_ref
  107.0 0.0 collective-permute-start.4
  107.1 2.9 %collective-permute-start.5 = (f32[160,128]{1,0:T(8,128)S(1)}, f32[160,128]{1,0:T(8,128)S(1)}, u32[]{:S(2)}, u32[]{:S(2)}) collective-permute-start(f32[160,128]{1,0:T(8,128)S(1)} %shard_map.69.field_ref.middle_ref), channel_id=1, source_target_pairs={{0,224},{32,0},{64,32},{96,64},{128,96},{160,128},{192,160},{224,1... | collective-permute-start | bytes 245768 | tf_op jit(solution)/shard_map/ppermute | solution.py:166
  110.0 2.5 %collective-permute-start.6 = (f32[160,128]{1,0:T(8,128)S(1)}, f32[160,128]{1,0:T(8,128)S(1)}, u32[]{:S(2)}, u32[]{:S(2)}) collective-permute-start(f32[160,128]{1,0:T(8,128)S(1)} %shard_map.69.field_ref.middle_ref), channel_id=1, source_target_pairs={{0,256},{256,512},{512,768},{1,257},{257,513},{513,769},{2,258},{2... | collective-permute-start | bytes 245768 | tf_op jit(solution)/shard_map/ppermute | solution.py:167
  112.5 3.4 %collective-permute-start.7 = (f32[160,128]{1,0:T(8,128)S(1)}, f32[160,128]{1,0:T(8,128)S(1)}, u32[]{:S(2)}, u32[]{:S(2)}) collective-permute-start(f32[160,128]{1,0:T(8,128)S(1)} %shard_map.69.field_ref.middle_ref), channel_id=1, source_target_pairs={{256,0},{512,256},{768,512},{257,1},{513,257},{769,513},{258,2},{5... | collective-permute-start | bytes 245768 | tf_op jit(solution)/shard_map/ppermute | solution.py:168
  115.9 0.0 collective-permute-done.4.a_ref
  115.9 0.0 collective-permute-done.5.b_ref
  115.9 1.1 shard_map.70.own_ref
  117.0 0.0 collective-permute-done.6.c_ref
  117.0 1.8 %collective-permute-done.7.d_ref = f32[160,128]{1,0:T(8,128)S(1)} collective-permute-done((f32[160,128]{1,0:T(8,128)S(1)}, f32[160,128]{1,0:T(8,128)S(1)}, u32[]{:S(2)}, u32[]{:S(2)}) %collective-permute-start.7) | collective-permute-done | bytes 81952 | tf_op jit(solution)/shard_map/ppermute | solution.py:168
  118.8 1.3 %shard_map.71 = f32[128,160]{1,0:T(8,128)} custom-call(f32[160,128]{1,0:T(8,128)S(1)} %shard_map.70.own_ref, f32[160,128]{1,0:T(8,128)S(1)} %collective-permute-done.6.c_ref, f32[160,128]{1,0:T(8,128)S(1)} %collective-permute-done.7.d_ref, f32[4,7,160,160]{3,2,1,0:T(8,128)S(1)} %copy-done, f32[160,128]{1,0:T(8,128)S(1)} %shard_map.69.field_ref.middle_ref, ...), custom_call_target="tpu_custom_call" | custom-call | flops 157286400 | bytes 1529173 | tf_op jit(solution)/shard_map/pallas_call | solution.py:196
  (1 shorter events, 0.0 us)
Async XLA Ops:
  0.0 104.6 %copy-start = (f32[4,7,160,160]{3,2,1,0:T(8,128)S(1)}, f32[4,7,160,160]{3,2,1,0:T(8,128)}, u32[]{:S(2)}) copy-start(f32[4,7,160,160]{3,2,1,0:T(8,128)} %hamiltonian_ref.7) | copy-start | bytes 8601604
  0.0 1.1 copy-start.1
  1.1 1.1 copy-start.2
  2.2 0.7 copy-start.3
  94.5 10.1 %collective-permute-start = (f32[160,128]{1,0:T(8,128)S(1)}, f32[160,128]{1,0:T(8,128)S(1)}, u32[]{:S(2)}, u32[]{:S(2)}) collective-permute-start(f32[160,128]{1,0:T(8,128)S(1)} %shard_map.67.field_ref.start_ref), channel_id=1, source_target_pairs={{0,32},{32,64},{64,96},{96,128},{128,160},{160,192},{192,224},{224... | collective-permute-start | bytes 245768 | tf_op jit(solution)/shard_map/ppermute | solution.py:165
  94.5 10.1 %collective-permute-start.1 = (f32[160,128]{1,0:T(8,128)S(1)}, f32[160,128]{1,0:T(8,128)S(1)}, u32[]{:S(2)}, u32[]{:S(2)}) collective-permute-start(f32[160,128]{1,0:T(8,128)S(1)} %shard_map.67.field_ref.start_ref), channel_id=1, source_target_pairs={{0,224},{32,0},{64,32},{96,64},{128,96},{160,128},{192,160},{224,1... | collective-permute-start | bytes 245768 | tf_op jit(solution)/shard_map/ppermute | solution.py:166
  97.4 8.3 %collective-permute-start.2 = (f32[160,128]{1,0:T(8,128)S(1)}, f32[160,128]{1,0:T(8,128)S(1)}, u32[]{:S(2)}, u32[]{:S(2)}) collective-permute-start(f32[160,128]{1,0:T(8,128)S(1)} %shard_map.67.field_ref.start_ref), channel_id=1, source_target_pairs={{0,256},{256,512},{512,768},{1,257},{257,513},{513,769},{2,258},{2... | collective-permute-start | bytes 245768 | tf_op jit(solution)/shard_map/ppermute | solution.py:167
  100.2 6.3 %collective-permute-start.3 = (f32[160,128]{1,0:T(8,128)S(1)}, f32[160,128]{1,0:T(8,128)S(1)}, u32[]{:S(2)}, u32[]{:S(2)}) collective-permute-start(f32[160,128]{1,0:T(8,128)S(1)} %shard_map.67.field_ref.start_ref), channel_id=1, source_target_pairs={{256,0},{512,256},{768,512},{257,1},{513,257},{769,513},{258,2},{5... | collective-permute-start | bytes 245768 | tf_op jit(solution)/shard_map/ppermute | solution.py:168
  107.0 8.8 %collective-permute-start.4 = (f32[160,128]{1,0:T(8,128)S(1)}, f32[160,128]{1,0:T(8,128)S(1)}, u32[]{:S(2)}, u32[]{:S(2)}) collective-permute-start(f32[160,128]{1,0:T(8,128)S(1)} %shard_map.69.field_ref.middle_ref), channel_id=1, source_target_pairs={{0,32},{32,64},{64,96},{96,128},{128,160},{160,192},{192,224},{224... | collective-permute-start | bytes 245768 | tf_op jit(solution)/shard_map/ppermute | solution.py:165
  107.1 8.8 %collective-permute-start.5 = (f32[160,128]{1,0:T(8,128)S(1)}, f32[160,128]{1,0:T(8,128)S(1)}, u32[]{:S(2)}, u32[]{:S(2)}) collective-permute-start(f32[160,128]{1,0:T(8,128)S(1)} %shard_map.69.field_ref.middle_ref), channel_id=1, source_target_pairs={{0,224},{32,0},{64,32},{96,64},{128,96},{160,128},{192,160},{224,1... | collective-permute-start | bytes 245768 | tf_op jit(solution)/shard_map/ppermute | solution.py:166
  110.0 7.0 %collective-permute-start.6 = (f32[160,128]{1,0:T(8,128)S(1)}, f32[160,128]{1,0:T(8,128)S(1)}, u32[]{:S(2)}, u32[]{:S(2)}) collective-permute-start(f32[160,128]{1,0:T(8,128)S(1)} %shard_map.69.field_ref.middle_ref), channel_id=1, source_target_pairs={{0,256},{256,512},{512,768},{1,257},{257,513},{513,769},{2,258},{2... | collective-permute-start | bytes 245768 | tf_op jit(solution)/shard_map/ppermute | solution.py:167
  112.5 6.3 %collective-permute-start.7 = (f32[160,128]{1,0:T(8,128)S(1)}, f32[160,128]{1,0:T(8,128)S(1)}, u32[]{:S(2)}, u32[]{:S(2)}) collective-permute-start(f32[160,128]{1,0:T(8,128)S(1)} %shard_map.69.field_ref.middle_ref), channel_id=1, source_target_pairs={{256,0},{512,256},{768,512},{257,1},{513,257},{769,513},{258,2},{5... | collective-permute-start | bytes 245768 | tf_op jit(solution)/shard_map/ppermute | solution.py:168

commit v3 on v2

v3 whole, which is shorter than its diff:
```python
import jax
import jax.numpy as jnp
from jax import lax
from jax.experimental import pallas as pl
from jax.experimental.pallas import tpu as pltpu
from jax.sharding import Mesh
from jax.sharding import PartitionSpec as P

LAYERS, COLUMNS, CORES = 4, 4, 2
FAR, NEAR = 4, 8
ELEMS, ROWS, WIDE = 4, 160, 128
BANDS = 32
PIECE = 5
ELEM = ("layer", "column", "core")
RING = ("column", "core")
NEARS = ("z_lo", "y_hi")
BAND = ("z_hi",) + NEARS
F32, BF16 = jnp.float32, jnp.bfloat16


def call(kernel, out, flops, moved, spaces, scratch=(), kind=F32):
    several = isinstance(out[0], tuple)
    shapes = tuple(jax.ShapeDtypeStruct(o, kind) for o in (out if several else (out,)))
    specs = tuple(pl.BlockSpec(memory_space=pltpu.VMEM) for _ in shapes)
    return pl.pallas_call(
        kernel,
        out_shape=shapes if several else shapes[0],
        in_specs=[pl.BlockSpec(memory_space=s) for s in spaces],
        out_specs=specs if several else specs[0],
        scratch_shapes=scratch,
        compiler_params=pltpu.CompilerParams(vmem_limit_bytes=32 << 20),
        cost_estimate=pl.CostEstimate(flops=flops, bytes_accessed=moved, transcendentals=0),
    )


def split(v):
    high = v.astype(BF16)
    return high, (v - high.astype(F32)).astype(BF16)


def dot3(a, b):
    def dot(x, y):
        return jnp.dot(x, y, preferred_element_type=F32)

    return dot(a[0], b[0]) + (dot(a[0], b[1]) + dot(a[1], b[0]))


def lane_owner(shape):
    return lax.broadcasted_iota(jnp.int32, shape, len(shape) - 1) // BANDS


def by_owner(parts):
    owner = lane_owner(parts[0].shape)
    picked = parts[0]
    for e in range(1, ELEMS):
        picked = jnp.where(owner == e, parts[e], picked)
    return picked


def turned(v, by):
    by = by % ELEMS
    return pltpu.roll(v, by * BANDS, 1) if by else v


def alive(counts_ref):
    owner = lane_owner((ROWS, WIDE))
    row = lax.broadcasted_iota(jnp.int32, (ROWS, WIDE), 0)
    limit = jnp.full((ROWS, WIDE), counts_ref[0], jnp.int32)
    for e in range(1, ELEMS):
        limit = jnp.where(owner == e, counts_ref[e], limit)
    return row < limit


def cut_columns(orbitals_ref, rotation_ref, counts_ref, out_ref, slices_ref, live_ref):
    live_ref[...] = jnp.where(alive(counts_ref), 1.0, 0.0)
    for far in range(FAR):
        for half in range(2):
            slices_ref[far, pl.ds(32 * half, 32), :] = rotation_ref[:, pl.ds(256 * far + 128 * half, 128)]
    for i in range(PIECE):
        for near in range(NEAR):
            half, place = divmod(near, ELEMS)
            parts = [
                turned(orbitals_ref[i, :, pl.ds(256 * far + 128 * half, 128)], far - place)
                for far in range(FAR)
            ]
            out_ref[near, pl.ds(ELEMS * i, ELEMS), :] = by_owner(parts)


def far_place(by):
    return lax.rem(lax.axis_index("z_hi") + by, FAR)


HALF = ROWS // 2
PASS = HALF + 32


def pack(rows_ref, slices_ref, up_ref, down_ref):
    for e in range(ELEMS):
        top, mine = divmod(e, 2)
        first, second = (down_ref, up_ref) if top else (up_ref, down_ref)
        for near in range(NEAR):
            for i in range(PIECE):
                at = 40 * mine + PIECE * near + i
                row = rows_ref[near, pl.ds(ELEMS * i + e, 1), :]
                first[pl.ds(at, 1), :] = row
                second[pl.ds(PASS + at, 1), :] = row
    opposite = far_place(2)
    up_ref[HALF:PASS, :] = slices_ref[opposite, :32, :]
    down_ref[HALF:PASS, :] = slices_ref[opposite, 32:, :]
    up_ref[PASS + HALF :, :] = slices_ref[far_place(1)]
    down_ref[PASS + HALF :, :] = slices_ref[far_place(3)]


def rotate(up_ref, down_ref, slices_ref, below_ref, above_ref, passed_up_ref, passed_down_ref, out_ref, left_ref, right_ref):
    own = slices_ref[far_place(0)]
    sides = [
        (0, own[:32], own[32:], up_ref[:HALF, :], down_ref[:HALF, :]),
        (3, below_ref[PASS + HALF : PASS + HALF + 32, :], below_ref[PASS + HALF + 32 :, :],
         below_ref[:HALF, :], below_ref[PASS : PASS + HALF, :]),
        (1, above_ref[PASS + HALF : PASS + HALF + 32, :], above_ref[PASS + HALF + 32 :, :],
         above_ref[PASS : PASS + HALF, :], above_ref[:HALF, :]),
        (2, passed_up_ref[HALF:, :], passed_down_ref[HALF:, :], passed_up_ref[:HALF, :], passed_down_ref[:HALF, :]),
    ]
    for by, left, right, _, _ in sides:
        at = pl.ds(pl.multiple_of(32 * far_place(by), 32), 32)
        left_ref[at, :] = left
        right_ref[at, :] = right
    halves = [split(left_ref[...]), split(right_ref[...])]
    for by, _, _, top, bottom in sides:
        rows = split(jnp.concatenate([top, bottom], axis=0))
        products = [dot3(rows, half) for half in halves]
        at = pl.ds(pl.multiple_of(40 * far_place(by), 8), 40)
        for near in range(NEAR):
            half, place = divmod(near, ELEMS)
            out_ref[near, at, :] = by_owner(
                [turned(products[half][40 * e : 40 * e + 40], e - place) for e in range(ELEMS)]
            )


def add_up(parts_ref, live_ref, out_ref):
    total = parts_ref[0]
    for near in range(1, NEAR):
        total = total + parts_ref[near]
    out_ref[...] = jnp.where(live_ref[...] > 0.5, total, 0.0)


def split_blocks(hamiltonian_ref, high_ref, low_ref):
    for e in range(ELEMS):
        for slot in range(7):
            high_ref[e, slot], low_ref[e, slot] = split(hamiltonian_ref[e, slot])


def blocks_times(high_ref, low_ref, slots, fields):
    def dot(x, y):
        return jnp.dot(x, y, preferred_element_type=F32)

    fields = [split(f) for f in fields]
    pairs = [jnp.concatenate(f, axis=1) for f in fields]
    totals = []
    for e in range(ELEMS):
        wide = narrow = None
        for slot, field, pair in zip(slots, fields, pairs):
            first, second = dot(high_ref[e, slot], pair), dot(low_ref[e, slot], field[0])
            wide = first if wide is None else wide + first
            narrow = second if narrow is None else narrow + second
        totals.append(wide[:, :WIDE] + (wide[:, WIDE:] + narrow))
    return by_owner(totals)


def own_and_ring(field_ref, a_ref, b_ref, high_ref, low_ref, out_ref):
    field = field_ref[...]
    out_ref[...] = blocks_times(
        high_ref, low_ref, range(5), (field, turned(field, 1), turned(field, -1), a_ref[...], b_ref[...])
    )


def applied(own_ref, c_ref, d_ref, high_ref, low_ref, live_ref):
    total = own_ref[...] + blocks_times(high_ref, low_ref, (5, 6), (c_ref[...], d_ref[...]))
    return jnp.where(live_ref[...] > 0.5, total, 0.0)


def first_step(own_ref, c_ref, d_ref, high_ref, low_ref, start_ref, live_ref, center_ref, width_ref, out_ref):
    total = applied(own_ref, c_ref, d_ref, high_ref, low_ref, live_ref)
    out_ref[...] = (total - center_ref[0] * start_ref[...]) / width_ref[0]


def second_step(own_ref, c_ref, d_ref, high_ref, low_ref, middle_ref, start_ref, live_ref, center_ref, width_ref, out_ref):
    total = applied(own_ref, c_ref, d_ref, high_ref, low_ref, live_ref)
    filtered = 2.0 * (total - center_ref[0] * middle_ref[...]) / width_ref[0] - start_ref[...]
    out_ref[...] = jnp.transpose(filtered)


def neighbours(field):
    ring = COLUMNS * CORES
    return (
        lax.ppermute(field, RING, [(i, (i + 1) % ring) for i in range(ring)]),
        lax.ppermute(field, RING, [(i, (i - 1) % ring) for i in range(ring)]),
        lax.ppermute(field, "layer", [(i, i + 1) for i in range(LAYERS - 1)]),
        lax.ppermute(field, "layer", [(i + 1, i) for i in range(LAYERS - 1)]),
    )


def far_step(v, by):
    return lax.ppermute(v, "z_hi", [(i, (i + by) % FAR) for i in range(FAR)])


V, S = pltpu.VMEM, pltpu.SMEM
FIELD = ROWS * WIDE * 4
BLOCKS = ELEMS * 7 * ROWS * 256 * 4


def shards(orbitals, rotation, counts, hamiltonian, center, width):
    pieces = jnp.transpose(orbitals, (1, 0, 2))
    shapes = ((NEAR, ELEMS * PIECE, WIDE), (FAR, 64, WIDE), (ROWS, WIDE))
    cut, slices, live = call(cut_columns, shapes, 0, 6 * FIELD, (V, V, S))(pieces, rotation, counts)
    cut = lax.all_to_all(cut, NEARS, split_axis=0, concat_axis=0, tiled=True)
    message = (2 * PASS + 32, WIDE)
    up, down = call(pack, (message, message), 0, 6 * FIELD, (V, V))(cut, slices)
    above, below = far_step(down, -1), far_step(up, 1)
    passed_up, passed_down = far_step(below[:PASS], 1), far_step(above[:PASS], -1)
    blocks = call(split_blocks, (hamiltonian.shape,) * 2, 0, 2 * BLOCKS, (V,), (), BF16)(hamiltonian)
    slices, *blocks = lax.optimization_barrier((slices, *blocks))
    scratch = [V((WIDE, WIDE), F32)] * 2
    parts = call(rotate, (NEAR, ROWS, WIDE), 6 * 640 * 128 * 256, 13 * FIELD, (V,) * 7, scratch)(
        up, down, slices, below, above, passed_up, passed_down
    )
    parts = lax.all_to_all(parts, NEARS, split_axis=0, concat_axis=0, tiled=True)
    start = call(add_up, (ROWS, WIDE), 0, 9 * FIELD, (V, V))(parts, live)

    own = call(own_and_ring, (ROWS, WIDE), 6 * 20 * ROWS * ROWS * WIDE, BLOCKS, (V,) * 5)
    first = call(first_step, (ROWS, WIDE), 6 * 8 * ROWS * ROWS * WIDE, BLOCKS // 3, (V,) * 7 + (S,) * 2)
    second = call(second_step, (WIDE, ROWS), 6 * 8 * ROWS * ROWS * WIDE, BLOCKS // 3, (V,) * 8 + (S,) * 2)
    a, b, c, d = neighbours(start)
    own_part = own(start, a, b, *blocks)
    middle = first(own_part, c, d, *blocks, start, live, center, width)
    a, b, c, d = neighbours(middle)
    own_part = own(middle, a, b, *blocks)
    filtered = second(own_part, c, d, *blocks, middle, start, live, center, width)
    return jnp.transpose(filtered.reshape(ELEMS, BANDS, ROWS), (0, 2, 1))


def solution(mesh):
    inner = Mesh(
        mesh.devices.reshape(LAYERS, COLUMNS, CORES, FAR, NEAR // 2, 2), ELEM + BAND
    )
    return jax.shard_map(
        shards,
        mesh=inner,
        in_specs=(P(ELEM, BAND, None), P(BAND, None), P(ELEM), P(ELEM, None, None, None), P(), P()),
        out_specs=P(ELEM, None, BAND),
        check_vma=False,
    )
```

time: 120 us -> 116 us (0.967)
  blocking collectives: 90 us -> 46.6 us
  starting transfers between devices: 17.6 us -> 43.3 us
  waiting for transfers between devices: 2.66 us -> 13.1 us
  local copies, waits for them, and re-layouts: 2.86 us -> 4.75 us
    all_to_all x1 -> x0, blocking collectives: 38.5 us -> none  [shards(): lax.all_to_all(packed, 'z_hi', split_axis=0, concat_axis=0, tiled=True)]
    ppermute x0 -> x4, starting transfers between devices: none -> 25.7 us  [far_step(): return lax.ppermute(v, 'z_hi', [(i, (i + by) % FAR) for i in range(FAR)])]
    ppermute x0 -> x4, waiting for transfers between devices: none -> 11.5 us  [far_step(): return lax.ppermute(v, 'z_hi', [(i, (i + by) % FAR) for i in range(FAR)])]
    all_to_all x1, blocking collectives: 29.1 us -> 24.1 us  [shards(): lax.all_to_all(parts, NEARS, split_axis=0, concat_axis=0, tiled=True)]
    unnamed x8, local copies, waits for them, and re-layouts: 2.86 us -> 4.74 us
    pallas_call x6 -> x7, Pallas kernels: 4.77 us -> 5.45 us  [the longest x1 1.26 us: shards(): second(own_part, c, d, *blocks, middle, start, live, center, width)]
  transfers between devices with their start and end apart: 8 -> 12, of which waited for: 2 -> 5; matrix products, arithmetic and copies ran while one was open for 0% -> 0% of each run, Pallas kernels for 2% -> 2%
where the time goes in v3:
time: 116 us; the launch traced here: 115 us
  blocking collectives  46.6 us (40%)
  starting transfers between devices  43.3 us (37%)
  waiting for transfers between devices  13.1 us (11%)
  Pallas kernels  6.22 us (5%)
  local copies, waits for them, and re-layouts  4.75 us (4%)
  between operations  1.5 us (1%)
    ppermute x4, starting transfers between devices, far_step(): return lax.ppermute(v, 'z_hi', [(i, (i + by) % FAR) for i in range(FAR)])  25.7 us
    all_to_all x1, blocking collectives, shards(): lax.all_to_all(parts, NEARS, split_axis=0, concat_axis=0, tiled=True)  24.1 us
    all_to_all x1, blocking collectives, shards(): cut = lax.all_to_all(cut, NEARS, split_axis=0, concat_axis=0, tiled=True)  22.5 us
    ppermute x4, waiting for transfers between devices, far_step(): return lax.ppermute(v, 'z_hi', [(i, (i + by) % FAR) for i in range(FAR)])  11.5 us
    ppermute x2, starting transfers between devices, neighbours(): lax.ppermute(field, 'layer', [(i + 1, i) for i in range(LAYERS - 1)])  7.57 us
    ppermute x2, starting transfers between devices, neighbours(): lax.ppermute(field, RING, [(i, (i - 1) % ring) for i in range(ring)])  5.89 us
    unnamed x8, local copies, waits for them, and re-layouts  4.74 us
    ppermute x2, starting transfers between devices, neighbours(): lax.ppermute(field, 'layer', [(i, i + 1) for i in range(LAYERS - 1)])  4.09 us
  transfers between devices with their start and end apart: 12, of which 5 were waited for; matrix products, arithmetic and copies ran while one was open for 0% of the time, Pallas kernels for 2%

profile of v3, /device:TPU:8, one launch (start us, length us, event | category | flops | bytes accessed | tf_op | source)
XLA Modules:
  0.0 115.4 jit_solution(12789266008354283687)
XLA Ops:
  0.0 0.0 copy-start.1
  0.0 0.9 copy-done.1
  0.9 0.0 copy-start.2
  0.9 0.9 copy-done.2
  1.8 0.0 copy-start.3
  1.8 0.7 copy-done.3
  2.4 0.7 shard_map.64
  3.2 22.5 %all_to_all.10.rows_ref = f32[8,20,128]{2,1,0:T(8,128)S(1)} all-to-all(f32[8,20,128]{2,1,0:T(8,128)S(1)} %get-tuple-element.15), channel_id=1, replica_groups=mesh['layer'=4,'column'=4,'core'=2,'z_hi'=4,'z_lo'=4,'y_hi'=2] {'z_lo','..., dimensions={0} | all-to-all | bytes 163840 | tf_op jit(solution)/shard_map/all_to_all | solution.py:216
  25.6 0.1 shard_map.65
  25.7 10.9 %collective-permute-start = (f32[256,128]{1,0:T(8,128)S(1)}, f32[256,128]{1,0:T(8,128)S(1)}, u32[]{:S(2)}, u32[]{:S(2)}) collective-permute-start(f32[256,128]{1,0:T(8,128)S(1)} %get-tuple-element.17.up_ref), channel_id=1, source_target_pairs={{0,8},{8,16},{16,24},{24,0},{1,9},{9,17},{17,25},{25,1},{2,10},{10... | collective-permute-start | bytes 393224 | tf_op jit(solution)/shard_map/ppermute | solution.py:204
  36.7 6.5 %collective-permute-start.1 = (f32[256,128]{1,0:T(8,128)S(1)}, f32[256,128]{1,0:T(8,128)S(1)}, u32[]{:S(2)}, u32[]{:S(2)}) collective-permute-start(f32[256,128]{1,0:T(8,128)S(1)} %get-tuple-element.18.down_ref), channel_id=1, source_target_pairs={{0,24},{8,0},{16,8},{24,16},{1,25},{9,1},{17,9},{25,17},{2,26},{10... | collective-permute-start | bytes 393224 | tf_op jit(solution)/shard_map/ppermute | solution.py:204
  43.2 7.5 %collective-permute-done.below_ref = f32[256,128]{1,0:T(8,128)S(1)} collective-permute-done((f32[256,128]{1,0:T(8,128)S(1)}, f32[256,128]{1,0:T(8,128)S(1)}, u32[]{:S(2)}, u32[]{:S(2)}) %collective-permute-start) | collective-permute-done | bytes 131104 | tf_op jit(solution)/shard_map/ppermute | solution.py:204
  50.7 2.1 %collective-permute-start.2 = (f32[112,128]{1,0:T(8,128)S(1)}, f32[112,128]{1,0:T(8,128)S(1)}, u32[]{:S(2)}, u32[]{:S(2)}) collective-permute-start(f32[112,128]{1,0:T(8,128)S(1)} %slice.8), channel_id=1, source_target_pairs={{0,8},{8,16},{16,24},{24,0},{1,9},{9,17},{17,25},{25,1},{2,10},{10... | collective-permute-start | bytes 172040 | tf_op jit(solution)/shard_map/ppermute | solution.py:204
  52.8 1.8 %collective-permute-done.1.above_ref = f32[256,128]{1,0:T(8,128)S(1)} collective-permute-done((f32[256,128]{1,0:T(8,128)S(1)}, f32[256,128]{1,0:T(8,128)S(1)}, u32[]{:S(2)}, u32[]{:S(2)}) %collective-permute-start.1) | collective-permute-done | bytes 131104 | tf_op jit(solution)/shard_map/ppermute | solution.py:204
  54.6 6.2 %collective-permute-start.3 = (f32[112,128]{1,0:T(8,128)S(1)}, f32[112,128]{1,0:T(8,128)S(1)}, u32[]{:S(2)}, u32[]{:S(2)}) collective-permute-start(f32[112,128]{1,0:T(8,128)S(1)} %slice.9), channel_id=1, source_target_pairs={{0,24},{8,0},{16,8},{24,16},{1,25},{9,1},{17,9},{25,17},{2,26},{10... | collective-permute-start | bytes 172040 | tf_op jit(solution)/shard_map/ppermute | solution.py:204
  60.8 0.0 copy-start
  60.8 2.3 %copy-done = f32[4,7,160,160]{3,2,1,0:T(8,128)S(1)} copy-done((f32[4,7,160,160]{3,2,1,0:T(8,128)S(1)}, f32[4,7,160,160]{3,2,1,0:T(8,128)}, u32[]{:S(2)}) %copy-start) | copy-done | bytes 2867224
  63.1 0.6 shard_map.66
  63.7 0.0 collective-permute-done.2.passed_up_ref
  63.7 2.2 %collective-permute-done.3.passed_down_ref = f32[112,128]{1,0:T(8,128)S(1)} collective-permute-done((f32[112,128]{1,0:T(8,128)S(1)}, f32[112,128]{1,0:T(8,128)S(1)}, u32[]{:S(2)}, u32[]{:S(2)}) %collective-permute-start.3) | collective-permute-done | bytes 57376 | tf_op jit(solution)/shard_map/ppermute | solution.py:204
  65.9 0.8 shard_map.67
  66.8 24.1 %all_to_all.11.parts_ref = f32[8,160,128]{2,1,0:T(8,128)S(1)} all-to-all(f32[8,160,128]{2,1,0:T(8,128)S(1)} %shard_map.67), channel_id=1, replica_groups=mesh['layer'=4,'column'=4,'core'=2,'z_hi'=4,'z_lo'=4,'y_hi'=2] {'z_lo','..., dimensions={0} | all-to-all | bytes 1310720 | tf_op jit(solution)/shard_map/all_to_all | solution.py:227
  90.9 0.0 collective-permute-start.4
  91.0 2.9 %collective-permute-start.5 = (f32[160,128]{1,0:T(8,128)S(1)}, f32[160,128]{1,0:T(8,128)S(1)}, u32[]{:S(2)}, u32[]{:S(2)}) collective-permute-start(f32[160,128]{1,0:T(8,128)S(1)} %shard_map.68.field_ref.start_ref), channel_id=1, source_target_pairs={{0,224},{32,0},{64,32},{96,64},{128,96},{160,128},{192,160},{224,1... | collective-permute-start | bytes 245768 | tf_op jit(solution)/shard_map/ppermute | solution.py:197
  93.9 2.2 %collective-permute-start.6 = (f32[160,128]{1,0:T(8,128)S(1)}, f32[160,128]{1,0:T(8,128)S(1)}, u32[]{:S(2)}, u32[]{:S(2)}) collective-permute-start(f32[160,128]{1,0:T(8,128)S(1)} %shard_map.68.field_ref.start_ref), channel_id=1, source_target_pairs={{0,256},{256,512},{512,768},{1,257},{257,513},{513,769},{2,258},{2... | collective-permute-start | bytes 245768 | tf_op jit(solution)/shard_map/ppermute | solution.py:198
  96.1 3.7 %collective-permute-start.7 = (f32[160,128]{1,0:T(8,128)S(1)}, f32[160,128]{1,0:T(8,128)S(1)}, u32[]{:S(2)}, u32[]{:S(2)}) collective-permute-start(f32[160,128]{1,0:T(8,128)S(1)} %shard_map.68.field_ref.start_ref), channel_id=1, source_target_pairs={{256,0},{512,256},{768,512},{257,1},{513,257},{769,513},{258,2},{5... | collective-permute-start | bytes 245768 | tf_op jit(solution)/shard_map/ppermute | solution.py:199
  101.0 0.0 collective-permute-done.4.a_ref
  101.0 0.0 collective-permute-done.5.b_ref
  101.1 1.1 shard_map.69.own_ref
  102.1 0.0 collective-permute-done.6.c_ref
  102.2 0.3 collective-permute-done.7.d_ref
  102.4 0.5 shard_map.70.field_ref.middle_ref
  102.9 0.0 collective-permute-start.8
  102.9 2.9 %collective-permute-start.9 = (f32[160,128]{1,0:T(8,128)S(1)}, f32[160,128]{1,0:T(8,128)S(1)}, u32[]{:S(2)}, u32[]{:S(2)}) collective-permute-start(f32[160,128]{1,0:T(8,128)S(1)} %shard_map.70.field_ref.middle_ref), channel_id=1, source_target_pairs={{0,224},{32,0},{64,32},{96,64},{128,96},{160,128},{192,160},{224,1... | collective-permute-start | bytes 245768 | tf_op jit(solution)/shard_map/ppermute | solution.py:197
  105.9 1.9 %collective-permute-start.10 = (f32[160,128]{1,0:T(8,128)S(1)}, f32[160,128]{1,0:T(8,128)S(1)}, u32[]{:S(2)}, u32[]{:S(2)}) collective-permute-start(f32[160,128]{1,0:T(8,128)S(1)} %shard_map.70.field_ref.middle_ref), channel_id=1, source_target_pairs={{0,256},{256,512},{512,768},{1,257},{257,513},{513,769},{2,258},{2... | collective-permute-start | bytes 245768 | tf_op jit(solution)/shard_map/ppermute | solution.py:198
  107.8 3.9 %collective-permute-start.11 = (f32[160,128]{1,0:T(8,128)S(1)}, f32[160,128]{1,0:T(8,128)S(1)}, u32[]{:S(2)}, u32[]{:S(2)}) collective-permute-start(f32[160,128]{1,0:T(8,128)S(1)} %shard_map.70.field_ref.middle_ref), channel_id=1, source_target_pairs={{256,0},{512,256},{768,512},{257,1},{513,257},{769,513},{258,2},{5... | collective-permute-start | bytes 245768 | tf_op jit(solution)/shard_map/ppermute | solution.py:199
  111.7 0.0 collective-permute-done.8.a_ref
  111.7 0.0 collective-permute-done.9.b_ref
  111.8 1.1 shard_map.71.own_ref
  112.8 0.0 collective-permute-done.10.c_ref
  112.8 1.3 %collective-permute-done.11.d_ref = f32[160,128]{1,0:T(8,128)S(1)} collective-permute-done((f32[160,128]{1,0:T(8,128)S(1)}, f32[160,128]{1,0:T(8,128)S(1)}, u32[]{:S(2)}, u32[]{:S(2)}) %collective-permute-start.11) | collective-permute-done | bytes 81952 | tf_op jit(solution)/shard_map/ppermute | solution.py:199
  114.2 1.3 %shard_map.72 = f32[128,160]{1,0:T(8,128)} custom-call(f32[160,128]{1,0:T(8,128)S(1)} %shard_map.71.own_ref, f32[160,128]{1,0:T(8,128)S(1)} %collective-permute-done.10.c_ref, f32[160,128]{1,0:T(8,128)S(1)} %collective-permute-done.11.d_ref, bf16[4,7,160,160]{3,2,1,0:T(8,128)(2,1)S(1)} %get-tuple-element.23.high_ref, ...), custom_call_target="tpu_custom_call" | custom-call | flops 157286400 | bytes 1529173 | tf_op jit(solution)/shard_map/pallas_call | solution.py:238
  (3 shorter events, 0.0 us)
Async XLA Ops:
  0.0 0.9 copy-start.1
  0.9 0.9 copy-start.2
  1.8 0.7 copy-start.3
  25.7 24.9 %collective-permute-start = (f32[256,128]{1,0:T(8,128)S(1)}, f32[256,128]{1,0:T(8,128)S(1)}, u32[]{:S(2)}, u32[]{:S(2)}) collective-permute-start(f32[256,128]{1,0:T(8,128)S(1)} %get-tuple-element.17.up_ref), channel_id=1, source_target_pairs={{0,8},{8,16},{16,24},{24,0},{1,9},{9,17},{17,25},{25,1},{2,10},{10... | collective-permute-start | bytes 393224 | tf_op jit(solution)/shard_map/ppermute | solution.py:204
  36.7 17.9 %collective-permute-start.1 = (f32[256,128]{1,0:T(8,128)S(1)}, f32[256,128]{1,0:T(8,128)S(1)}, u32[]{:S(2)}, u32[]{:S(2)}) collective-permute-start(f32[256,128]{1,0:T(8,128)S(1)} %get-tuple-element.18.down_ref), channel_id=1, source_target_pairs={{0,24},{8,0},{16,8},{24,16},{1,25},{9,1},{17,9},{25,17},{2,26},{10... | collective-permute-start | bytes 393224 | tf_op jit(solution)/shard_map/ppermute | solution.py:204
  50.7 13.0 %collective-permute-start.2 = (f32[112,128]{1,0:T(8,128)S(1)}, f32[112,128]{1,0:T(8,128)S(1)}, u32[]{:S(2)}, u32[]{:S(2)}) collective-permute-start(f32[112,128]{1,0:T(8,128)S(1)} %slice.8), channel_id=1, source_target_pairs={{0,8},{8,16},{16,24},{24,0},{1,9},{9,17},{17,25},{25,1},{2,10},{10... | collective-permute-start | bytes 172040 | tf_op jit(solution)/shard_map/ppermute | solution.py:204
  54.6 11.4 %collective-permute-start.3 = (f32[112,128]{1,0:T(8,128)S(1)}, f32[112,128]{1,0:T(8,128)S(1)}, u32[]{:S(2)}, u32[]{:S(2)}) collective-permute-start(f32[112,128]{1,0:T(8,128)S(1)} %slice.9), channel_id=1, source_target_pairs={{0,24},{8,0},{16,8},{24,16},{1,25},{9,1},{17,9},{25,17},{2,26},{10... | collective-permute-start | bytes 172040 | tf_op jit(solution)/shard_map/ppermute | solution.py:204
  60.8 2.3 %copy-start = (f32[4,7,160,160]{3,2,1,0:T(8,128)S(1)}, f32[4,7,160,160]{3,2,1,0:T(8,128)}, u32[]{:S(2)}) copy-start(f32[4,7,160,160]{3,2,1,0:T(8,128)} %hamiltonian_ref.1) | copy-start | bytes 8601604
  90.9 10.1 %collective-permute-start.4 = (f32[160,128]{1,0:T(8,128)S(1)}, f32[160,128]{1,0:T(8,128)S(1)}, u32[]{:S(2)}, u32[]{:S(2)}) collective-permute-start(f32[160,128]{1,0:T(8,128)S(1)} %shard_map.68.field_ref.start_ref), channel_id=1, source_target_pairs={{0,32},{32,64},{64,96},{96,128},{128,160},{160,192},{192,224},{224... | collective-permute-start | bytes 245768 | tf_op jit(solution)/shard_map/ppermute | solution.py:196
  91.0 10.1 %collective-permute-start.5 = (f32[160,128]{1,0:T(8,128)S(1)}, f32[160,128]{1,0:T(8,128)S(1)}, u32[]{:S(2)}, u32[]{:S(2)}) collective-permute-start(f32[160,128]{1,0:T(8,128)S(1)} %shard_map.68.field_ref.start_ref), channel_id=1, source_target_pairs={{0,224},{32,0},{64,32},{96,64},{128,96},{160,128},{192,160},{224,1... | collective-permute-start | bytes 245768 | tf_op jit(solution)/shard_map/ppermute | solution.py:197
  93.9 8.2 %collective-permute-start.6 = (f32[160,128]{1,0:T(8,128)S(1)}, f32[160,128]{1,0:T(8,128)S(1)}, u32[]{:S(2)}, u32[]{:S(2)}) collective-permute-start(f32[160,128]{1,0:T(8,128)S(1)} %shard_map.68.field_ref.start_ref), channel_id=1, source_target_pairs={{0,256},{256,512},{512,768},{1,257},{257,513},{513,769},{2,258},{2... | collective-permute-start | bytes 245768 | tf_op jit(solution)/shard_map/ppermute | solution.py:198
  96.1 6.3 %collective-permute-start.7 = (f32[160,128]{1,0:T(8,128)S(1)}, f32[160,128]{1,0:T(8,128)S(1)}, u32[]{:S(2)}, u32[]{:S(2)}) collective-permute-start(f32[160,128]{1,0:T(8,128)S(1)} %shard_map.68.field_ref.start_ref), channel_id=1, source_target_pairs={{256,0},{512,256},{768,512},{257,1},{513,257},{769,513},{258,2},{5... | collective-permute-start | bytes 245768 | tf_op jit(solution)/shard_map/ppermute | solution.py:199
  102.9 8.8 %collective-permute-start.8 = (f32[160,128]{1,0:T(8,128)S(1)}, f32[160,128]{1,0:T(8,128)S(1)}, u32[]{:S(2)}, u32[]{:S(2)}) collective-permute-start(f32[160,128]{1,0:T(8,128)S(1)} %shard_map.70.field_ref.middle_ref), channel_id=1, source_target_pairs={{0,32},{32,64},{64,96},{96,128},{128,160},{160,192},{192,224},{224... | collective-permute-start | bytes 245768 | tf_op jit(solution)/shard_map/ppermute | solution.py:196
  102.9 8.8 %collective-permute-start.9 = (f32[160,128]{1,0:T(8,128)S(1)}, f32[160,128]{1,0:T(8,128)S(1)}, u32[]{:S(2)}, u32[]{:S(2)}) collective-permute-start(f32[160,128]{1,0:T(8,128)S(1)} %shard_map.70.field_ref.middle_ref), channel_id=1, source_target_pairs={{0,224},{32,0},{64,32},{96,64},{128,96},{160,128},{192,160},{224,1... | collective-permute-start | bytes 245768 | tf_op jit(solution)/shard_map/ppermute | solution.py:197
  105.9 7.0 %collective-permute-start.10 = (f32[160,128]{1,0:T(8,128)S(1)}, f32[160,128]{1,0:T(8,128)S(1)}, u32[]{:S(2)}, u32[]{:S(2)}) collective-permute-start(f32[160,128]{1,0:T(8,128)S(1)} %shard_map.70.field_ref.middle_ref), channel_id=1, source_target_pairs={{0,256},{256,512},{512,768},{1,257},{257,513},{513,769},{2,258},{2... | collective-permute-start | bytes 245768 | tf_op jit(solution)/shard_map/ppermute | solution.py:198
  107.8 6.3 %collective-permute-start.11 = (f32[160,128]{1,0:T(8,128)S(1)}, f32[160,128]{1,0:T(8,128)S(1)}, u32[]{:S(2)}, u32[]{:S(2)}) collective-permute-start(f32[160,128]{1,0:T(8,128)S(1)} %shard_map.70.field_ref.middle_ref), channel_id=1, source_target_pairs={{256,0},{512,256},{768,512},{257,1},{513,257},{769,513},{258,2},{5... | collective-permute-start | bytes 245768 | tf_op jit(solution)/shard_map/ppermute | solution.py:199

commit v4 on v3

--- a/solution.py
+++ b/solution.py
@@ -7,7 +7,7 @@
 from jax.sharding import PartitionSpec as P
 
 LAYERS, COLUMNS, CORES = 4, 4, 2
-FAR, NEAR = 4, 8
+FAR, LOW, NEAR = 4, 4, 8
 ELEMS, ROWS, WIDE = 4, 160, 128
 BANDS = 32
 PIECE = 5
@@ -71,19 +71,16 @@
     return row < limit
 
 
-def cut_columns(orbitals_ref, rotation_ref, counts_ref, out_ref, slices_ref, live_ref):
+def cut_columns(orbitals_ref, counts_ref, out_ref, live_ref):
     live_ref[...] = jnp.where(alive(counts_ref), 1.0, 0.0)
-    for far in range(FAR):
-        for half in range(2):
-            slices_ref[far, pl.ds(32 * half, 32), :] = rotation_ref[:, pl.ds(256 * far + 128 * half, 128)]
+    first = lax.broadcasted_iota(jnp.int32, (ELEMS, WIDE), 1) < 64
     for i in range(PIECE):
-        for near in range(NEAR):
-            half, place = divmod(near, ELEMS)
-            parts = [
-                turned(orbitals_ref[i, :, pl.ds(256 * far + 128 * half, 128)], far - place)
-                for far in range(FAR)
-            ]
-            out_ref[near, pl.ds(ELEMS * i, ELEMS), :] = by_owner(parts)
+        for low in range(LOW):
+            half, odd = divmod(low, 2)
+            for k in range(2):
+                parts = [orbitals_ref[i, :, pl.ds(256 * far + 128 * half, 128)] for far in (2 * k, 2 * k + 1)]
+                parts[1 - odd] = turned(parts[1 - odd], 2)
+                out_ref[low, pl.ds(20 * k + ELEMS * i, ELEMS), :] = jnp.where(first, parts[0], parts[1])
 
 
 def far_place(by):
@@ -91,57 +88,72 @@
 
 
 HALF = ROWS // 2
-PASS = HALF + 32
-
-
-def pack(rows_ref, slices_ref, up_ref, down_ref):
-    for e in range(ELEMS):
-        top, mine = divmod(e, 2)
-        first, second = (down_ref, up_ref) if top else (up_ref, down_ref)
-        for near in range(NEAR):
-            for i in range(PIECE):
-                at = 40 * mine + PIECE * near + i
-                row = rows_ref[near, pl.ds(ELEMS * i + e, 1), :]
-                first[pl.ds(at, 1), :] = row
-                second[pl.ds(PASS + at, 1), :] = row
-    opposite = far_place(2)
-    up_ref[HALF:PASS, :] = slices_ref[opposite, :32, :]
-    down_ref[HALF:PASS, :] = slices_ref[opposite, 32:, :]
-    up_ref[PASS + HALF :, :] = slices_ref[far_place(1)]
-    down_ref[PASS + HALF :, :] = slices_ref[far_place(3)]
-
-
-def rotate(up_ref, down_ref, slices_ref, below_ref, above_ref, passed_up_ref, passed_down_ref, out_ref, left_ref, right_ref):
-    own = slices_ref[far_place(0)]
+PASS = HALF + 64
+
+
+def pack(rows_ref, mine_ref, other_ref, up_ref, down_ref, own_ref):
+    for k in range(2):
+        first, second = (down_ref, up_ref) if k else (up_ref, down_ref)
+        for e in range(ELEMS):
+            for low in range(LOW):
+                for i in range(PIECE):
+                    at = 20 * e + PIECE * low + i
+                    row = rows_ref[low, pl.ds(20 * k + ELEMS * i + e, 1), :]
+                    first[pl.ds(at, 1), :] = row
+                    second[pl.ds(PASS + at, 1), :] = row
+    here = lax.axis_index("y_hi")
+    for place, ref in ((here, mine_ref), (1 - here, other_ref)):
+
+        def put(to, start, far, half):
+            lanes = pl.ds(pl.multiple_of(256 * far + 128 * half, 128), 128)
+            to[pl.ds(pl.multiple_of(start + 32 * place, 16), 32), :] = ref[:, lanes]
+
+        put(up_ref, HALF, far_place(2), 0)
+        put(down_ref, HALF, far_place(2), 1)
+        for half in range(2):
+            put(up_ref, PASS + HALF + 64 * half, far_place(1), half)
+            put(down_ref, PASS + HALF + 64 * half, far_place(3), half)
+            put(own_ref, 64 * half, far_place(0), half)
+
+
+def rotate(
+    up_ref, down_ref, own_ref, below_ref, above_ref, passed_up_ref, passed_down_ref, out_ref, left_ref, right_ref, sum_ref
+):
+    tail = PASS + HALF
     sides = [
-        (0, own[:32], own[32:], up_ref[:HALF, :], down_ref[:HALF, :]),
-        (3, below_ref[PASS + HALF : PASS + HALF + 32, :], below_ref[PASS + HALF + 32 :, :],
-         below_ref[:HALF, :], below_ref[PASS : PASS + HALF, :]),
-        (1, above_ref[PASS + HALF : PASS + HALF + 32, :], above_ref[PASS + HALF + 32 :, :],
-         above_ref[PASS : PASS + HALF, :], above_ref[:HALF, :]),
+        (0, own_ref[:64, :], own_ref[64:, :], up_ref[:HALF, :], down_ref[:HALF, :]),
+        (3, below_ref[tail : tail + 64, :], below_ref[tail + 64 :, :], below_ref[:HALF, :], below_ref[PASS:tail, :]),
+        (1, above_ref[tail : tail + 64, :], above_ref[tail + 64 :, :], above_ref[PASS:tail, :], above_ref[:HALF, :]),
         (2, passed_up_ref[HALF:, :], passed_down_ref[HALF:, :], passed_up_ref[:HALF, :], passed_down_ref[:HALF, :]),
     ]
     for by, left, right, _, _ in sides:
-        at = pl.ds(pl.multiple_of(32 * far_place(by), 32), 32)
+        at = pl.ds(pl.multiple_of(64 * far_place(by), 64), 64)
         left_ref[at, :] = left
         right_ref[at, :] = right
     halves = [split(left_ref[...]), split(right_ref[...])]
     for by, _, _, top, bottom in sides:
-        rows = split(jnp.concatenate([top, bottom], axis=0))
-        products = [dot3(rows, half) for half in halves]
-        at = pl.ds(pl.multiple_of(40 * far_place(by), 8), 40)
+        rows = split(jnp.concatenate([top, bottom], axis=1))
+        for half in range(2):
+            sum_ref[half] = dot3(rows, halves[half])
         for near in range(NEAR):
             half, place = divmod(near, ELEMS)
-            out_ref[near, at, :] = by_owner(
-                [turned(products[half][40 * e : 40 * e + 40], e - place) for e in range(ELEMS)]
+            out_ref[near, pl.ds(20 * by, 20), :] = by_owner(
+                [turned(sum_ref[half, pl.ds(20 * e, 20), :], e - place) for e in range(ELEMS)]
             )
 
 
-def add_up(parts_ref, live_ref, out_ref):
-    total = parts_ref[0]
-    for near in range(1, NEAR):
-        total = total + parts_ref[near]
-    out_ref[...] = jnp.where(live_ref[...] > 0.5, total, 0.0)
+def add_up(parts_ref, live_ref, out_ref, sum_ref, rows_ref):
+    for share in range(2):
+        total = parts_ref[share]
+        for low in range(1, LOW):
+            total = total + parts_ref[2 * low + share]
+        sum_ref[share] = total
+    for by in range(FAR):
+        for share in range(2):
+            for low in range(LOW):
+                rows_ref[pl.ds(10 * low + PIECE * share, PIECE), :] = sum_ref[share, pl.ds(20 * by + PIECE * low, PIECE), :]
+        at = pl.ds(pl.multiple_of(40 * far_place(by), 8), 40)
+        out_ref[at, :] = jnp.where(live_ref[at, :] > 0.5, rows_ref[...], 0.0)
 
 
 def split_blocks(hamiltonian_ref, high_ref, low_ref):
@@ -211,21 +223,22 @@
 
 def shards(orbitals, rotation, counts, hamiltonian, center, width):
     pieces = jnp.transpose(orbitals, (1, 0, 2))
-    shapes = ((NEAR, ELEMS * PIECE, WIDE), (FAR, 64, WIDE), (ROWS, WIDE))
-    cut, slices, live = call(cut_columns, shapes, 0, 6 * FIELD, (V, V, S))(pieces, rotation, counts)
-    cut = lax.all_to_all(cut, NEARS, split_axis=0, concat_axis=0, tiled=True)
-    message = (2 * PASS + 32, WIDE)
-    up, down = call(pack, (message, message), 0, 6 * FIELD, (V, V))(cut, slices)
+    other = lax.ppermute(rotation, "y_hi", [(0, 1), (1, 0)])
+    cut, live = call(cut_columns, ((LOW, 2 * ELEMS * PIECE, WIDE), (ROWS, WIDE)), 0, 3 * FIELD, (V, S))(pieces, counts)
+    cut = lax.all_to_all(cut, "z_lo", split_axis=0, concat_axis=0, tiled=True)
+    message = (2 * PASS + 64, WIDE)
+    up, down, slices = call(pack, (message, message, (WIDE, WIDE)), 0, 8 * FIELD, (V,) * 3)(cut, rotation, other)
     above, below = far_step(down, -1), far_step(up, 1)
     passed_up, passed_down = far_step(below[:PASS], 1), far_step(above[:PASS], -1)
     blocks = call(split_blocks, (hamiltonian.shape,) * 2, 0, 2 * BLOCKS, (V,), (), BF16)(hamiltonian)
     slices, *blocks = lax.optimization_barrier((slices, *blocks))
-    scratch = [V((WIDE, WIDE), F32)] * 2
-    parts = call(rotate, (NEAR, ROWS, WIDE), 6 * 640 * 128 * 256, 13 * FIELD, (V,) * 7, scratch)(
+    scratch = [V((256, WIDE), F32)] * 2 + [V((2, HALF, WIDE), F32)]
+    parts = call(rotate, (NEAR, HALF, WIDE), 6 * 320 * 256 * 256, 11 * FIELD, (V,) * 7, scratch)(
         up, down, slices, below, above, passed_up, passed_down
     )
     parts = lax.all_to_all(parts, NEARS, split_axis=0, concat_axis=0, tiled=True)
-    start = call(add_up, (ROWS, WIDE), 0, 9 * FIELD, (V, V))(parts, live)
+    scratch = [V((2, HALF, WIDE), F32), V((40, WIDE), F32)]
+    start = call(add_up, (ROWS, WIDE), 0, 5 * FIELD, (V, V), scratch)(parts, live)
 
     own = call(own_and_ring, (ROWS, WIDE), 6 * 20 * ROWS * ROWS * WIDE, BLOCKS, (V,) * 5)
     first = call(first_step, (ROWS, WIDE), 6 * 8 * ROWS * ROWS * WIDE, BLOCKS // 3, (V,) * 7 + (S,) * 2)

time: 116 us -> 118 us (1.017)
  blocking collectives: 46.6 us -> 22.1 us
  starting transfers between devices: 43.3 us -> 65 us
  waiting for transfers between devices: 13.1 us -> 17.3 us
    all_to_all x1 -> x0, blocking collectives: 22.5 us -> none  [shards(): cut = lax.all_to_all(cut, NEARS, split_axis=0, concat_axis=0, tiled=True)]
    ppermute x4, starting transfers between devices: 25.7 us -> 35.8 us  [far_step(): return lax.ppermute(v, 'z_hi', [(i, (i + by) % FAR) for i in range(FAR)])]
    all_to_all x0 -> x1, starting transfers between devices: none -> 7.26 us  [shards(): cut = lax.all_to_all(cut, 'z_lo', split_axis=0, concat_axis=0, tiled=True)]
    ppermute x0 -> x1, starting transfers between devices: none -> 6.82 us  [shards(): other = lax.ppermute(rotation, 'y_hi', [(0, 1), (1, 0)])]
    ppermute x0 -> x1, waiting for transfers between devices: none -> 6.79 us  [shards(): other = lax.ppermute(rotation, 'y_hi', [(0, 1), (1, 0)])]
    ppermute x4, waiting for transfers between devices: 11.5 us -> 5.36 us  [far_step(): return lax.ppermute(v, 'z_hi', [(i, (i + by) % FAR) for i in range(FAR)])]
    ppermute x2, waiting for transfers between devices: 1.57 us -> 5.12 us  [neighbours(): lax.ppermute(field, 'layer', [(i + 1, i) for i in range(LAYERS - 1)])]
    ppermute x2, starting transfers between devices: 5.89 us -> 2.96 us  [neighbours(): lax.ppermute(field, RING, [(i, (i - 1) % ring) for i in range(ring)])]
  transfers between devices with their start and end apart: 12 -> 14, of which waited for: 5 -> 5; matrix products, arithmetic and copies ran while one was open for 0% -> 0% of each run, Pallas kernels for 2% -> 2%
where the time goes in v4:
time: 118 us; the launch traced here: 117 us
  starting transfers between devices  65 us (55%)
  blocking collectives  22.1 us (19%)
  waiting for transfers between devices  17.3 us (15%)
  Pallas kernels  6.58 us (6%)
  local copies, waits for them, and re-layouts  4.75 us (4%)
  between operations  1.51 us (1%)
    ppermute x4, starting transfers between devices, far_step(): return lax.ppermute(v, 'z_hi', [(i, (i + by) % FAR) for i in range(FAR)])  35.8 us
    all_to_all x1, blocking collectives, shards(): lax.all_to_all(parts, NEARS, split_axis=0, concat_axis=0, tiled=True)  22.1 us
    all_to_all x1, starting transfers between devices, shards(): cut = lax.all_to_all(cut, 'z_lo', split_axis=0, concat_axis=0, tiled=True)  7.26 us
    ppermute x1, starting transfers between devices, shards(): other = lax.ppermute(rotation, 'y_hi', [(0, 1), (1, 0)])  6.82 us
    ppermute x1, waiting for transfers between devices, shards(): other = lax.ppermute(rotation, 'y_hi', [(0, 1), (1, 0)])  6.79 us
    ppermute x2, starting transfers between devices, neighbours(): lax.ppermute(field, 'layer', [(i + 1, i) for i in range(LAYERS - 1)])  5.84 us
    ppermute x2, starting transfers between devices, neighbours(): lax.ppermute(field, 'layer', [(i, i + 1) for i in range(LAYERS - 1)])  5.82 us
    ppermute x4, waiting for transfers between devices, far_step(): return lax.ppermute(v, 'z_hi', [(i, (i + by) % FAR) for i in range(FAR)])  5.36 us
  transfers between devices with their start and end apart: 14, of which 5 were waited for; matrix products, arithmetic and copies ran while one was open for 0% of the time, Pallas kernels for 2%

profile of v4, /device:TPU:8, one launch (start us, length us, event | category | flops | bytes accessed | tf_op | source)
XLA Modules:
  0.0 117.2 jit_solution(9224810338333769076)
XLA Ops:
  0.0 0.0 copy-start.2
  0.0 0.9 copy-done.2
  0.9 0.0 copy-start.3
  0.9 0.7 copy-done.3
  1.5 1.3 %shard_map.64 = (f32[4,40,128]{2,1,0:T(8,128)}, f32[160,128]{1,0:T(8,128)S(1)}) custom-call(f32[5,4,1024]{2,1,0:T(4,128)S(1)} %bitcast.4, s32[4]{0:T(128)S(1)} %copy-done.3), custom_call_target="tpu_custom_call" | custom-call | bytes 245760 | tf_op jit(solution)/shard_map/pallas_call | solution.py:227
  2.8 7.3 %all-to-all-start = ((f32[4,40,128]{2,1,0:T(8,128)}), f32[4,40,128]{2,1,0:T(8,128)S(1)}, u32[]{:S(2)}, u32[]{:S(2)}) async-start(f32[4,40,128]{2,1,0:T(8,128)} %get-tuple-element.15), calls=%async_computation | async-start | bytes 163840 | tf_op jit(solution)/shard_map/all_to_all | solution.py:228
  10.1 6.8 %collective-permute-start = (f32[32,1024]{1,0:T(8,128)}, f32[32,1024]{1,0:T(8,128)S(1)}, u32[]{:S(2)}, u32[]{:S(2)}) collective-permute-start(f32[32,1024]{1,0:T(8,128)} %mine_ref.1), channel_id=1, source_target_pairs={{0,1},{1,0},{2,3},{3,2},{4,5},{5,4},{6,7},{7,6},{8,9},{9,8},{10,11... | collective-permute-start | bytes 393224 | tf_op jit(solution)/shard_map/ppermute | solution.py:226
  16.9 6.8 %collective-permute-done.other_ref = f32[32,1024]{1,0:T(8,128)S(1)} collective-permute-done((f32[32,1024]{1,0:T(8,128)}, f32[32,1024]{1,0:T(8,128)S(1)}, u32[]{:S(2)}, u32[]{:S(2)}) %collective-permute-start) | collective-permute-done | bytes 131104 | tf_op jit(solution)/shard_map/ppermute | solution.py:226
  23.7 0.0 all-to-all-done.rows_ref
  23.7 0.0 copy-start.1
  23.7 0.9 copy-done.1
  24.6 0.1 shard_map.65
  24.7 10.9 %collective-permute-start.1 = (f32[352,128]{1,0:T(8,128)S(1)}, f32[352,128]{1,0:T(8,128)S(1)}, u32[]{:S(2)}, u32[]{:S(2)}) collective-permute-start(f32[352,128]{1,0:T(8,128)S(1)} %get-tuple-element.16.up_ref), channel_id=1, source_target_pairs={{0,8},{8,16},{16,24},{24,0},{1,9},{9,17},{17,25},{25,1},{2,10},{10... | collective-permute-start | bytes 540680 | tf_op jit(solution)/shard_map/ppermute | solution.py:216
  35.7 6.5 %collective-permute-start.2 = (f32[352,128]{1,0:T(8,128)S(1)}, f32[352,128]{1,0:T(8,128)S(1)}, u32[]{:S(2)}, u32[]{:S(2)}) collective-permute-start(f32[352,128]{1,0:T(8,128)S(1)} %get-tuple-element.17.down_ref), channel_id=1, source_target_pairs={{0,24},{8,0},{16,8},{24,16},{1,25},{9,1},{17,9},{25,17},{2,26},{10... | collective-permute-start | bytes 540680 | tf_op jit(solution)/shard_map/ppermute | solution.py:216
  42.2 1.9 %collective-permute-done.1.below_ref = f32[352,128]{1,0:T(8,128)S(1)} collective-permute-done((f32[352,128]{1,0:T(8,128)S(1)}, f32[352,128]{1,0:T(8,128)S(1)}, u32[]{:S(2)}, u32[]{:S(2)}) %collective-permute-start.1) | collective-permute-done | bytes 180256 | tf_op jit(solution)/shard_map/ppermute | solution.py:216
  44.0 12.4 %collective-permute-start.3 = (f32[144,128]{1,0:T(8,128)S(1)}, f32[144,128]{1,0:T(8,128)S(1)}, u32[]{:S(2)}, u32[]{:S(2)}) collective-permute-start(f32[144,128]{1,0:T(8,128)S(1)} %slice.8), channel_id=1, source_target_pairs={{0,8},{8,16},{16,24},{24,0},{1,9},{9,17},{17,25},{25,1},{2,10},{10... | collective-permute-start | bytes 221192 | tf_op jit(solution)/shard_map/ppermute | solution.py:216
  56.5 0.0 collective-permute-done.2.above_ref
  56.5 6.0 %collective-permute-start.4 = (f32[144,128]{1,0:T(8,128)S(1)}, f32[144,128]{1,0:T(8,128)S(1)}, u32[]{:S(2)}, u32[]{:S(2)}) collective-permute-start(f32[144,128]{1,0:T(8,128)S(1)} %slice.9), channel_id=1, source_target_pairs={{0,24},{8,0},{16,8},{24,16},{1,25},{9,1},{17,9},{25,17},{2,26},{10... | collective-permute-start | bytes 221192 | tf_op jit(solution)/shard_map/ppermute | solution.py:216
  62.5 0.0 copy-start
  62.5 2.3 %copy-done = f32[4,7,160,160]{3,2,1,0:T(8,128)S(1)} copy-done((f32[4,7,160,160]{3,2,1,0:T(8,128)S(1)}, f32[4,7,160,160]{3,2,1,0:T(8,128)}, u32[]{:S(2)}) %copy-start) | copy-done | bytes 2867224
  64.8 0.6 shard_map.66
  65.4 0.0 collective-permute-done.3.passed_up_ref
  65.4 3.5 %collective-permute-done.4.passed_down_ref = f32[144,128]{1,0:T(8,128)S(1)} collective-permute-done((f32[144,128]{1,0:T(8,128)S(1)}, f32[144,128]{1,0:T(8,128)S(1)}, u32[]{:S(2)}, u32[]{:S(2)}) %collective-permute-start.4) | collective-permute-done | bytes 73760 | tf_op jit(solution)/shard_map/ppermute | solution.py:216
  68.9 0.6 shard_map.67
  69.5 22.1 %all_to_all.10.parts_ref = f32[8,80,128]{2,1,0:T(8,128)S(1)} all-to-all(f32[8,80,128]{2,1,0:T(8,128)S(1)} %shard_map.67), channel_id=1, replica_groups=mesh['layer'=4,'column'=4,'core'=2,'z_hi'=4,'z_lo'=4,'y_hi'=2] {'z_lo','..., dimensions={0} | all-to-all | bytes 655360 | tf_op jit(solution)/shard_map/all_to_all | solution.py:239
  91.6 0.1 shard_map.68.field_ref.start_ref
  91.7 0.0 collective-permute-start.5
  91.7 2.9 %collective-permute-start.6 = (f32[160,128]{1,0:T(8,128)S(1)}, f32[160,128]{1,0:T(8,128)S(1)}, u32[]{:S(2)}, u32[]{:S(2)}) collective-permute-start(f32[160,128]{1,0:T(8,128)S(1)} %shard_map.68.field_ref.start_ref), channel_id=1, source_target_pairs={{0,224},{32,0},{64,32},{96,64},{128,96},{160,128},{192,160},{224,1... | collective-permute-start | bytes 245768 | tf_op jit(solution)/shard_map/ppermute | solution.py:209
  94.6 1.9 %collective-permute-start.7 = (f32[160,128]{1,0:T(8,128)S(1)}, f32[160,128]{1,0:T(8,128)S(1)}, u32[]{:S(2)}, u32[]{:S(2)}) collective-permute-start(f32[160,128]{1,0:T(8,128)S(1)} %shard_map.68.field_ref.start_ref), channel_id=1, source_target_pairs={{0,256},{256,512},{512,768},{1,257},{257,513},{513,769},{2,258},{2... | collective-permute-start | bytes 245768 | tf_op jit(solution)/shard_map/ppermute | solution.py:210
  96.5 3.9 %collective-permute-start.8 = (f32[160,128]{1,0:T(8,128)S(1)}, f32[160,128]{1,0:T(8,128)S(1)}, u32[]{:S(2)}, u32[]{:S(2)}) collective-permute-start(f32[160,128]{1,0:T(8,128)S(1)} %shard_map.68.field_ref.start_ref), channel_id=1, source_target_pairs={{256,0},{512,256},{768,512},{257,1},{513,257},{769,513},{258,2},{5... | collective-permute-start | bytes 245768 | tf_op jit(solution)/shard_map/ppermute | solution.py:211
  101.8 0.0 collective-permute-done.5.a_ref
  101.8 0.0 collective-permute-done.6.b_ref
  101.8 1.1 shard_map.69.own_ref
  102.9 0.0 collective-permute-done.7.c_ref
  102.9 1.8 %collective-permute-done.8.d_ref = f32[160,128]{1,0:T(8,128)S(1)} collective-permute-done((f32[160,128]{1,0:T(8,128)S(1)}, f32[160,128]{1,0:T(8,128)S(1)}, u32[]{:S(2)}, u32[]{:S(2)}) %collective-permute-start.8) | collective-permute-done | bytes 81952 | tf_op jit(solution)/shard_map/ppermute | solution.py:211
  104.7 0.5 shard_map.70.field_ref.middle_ref
  105.2 0.0 collective-permute-start.10
  105.2 0.5 collective-permute-start.9
  105.7 3.9 %collective-permute-start.11 = (f32[160,128]{1,0:T(8,128)S(1)}, f32[160,128]{1,0:T(8,128)S(1)}, u32[]{:S(2)}, u32[]{:S(2)}) collective-permute-start(f32[160,128]{1,0:T(8,128)S(1)} %shard_map.70.field_ref.middle_ref), channel_id=1, source_target_pairs={{0,256},{256,512},{512,768},{1,257},{257,513},{513,769},{2,258},{2... | collective-permute-start | bytes 245768 | tf_op jit(solution)/shard_map/ppermute | solution.py:210
  109.7 1.9 %collective-permute-start.12 = (f32[160,128]{1,0:T(8,128)S(1)}, f32[160,128]{1,0:T(8,128)S(1)}, u32[]{:S(2)}, u32[]{:S(2)}) collective-permute-start(f32[160,128]{1,0:T(8,128)S(1)} %shard_map.70.field_ref.middle_ref), channel_id=1, source_target_pairs={{256,0},{512,256},{768,512},{257,1},{513,257},{769,513},{258,2},{5... | collective-permute-start | bytes 245768 | tf_op jit(solution)/shard_map/ppermute | solution.py:211
  111.6 0.0 collective-permute-done.10.b_ref
  111.6 0.0 collective-permute-done.9.a_ref
  111.6 1.1 shard_map.71.own_ref
  112.7 0.0 collective-permute-done.11.c_ref
  112.7 3.3 %collective-permute-done.12.d_ref = f32[160,128]{1,0:T(8,128)S(1)} collective-permute-done((f32[160,128]{1,0:T(8,128)S(1)}, f32[160,128]{1,0:T(8,128)S(1)}, u32[]{:S(2)}, u32[]{:S(2)}) %collective-permute-start.12) | collective-permute-done | bytes 81952 | tf_op jit(solution)/shard_map/ppermute | solution.py:211
  116.0 1.3 %shard_map.72 = f32[128,160]{1,0:T(8,128)} custom-call(f32[160,128]{1,0:T(8,128)S(1)} %shard_map.71.own_ref, f32[160,128]{1,0:T(8,128)S(1)} %collective-permute-done.11.c_ref, f32[160,128]{1,0:T(8,128)S(1)} %collective-permute-done.12.d_ref, bf16[4,7,160,160]{3,2,1,0:T(8,128)(2,1)S(1)} %get-tuple-element.23.high_ref, ...), custom_call_target="tpu_custom_call" | custom-call | flops 157286400 | bytes 1529173 | tf_op jit(solution)/shard_map/pallas_call | solution.py:251
  (2 shorter events, 0.0 us)
Async XLA Ops:
  0.0 0.9 copy-start.2
  0.9 0.7 copy-start.3
  2.8 20.9 %all-to-all-start = ((f32[4,40,128]{2,1,0:T(8,128)}), f32[4,40,128]{2,1,0:T(8,128)S(1)}, u32[]{:S(2)}, u32[]{:S(2)}) async-start(f32[4,40,128]{2,1,0:T(8,128)} %get-tuple-element.15), calls=%async_computation | async-start | bytes 163840 | tf_op jit(solution)/shard_map/all_to_all | solution.py:228
  10.1 13.6 %collective-permute-start = (f32[32,1024]{1,0:T(8,128)}, f32[32,1024]{1,0:T(8,128)S(1)}, u32[]{:S(2)}, u32[]{:S(2)}) collective-permute-start(f32[32,1024]{1,0:T(8,128)} %mine_ref.1), channel_id=1, source_target_pairs={{0,1},{1,0},{2,3},{3,2},{4,5},{5,4},{6,7},{7,6},{8,9},{9,8},{10,11... | collective-permute-start | bytes 393224 | tf_op jit(solution)/shard_map/ppermute | solution.py:226
  23.7 0.9 copy-start.1
  24.7 19.3 %collective-permute-start.1 = (f32[352,128]{1,0:T(8,128)S(1)}, f32[352,128]{1,0:T(8,128)S(1)}, u32[]{:S(2)}, u32[]{:S(2)}) collective-permute-start(f32[352,128]{1,0:T(8,128)S(1)} %get-tuple-element.16.up_ref), channel_id=1, source_target_pairs={{0,8},{8,16},{16,24},{24,0},{1,9},{9,17},{17,25},{25,1},{2,10},{10... | collective-permute-start | bytes 540680 | tf_op jit(solution)/shard_map/ppermute | solution.py:216
  35.7 20.8 %collective-permute-start.2 = (f32[352,128]{1,0:T(8,128)S(1)}, f32[352,128]{1,0:T(8,128)S(1)}, u32[]{:S(2)}, u32[]{:S(2)}) collective-permute-start(f32[352,128]{1,0:T(8,128)S(1)} %get-tuple-element.17.down_ref), channel_id=1, source_target_pairs={{0,24},{8,0},{16,8},{24,16},{1,25},{9,1},{17,9},{25,17},{2,26},{10... | collective-permute-start | bytes 540680 | tf_op jit(solution)/shard_map/ppermute | solution.py:216
  44.0 21.4 %collective-permute-start.3 = (f32[144,128]{1,0:T(8,128)S(1)}, f32[144,128]{1,0:T(8,128)S(1)}, u32[]{:S(2)}, u32[]{:S(2)}) collective-permute-start(f32[144,128]{1,0:T(8,128)S(1)} %slice.8), channel_id=1, source_target_pairs={{0,8},{8,16},{16,24},{24,0},{1,9},{9,17},{17,25},{25,1},{2,10},{10... | collective-permute-start | bytes 221192 | tf_op jit(solution)/shard_map/ppermute | solution.py:216
  56.5 12.4 %collective-permute-start.4 = (f32[144,128]{1,0:T(8,128)S(1)}, f32[144,128]{1,0:T(8,128)S(1)}, u32[]{:S(2)}, u32[]{:S(2)}) collective-permute-start(f32[144,128]{1,0:T(8,128)S(1)} %slice.9), channel_id=1, source_target_pairs={{0,24},{8,0},{16,8},{24,16},{1,25},{9,1},{17,9},{25,17},{2,26},{10... | collective-permute-start | bytes 221192 | tf_op jit(solution)/shard_map/ppermute | solution.py:216
  62.5 2.3 %copy-start = (f32[4,7,160,160]{3,2,1,0:T(8,128)S(1)}, f32[4,7,160,160]{3,2,1,0:T(8,128)}, u32[]{:S(2)}) copy-start(f32[4,7,160,160]{3,2,1,0:T(8,128)} %hamiltonian_ref.1) | copy-start | bytes 8601604
  91.7 10.1 %collective-permute-start.5 = (f32[160,128]{1,0:T(8,128)S(1)}, f32[160,128]{1,0:T(8,128)S(1)}, u32[]{:S(2)}, u32[]{:S(2)}) collective-permute-start(f32[160,128]{1,0:T(8,128)S(1)} %shard_map.68.field_ref.start_ref), channel_id=1, source_target_pairs={{0,32},{32,64},{64,96},{96,128},{128,160},{160,192},{192,224},{224... | collective-permute-start | bytes 245768 | tf_op jit(solution)/shard_map/ppermute | solution.py:208
  91.7 10.1 %collective-permute-start.6 = (f32[160,128]{1,0:T(8,128)S(1)}, f32[160,128]{1,0:T(8,128)S(1)}, u32[]{:S(2)}, u32[]{:S(2)}) collective-permute-start(f32[160,128]{1,0:T(8,128)S(1)} %shard_map.68.field_ref.start_ref), channel_id=1, source_target_pairs={{0,224},{32,0},{64,32},{96,64},{128,96},{160,128},{192,160},{224,1... | collective-permute-start | bytes 245768 | tf_op jit(solution)/shard_map/ppermute | solution.py:209
  94.6 8.2 %collective-permute-start.7 = (f32[160,128]{1,0:T(8,128)S(1)}, f32[160,128]{1,0:T(8,128)S(1)}, u32[]{:S(2)}, u32[]{:S(2)}) collective-permute-start(f32[160,128]{1,0:T(8,128)S(1)} %shard_map.68.field_ref.start_ref), channel_id=1, source_target_pairs={{0,256},{256,512},{512,768},{1,257},{257,513},{513,769},{2,258},{2... | collective-permute-start | bytes 245768 | tf_op jit(solution)/shard_map/ppermute | solution.py:210
  96.5 8.2 %collective-permute-start.8 = (f32[160,128]{1,0:T(8,128)S(1)}, f32[160,128]{1,0:T(8,128)S(1)}, u32[]{:S(2)}, u32[]{:S(2)}) collective-permute-start(f32[160,128]{1,0:T(8,128)S(1)} %shard_map.68.field_ref.start_ref), channel_id=1, source_target_pairs={{256,0},{512,256},{768,512},{257,1},{513,257},{769,513},{258,2},{5... | collective-permute-start | bytes 245768 | tf_op jit(solution)/shard_map/ppermute | solution.py:211
  105.2 6.4 %collective-permute-start.10 = (f32[160,128]{1,0:T(8,128)S(1)}, f32[160,128]{1,0:T(8,128)S(1)}, u32[]{:S(2)}, u32[]{:S(2)}) collective-permute-start(f32[160,128]{1,0:T(8,128)S(1)} %shard_map.70.field_ref.middle_ref), channel_id=1, source_target_pairs={{0,224},{32,0},{64,32},{96,64},{128,96},{160,128},{192,160},{224,1... | collective-permute-start | bytes 245768 | tf_op jit(solution)/shard_map/ppermute | solution.py:209
  105.2 6.4 %collective-permute-start.9 = (f32[160,128]{1,0:T(8,128)S(1)}, f32[160,128]{1,0:T(8,128)S(1)}, u32[]{:S(2)}, u32[]{:S(2)}) collective-permute-start(f32[160,128]{1,0:T(8,128)S(1)} %shard_map.70.field_ref.middle_ref), channel_id=1, source_target_pairs={{0,32},{32,64},{64,96},{96,128},{128,160},{160,192},{192,224},{224... | collective-permute-start | bytes 245768 | tf_op jit(solution)/shard_map/ppermute | solution.py:208
  105.7 7.0 %collective-permute-start.11 = (f32[160,128]{1,0:T(8,128)S(1)}, f32[160,128]{1,0:T(8,128)S(1)}, u32[]{:S(2)}, u32[]{:S(2)}) collective-permute-start(f32[160,128]{1,0:T(8,128)S(1)} %shard_map.70.field_ref.middle_ref), channel_id=1, source_target_pairs={{0,256},{256,512},{512,768},{1,257},{257,513},{513,769},{2,258},{2... | collective-permute-start | bytes 245768 | tf_op jit(solution)/shard_map/ppermute | solution.py:210
  109.7 6.3 %collective-permute-start.12 = (f32[160,128]{1,0:T(8,128)S(1)}, f32[160,128]{1,0:T(8,128)S(1)}, u32[]{:S(2)}, u32[]{:S(2)}) collective-permute-start(f32[160,128]{1,0:T(8,128)S(1)} %shard_map.70.field_ref.middle_ref), channel_id=1, source_target_pairs={{256,0},{512,256},{768,512},{257,1},{513,257},{769,513},{258,2},{5... | collective-permute-start | bytes 245768 | tf_op jit(solution)/shard_map/ppermute | solution.py:211

commit v5 on v4

--- a/solution.py
+++ b/solution.py
@@ -71,7 +71,10 @@
     return row < limit
 
 
-def cut_columns(orbitals_ref, counts_ref, out_ref, live_ref):
+def cut_columns(orbitals_ref, rotation_ref, counts_ref, out_ref, mine_ref, live_ref):
+    for far in range(FAR):
+        lanes = pl.ds(pl.multiple_of(256 * far + 128 * lax.axis_index("core"), 128), 128)
+        mine_ref[far] = rotation_ref[:, lanes]
     live_ref[...] = jnp.where(alive(counts_ref), 1.0, 0.0)
     first = lax.broadcasted_iota(jnp.int32, (ELEMS, WIDE), 1) < 64
     for i in range(PIECE):
@@ -88,7 +91,7 @@
 
 
 HALF = ROWS // 2
-PASS = HALF + 64
+PASS = HALF + 32
 
 
 def pack(rows_ref, mine_ref, other_ref, up_ref, down_ref, own_ref):
@@ -101,37 +104,40 @@
                     row = rows_ref[low, pl.ds(20 * k + ELEMS * i + e, 1), :]
                     first[pl.ds(at, 1), :] = row
                     second[pl.ds(PASS + at, 1), :] = row
-    here = lax.axis_index("y_hi")
-    for place, ref in ((here, mine_ref), (1 - here, other_ref)):
-
-        def put(to, start, far, half):
-            lanes = pl.ds(pl.multiple_of(256 * far + 128 * half, 128), 128)
-            to[pl.ds(pl.multiple_of(start + 32 * place, 16), 32), :] = ref[:, lanes]
-
-        put(up_ref, HALF, far_place(2), 0)
-        put(down_ref, HALF, far_place(2), 1)
-        for half in range(2):
-            put(up_ref, PASS + HALF + 64 * half, far_place(1), half)
-            put(down_ref, PASS + HALF + 64 * half, far_place(3), half)
-            put(own_ref, 64 * half, far_place(0), half)
+    lower = lax.axis_index("y_hi") == 0
+
+    def slices(by):
+        mine, other = mine_ref[far_place(by)], other_ref[far_place(by)]
+        return jnp.where(lower, mine, other), jnp.where(lower, other, mine)
+
+    up_ref[HALF:PASS, :], down_ref[HALF:PASS, :] = slices(2)
+    tail = PASS + HALF
+    up_ref[tail : tail + 32, :], up_ref[tail + 32 :, :] = slices(1)
+    down_ref[tail : tail + 32, :], down_ref[tail + 32 :, :] = slices(3)
+    own_ref[:32, :], own_ref[32:, :] = slices(0)
+
+
+def collect(own_ref, below_ref, above_ref, passed_up_ref, passed_down_ref, out_ref):
+    tail = PASS + HALF
+    passed = jnp.concatenate([passed_up_ref[HALF:, :], passed_down_ref[HALF:, :]], axis=0)
+    for by, piece in ((0, own_ref[...]), (3, below_ref[tail:, :]), (1, above_ref[tail:, :]), (2, passed)):
+        out_ref[pl.ds(pl.multiple_of(64 * far_place(by), 64), 64), :] = piece
 
 
 def rotate(
-    up_ref, down_ref, own_ref, below_ref, above_ref, passed_up_ref, passed_down_ref, out_ref, left_ref, right_ref, sum_ref
+    up_ref, down_ref, mine_ref, other_ref, below_ref, above_ref, passed_up_ref, passed_down_ref, out_ref, sum_ref
 ):
     tail = PASS + HALF
     sides = [
-        (0, own_ref[:64, :], own_ref[64:, :], up_ref[:HALF, :], down_ref[:HALF, :]),
-        (3, below_ref[tail : tail + 64, :], below_ref[tail + 64 :, :], below_ref[:HALF, :], below_ref[PASS:tail, :]),
-        (1, above_ref[tail : tail + 64, :], above_ref[tail + 64 :, :], above_ref[PASS:tail, :], above_ref[:HALF, :]),
-        (2, passed_up_ref[HALF:, :], passed_down_ref[HALF:, :], passed_up_ref[:HALF, :], passed_down_ref[:HALF, :]),
+        (0, up_ref[:HALF, :], down_ref[:HALF, :]),
+        (3, below_ref[:HALF, :], below_ref[PASS:tail, :]),
+        (1, above_ref[PASS:tail, :], above_ref[:HALF, :]),
+        (2, passed_up_ref[:HALF, :], passed_down_ref[:HALF, :]),
     ]
-    for by, left, right, _, _ in sides:
-        at = pl.ds(pl.multiple_of(64 * far_place(by), 64), 64)
-        left_ref[at, :] = left
-        right_ref[at, :] = right
-    halves = [split(left_ref[...]), split(right_ref[...])]
-    for by, _, _, top, bottom in sides:
+    first = lax.axis_index("core") == 0
+    mine, other = mine_ref[...], other_ref[...]
+    halves = [split(jnp.where(first, mine, other)), split(jnp.where(first, other, mine))]
+    for by, top, bottom in sides:
         rows = split(jnp.concatenate([top, bottom], axis=1))
         for half in range(2):
             sum_ref[half] = dot3(rows, halves[half])
@@ -223,18 +229,21 @@
 
 def shards(orbitals, rotation, counts, hamiltonian, center, width):
     pieces = jnp.transpose(orbitals, (1, 0, 2))
-    other = lax.ppermute(rotation, "y_hi", [(0, 1), (1, 0)])
-    cut, live = call(cut_columns, ((LOW, 2 * ELEMS * PIECE, WIDE), (ROWS, WIDE)), 0, 3 * FIELD, (V, S))(pieces, counts)
+    shapes = ((LOW, 2 * ELEMS * PIECE, WIDE), (FAR, 32, WIDE), (ROWS, WIDE))
+    cut, mine, live = call(cut_columns, shapes, 0, 4 * FIELD, (V, V, S))(pieces, rotation, counts)
+    other = lax.ppermute(mine, "y_hi", [(0, 1), (1, 0)])
     cut = lax.all_to_all(cut, "z_lo", split_axis=0, concat_axis=0, tiled=True)
-    message = (2 * PASS + 64, WIDE)
-    up, down, slices = call(pack, (message, message, (WIDE, WIDE)), 0, 8 * FIELD, (V,) * 3)(cut, rotation, other)
+    message = (2 * PASS + 32, WIDE)
+    up, down, slices = call(pack, (message, message, (64, WIDE)), 0, 6 * FIELD, (V,) * 3)(cut, mine, other)
     above, below = far_step(down, -1), far_step(up, 1)
     passed_up, passed_down = far_step(below[:PASS], 1), far_step(above[:PASS], -1)
     blocks = call(split_blocks, (hamiltonian.shape,) * 2, 0, 2 * BLOCKS, (V,), (), BF16)(hamiltonian)
     slices, *blocks = lax.optimization_barrier((slices, *blocks))
-    scratch = [V((256, WIDE), F32)] * 2 + [V((2, HALF, WIDE), F32)]
-    parts = call(rotate, (NEAR, HALF, WIDE), 6 * 320 * 256 * 256, 11 * FIELD, (V,) * 7, scratch)(
-        up, down, slices, below, above, passed_up, passed_down
+    mine = call(collect, (256, WIDE), 0, 4 * FIELD, (V,) * 5)(slices, below, above, passed_up, passed_down)
+    other = lax.ppermute(mine, "core", [(0, 1), (1, 0)])
+    scratch = [V((2, HALF, WIDE), F32)]
+    parts = call(rotate, (NEAR, HALF, WIDE), 6 * 320 * 256 * 256, 11 * FIELD, (V,) * 8, scratch)(
+        up, down, mine, other, below, above, passed_up, passed_down
     )
     parts = lax.all_to_all(parts, NEARS, split_axis=0, concat_axis=0, tiled=True)
     scratch = [V((2, HALF, WIDE), F32), V((40, WIDE), F32)]

time: 118 us -> 116 us (0.983)
  waiting for transfers between devices: 17.3 us -> 10.4 us
  blocking collectives: 22.1 us -> 24.5 us
  starting transfers between devices: 65 us -> 67.3 us
    ppermute x2, starting transfers between devices: 2.96 us -> 5.89 us  [neighbours(): lax.ppermute(field, RING, [(i, (i - 1) % ring) for i in range(ring)])]
    ppermute x4, waiting for transfers between devices: 5.36 us -> 2.72 us  [far_step(): return lax.ppermute(v, 'z_hi', [(i, (i + by) % FAR) for i in range(FAR)])]
    all_to_all x1, blocking collectives: 22.1 us -> 24.5 us  [shards(): lax.all_to_all(parts, NEARS, split_axis=0, concat_axis=0, tiled=True)]
    ppermute x1 -> x2, waiting for transfers between devices: 6.79 us -> 4.64 us  [the longest x1 3.33 us: shards(): other = lax.ppermute(mine, 'y_hi', [(0, 1), (1, 0)])]
    ppermute x2, waiting for transfers between devices: 5.12 us -> 2.98 us  [neighbours(): lax.ppermute(field, 'layer', [(i + 1, i) for i in range(LAYERS - 1)])]
    ppermute x4, starting transfers between devices: 35.8 us -> 33.7 us  [far_step(): return lax.ppermute(v, 'z_hi', [(i, (i + by) % FAR) for i in range(FAR)])]
    ppermute x1 -> x2, starting transfers between devices: 6.82 us -> 8.74 us  [the longest x1 6.82 us: shards(): other = lax.ppermute(mine, 'y_hi', [(0, 1), (1, 0)])]
  transfers between devices with their start and end apart: 14 -> 15, of which waited for: 5 -> 6; matrix products, arithmetic and copies ran while one was open for 0% -> 0% of each run, Pallas kernels for 2% -> 2%
where the time goes in v5:
time: 116 us; the launch traced here: 115 us
  starting transfers between devices  67.3 us (58%)
  blocking collectives  24.5 us (21%)
  waiting for transfers between devices  10.4 us (9%)
  Pallas kernels  6.56 us (6%)
  local copies, waits for them, and re-layouts  4.75 us (4%)
  between operations  1.53 us (1%)
    ppermute x4, starting transfers between devices, far_step(): return lax.ppermute(v, 'z_hi', [(i, (i + by) % FAR) for i in range(FAR)])  33.7 us
    all_to_all x1, blocking collectives, shards(): lax.all_to_all(parts, NEARS, split_axis=0, concat_axis=0, tiled=True)  24.5 us
    all_to_all x1, starting transfers between devices, shards(): cut = lax.all_to_all(cut, 'z_lo', split_axis=0, concat_axis=0, tiled=True)  7.26 us
    ppermute x1, starting transfers between devices, shards(): other = lax.ppermute(mine, 'y_hi', [(0, 1), (1, 0)])  6.82 us
    ppermute x2, starting transfers between devices, neighbours(): lax.ppermute(field, 'layer', [(i + 1, i) for i in range(LAYERS - 1)])  6.15 us
    ppermute x2, starting transfers between devices, neighbours(): lax.ppermute(field, RING, [(i, (i - 1) % ring) for i in range(ring)])  5.89 us
    ppermute x2, starting transfers between devices, neighbours(): lax.ppermute(field, 'layer', [(i, i + 1) for i in range(LAYERS - 1)])  5.51 us
    unnamed x8, local copies, waits for them, and re-layouts  4.74 us
  transfers between devices with their start and end apart: 15, of which 6 were waited for; matrix products, arithmetic and copies ran while one was open for 0% of the time, Pallas kernels for 2%

profile of v5, /device:TPU:8, one launch (start us, length us, event | category | flops | bytes accessed | tf_op | source)
XLA Modules:
  0.0 115.0 jit_solution(1909514713360222204)
XLA Ops:
  0.0 0.0 copy-start.1
  0.0 0.9 copy-done.1
  0.9 0.0 copy-start.2
  0.9 0.9 copy-done.2
  1.8 0.0 copy-start.3
  1.8 0.7 copy-done.3
  2.4 1.3 %shard_map.64 = (f32[4,40,128]{2,1,0:T(8,128)}, f32[4,32,128]{2,1,0:T(8,128)S(1)}, f32[160,128]{1,0:T(8,128)S(1)}) custom-call(f32[5,4,1024]{2,1,0:T(4,128)S(1)} %bitcast.4, f32[32,1024]{1,0:T(8,128)S(1)} %copy-done.1, s32[4]{0:T(128)S(1)} %copy-done.3), custom_call_target="tpu_custom_call" | custom-call | bytes 327680 | tf_op jit(solution)/shard_map/pallas_call | solution.py:233
  3.7 7.3 %all-to-all-start = ((f32[4,40,128]{2,1,0:T(8,128)}), f32[4,40,128]{2,1,0:T(8,128)S(1)}, u32[]{:S(2)}, u32[]{:S(2)}) async-start(f32[4,40,128]{2,1,0:T(8,128)} %get-tuple-element.16), calls=%async_computation | async-start | bytes 163840 | tf_op jit(solution)/shard_map/all_to_all | solution.py:235
  11.0 6.8 %collective-permute-start = (f32[4,32,128]{2,1,0:T(8,128)S(1)}, f32[4,32,128]{2,1,0:T(8,128)S(1)}, u32[]{:S(2)}, u32[]{:S(2)}) collective-permute-start(f32[4,32,128]{2,1,0:T(8,128)S(1)} %get-tuple-element.17.mine_ref), channel_id=1, source_target_pairs={{0,1},{1,0},{2,3},{3,2},{4,5},{5,4},{6,7},{7,6},{8,9},{9,8},{10,11... | collective-permute-start | bytes 196616 | tf_op jit(solution)/shard_map/ppermute | solution.py:234
  17.8 3.3 %collective-permute-done.other_ref = f32[4,32,128]{2,1,0:T(8,128)S(1)} collective-permute-done((f32[4,32,128]{2,1,0:T(8,128)S(1)}, f32[4,32,128]{2,1,0:T(8,128)S(1)}, u32[]{:S(2)}, u32[]{:S(2)}) %collective-permute-start) | collective-permute-done | bytes 65568 | tf_op jit(solution)/shard_map/ppermute | solution.py:234
  21.1 0.0 all-to-all-done.rows_ref
  21.2 0.1 shard_map.65
  21.3 10.9 %collective-permute-start.1 = (f32[256,128]{1,0:T(8,128)S(1)}, f32[256,128]{1,0:T(8,128)S(1)}, u32[]{:S(2)}, u32[]{:S(2)}) collective-permute-start(f32[256,128]{1,0:T(8,128)S(1)} %get-tuple-element.18.up_ref), channel_id=1, source_target_pairs={{0,8},{8,16},{16,24},{24,0},{1,9},{9,17},{17,25},{25,1},{2,10},{10... | collective-permute-start | bytes 393224 | tf_op jit(solution)/shard_map/ppermute | solution.py:222
  32.2 6.5 %collective-permute-start.2 = (f32[256,128]{1,0:T(8,128)S(1)}, f32[256,128]{1,0:T(8,128)S(1)}, u32[]{:S(2)}, u32[]{:S(2)}) collective-permute-start(f32[256,128]{1,0:T(8,128)S(1)} %get-tuple-element.19.down_ref), channel_id=1, source_target_pairs={{0,24},{8,0},{16,8},{24,16},{1,25},{9,1},{17,9},{25,17},{2,26},{10... | collective-permute-start | bytes 393224 | tf_op jit(solution)/shard_map/ppermute | solution.py:222
  38.7 1.3 %collective-permute-done.1.below_ref = f32[256,128]{1,0:T(8,128)S(1)} collective-permute-done((f32[256,128]{1,0:T(8,128)S(1)}, f32[256,128]{1,0:T(8,128)S(1)}, u32[]{:S(2)}, u32[]{:S(2)}) %collective-permute-start.1) | collective-permute-done | bytes 131104 | tf_op jit(solution)/shard_map/ppermute | solution.py:222
  40.0 10.1 %collective-permute-start.3 = (f32[112,128]{1,0:T(8,128)S(1)}, f32[112,128]{1,0:T(8,128)S(1)}, u32[]{:S(2)}, u32[]{:S(2)}) collective-permute-start(f32[112,128]{1,0:T(8,128)S(1)} %slice.8), channel_id=1, source_target_pairs={{0,8},{8,16},{16,24},{24,0},{1,9},{9,17},{17,25},{25,1},{2,10},{10... | collective-permute-start | bytes 172040 | tf_op jit(solution)/shard_map/ppermute | solution.py:222
  50.0 0.0 collective-permute-done.2.above_ref
  50.0 6.2 %collective-permute-start.4 = (f32[112,128]{1,0:T(8,128)S(1)}, f32[112,128]{1,0:T(8,128)S(1)}, u32[]{:S(2)}, u32[]{:S(2)}) collective-permute-start(f32[112,128]{1,0:T(8,128)S(1)} %slice.9), channel_id=1, source_target_pairs={{0,24},{8,0},{16,8},{24,16},{1,25},{9,1},{17,9},{25,17},{2,26},{10... | collective-permute-start | bytes 172040 | tf_op jit(solution)/shard_map/ppermute | solution.py:222
  56.3 0.0 copy-start
  56.3 2.3 %copy-done = f32[4,7,160,160]{3,2,1,0:T(8,128)S(1)} copy-done((f32[4,7,160,160]{3,2,1,0:T(8,128)S(1)}, f32[4,7,160,160]{3,2,1,0:T(8,128)}, u32[]{:S(2)}) %copy-start) | copy-done | bytes 2867224
  58.6 0.6 shard_map.66
  59.2 0.0 collective-permute-done.3.passed_up_ref
  59.2 1.5 %collective-permute-done.4.passed_down_ref = f32[112,128]{1,0:T(8,128)S(1)} collective-permute-done((f32[112,128]{1,0:T(8,128)S(1)}, f32[112,128]{1,0:T(8,128)S(1)}, u32[]{:S(2)}, u32[]{:S(2)}) %collective-permute-start.4) | collective-permute-done | bytes 57376 | tf_op jit(solution)/shard_map/ppermute | solution.py:222
  60.7 1.9 %collective-permute-start.5 = (f32[256,128]{1,0:T(8,128)S(1)}, f32[256,128]{1,0:T(8,128)S(1)}, u32[]{:S(2)}, u32[]{:S(2)}) collective-permute-start(f32[256,128]{1,0:T(8,128)S(1)} %shard_map.67.mine_ref), channel_id=1, source_target_pairs={{0,32},{32,0},{1,33},{33,1},{2,34},{34,2},{3,35},{35,3},{4,36},{36... | collective-permute-start | bytes 393224 | tf_op jit(solution)/shard_map/ppermute | solution.py:243
  62.6 1.3 %collective-permute-done.5.other_ref = f32[256,128]{1,0:T(8,128)S(1)} collective-permute-done((f32[256,128]{1,0:T(8,128)S(1)}, f32[256,128]{1,0:T(8,128)S(1)}, u32[]{:S(2)}, u32[]{:S(2)}) %collective-permute-start.5) | collective-permute-done | bytes 131104 | tf_op jit(solution)/shard_map/ppermute | solution.py:243
  64.0 0.6 shard_map.68
  64.5 24.5 %all_to_all.10.parts_ref = f32[8,80,128]{2,1,0:T(8,128)S(1)} all-to-all(f32[8,80,128]{2,1,0:T(8,128)S(1)} %shard_map.68), channel_id=1, replica_groups=mesh['layer'=4,'column'=4,'core'=2,'z_hi'=4,'z_lo'=4,'y_hi'=2] {'z_lo','..., dimensions={0} | all-to-all | bytes 655360 | tf_op jit(solution)/shard_map/all_to_all | solution.py:248
  89.0 0.1 shard_map.69.field_ref.start_ref
  89.1 0.0 collective-permute-start.6
  89.1 2.9 %collective-permute-start.7 = (f32[160,128]{1,0:T(8,128)S(1)}, f32[160,128]{1,0:T(8,128)S(1)}, u32[]{:S(2)}, u32[]{:S(2)}) collective-permute-start(f32[160,128]{1,0:T(8,128)S(1)} %shard_map.69.field_ref.start_ref), channel_id=1, source_target_pairs={{0,224},{32,0},{64,32},{96,64},{128,96},{160,128},{192,160},{224,1... | collective-permute-start | bytes 245768 | tf_op jit(solution)/shard_map/ppermute | solution.py:215
  92.0 2.0 %collective-permute-start.8 = (f32[160,128]{1,0:T(8,128)S(1)}, f32[160,128]{1,0:T(8,128)S(1)}, u32[]{:S(2)}, u32[]{:S(2)}) collective-permute-start(f32[160,128]{1,0:T(8,128)S(1)} %shard_map.69.field_ref.start_ref), channel_id=1, source_target_pairs={{0,256},{256,512},{512,768},{1,257},{257,513},{513,769},{2,258},{2... | collective-permute-start | bytes 245768 | tf_op jit(solution)/shard_map/ppermute | solution.py:216
  94.1 3.8 %collective-permute-start.9 = (f32[160,128]{1,0:T(8,128)S(1)}, f32[160,128]{1,0:T(8,128)S(1)}, u32[]{:S(2)}, u32[]{:S(2)}) collective-permute-start(f32[160,128]{1,0:T(8,128)S(1)} %shard_map.69.field_ref.start_ref), channel_id=1, source_target_pairs={{256,0},{512,256},{768,512},{257,1},{513,257},{769,513},{258,2},{5... | collective-permute-start | bytes 245768 | tf_op jit(solution)/shard_map/ppermute | solution.py:217
  99.2 0.0 collective-permute-done.6.a_ref
  99.2 0.0 collective-permute-done.7.b_ref
  99.2 1.1 shard_map.70.own_ref
  100.3 0.0 collective-permute-done.8.c_ref
  100.3 0.1 collective-permute-done.9.d_ref
  100.4 0.5 shard_map.71.field_ref.middle_ref
  100.9 0.0 collective-permute-start.10
  101.0 2.9 %collective-permute-start.11 = (f32[160,128]{1,0:T(8,128)S(1)}, f32[160,128]{1,0:T(8,128)S(1)}, u32[]{:S(2)}, u32[]{:S(2)}) collective-permute-start(f32[160,128]{1,0:T(8,128)S(1)} %shard_map.71.field_ref.middle_ref), channel_id=1, source_target_pairs={{0,224},{32,0},{64,32},{96,64},{128,96},{160,128},{192,160},{224,1... | collective-permute-start | bytes 245768 | tf_op jit(solution)/shard_map/ppermute | solution.py:215
  103.9 3.5 %collective-permute-start.12 = (f32[160,128]{1,0:T(8,128)S(1)}, f32[160,128]{1,0:T(8,128)S(1)}, u32[]{:S(2)}, u32[]{:S(2)}) collective-permute-start(f32[160,128]{1,0:T(8,128)S(1)} %shard_map.71.field_ref.middle_ref), channel_id=1, source_target_pairs={{0,256},{256,512},{512,768},{1,257},{257,513},{513,769},{2,258},{2... | collective-permute-start | bytes 245768 | tf_op jit(solution)/shard_map/ppermute | solution.py:216
  107.4 2.4 %collective-permute-start.13 = (f32[160,128]{1,0:T(8,128)S(1)}, f32[160,128]{1,0:T(8,128)S(1)}, u32[]{:S(2)}, u32[]{:S(2)}) collective-permute-start(f32[160,128]{1,0:T(8,128)S(1)} %shard_map.71.field_ref.middle_ref), channel_id=1, source_target_pairs={{256,0},{512,256},{768,512},{257,1},{513,257},{769,513},{258,2},{5... | collective-permute-start | bytes 245768 | tf_op jit(solution)/shard_map/ppermute | solution.py:217
  109.8 0.0 collective-permute-done.10.a_ref
  109.8 0.0 collective-permute-done.11.b_ref
  109.8 1.1 shard_map.72.own_ref
  110.9 0.0 collective-permute-done.12.c_ref
  110.9 2.8 %collective-permute-done.13.d_ref = f32[160,128]{1,0:T(8,128)S(1)} collective-permute-done((f32[160,128]{1,0:T(8,128)S(1)}, f32[160,128]{1,0:T(8,128)S(1)}, u32[]{:S(2)}, u32[]{:S(2)}) %collective-permute-start.13) | collective-permute-done | bytes 81952 | tf_op jit(solution)/shard_map/ppermute | solution.py:217
  113.7 1.3 %shard_map.73 = f32[128,160]{1,0:T(8,128)} custom-call(f32[160,128]{1,0:T(8,128)S(1)} %shard_map.72.own_ref, f32[160,128]{1,0:T(8,128)S(1)} %collective-permute-done.12.c_ref, f32[160,128]{1,0:T(8,128)S(1)} %collective-permute-done.13.d_ref, bf16[4,7,160,160]{3,2,1,0:T(8,128)(2,1)S(1)} %get-tuple-element.25.high_ref, ...), custom_call_target="tpu_custom_call" | custom-call | flops 157286400 | bytes 1529173 | tf_op jit(solution)/shard_map/pallas_call | solution.py:260
  (3 shorter events, 0.0 us)
Async XLA Ops:
  0.0 0.9 copy-start.1
  0.9 0.9 copy-start.2
  1.8 0.7 copy-start.3
  3.7 17.4 %all-to-all-start = ((f32[4,40,128]{2,1,0:T(8,128)}), f32[4,40,128]{2,1,0:T(8,128)S(1)}, u32[]{:S(2)}, u32[]{:S(2)}) async-start(f32[4,40,128]{2,1,0:T(8,128)} %get-tuple-element.16), calls=%async_computation | async-start | bytes 163840 | tf_op jit(solution)/shard_map/all_to_all | solution.py:235
  11.0 10.2 %collective-permute-start = (f32[4,32,128]{2,1,0:T(8,128)S(1)}, f32[4,32,128]{2,1,0:T(8,128)S(1)}, u32[]{:S(2)}, u32[]{:S(2)}) collective-permute-start(f32[4,32,128]{2,1,0:T(8,128)S(1)} %get-tuple-element.17.mine_ref), channel_id=1, source_target_pairs={{0,1},{1,0},{2,3},{3,2},{4,5},{5,4},{6,7},{7,6},{8,9},{9,8},{10,11... | collective-permute-start | bytes 196616 | tf_op jit(solution)/shard_map/ppermute | solution.py:234
  21.3 18.7 %collective-permute-start.1 = (f32[256,128]{1,0:T(8,128)S(1)}, f32[256,128]{1,0:T(8,128)S(1)}, u32[]{:S(2)}, u32[]{:S(2)}) collective-permute-start(f32[256,128]{1,0:T(8,128)S(1)} %get-tuple-element.18.up_ref), channel_id=1, source_target_pairs={{0,8},{8,16},{16,24},{24,0},{1,9},{9,17},{17,25},{25,1},{2,10},{10... | collective-permute-start | bytes 393224 | tf_op jit(solution)/shard_map/ppermute | solution.py:222
  32.2 17.8 %collective-permute-start.2 = (f32[256,128]{1,0:T(8,128)S(1)}, f32[256,128]{1,0:T(8,128)S(1)}, u32[]{:S(2)}, u32[]{:S(2)}) collective-permute-start(f32[256,128]{1,0:T(8,128)S(1)} %get-tuple-element.19.down_ref), channel_id=1, source_target_pairs={{0,24},{8,0},{16,8},{24,16},{1,25},{9,1},{17,9},{25,17},{2,26},{10... | collective-permute-start | bytes 393224 | tf_op jit(solution)/shard_map/ppermute | solution.py:222
  40.0 19.3 %collective-permute-start.3 = (f32[112,128]{1,0:T(8,128)S(1)}, f32[112,128]{1,0:T(8,128)S(1)}, u32[]{:S(2)}, u32[]{:S(2)}) collective-permute-start(f32[112,128]{1,0:T(8,128)S(1)} %slice.8), channel_id=1, source_target_pairs={{0,8},{8,16},{16,24},{24,0},{1,9},{9,17},{17,25},{25,1},{2,10},{10... | collective-permute-start | bytes 172040 | tf_op jit(solution)/shard_map/ppermute | solution.py:222
  50.0 10.6 %collective-permute-start.4 = (f32[112,128]{1,0:T(8,128)S(1)}, f32[112,128]{1,0:T(8,128)S(1)}, u32[]{:S(2)}, u32[]{:S(2)}) collective-permute-start(f32[112,128]{1,0:T(8,128)S(1)} %slice.9), channel_id=1, source_target_pairs={{0,24},{8,0},{16,8},{24,16},{1,25},{9,1},{17,9},{25,17},{2,26},{10... | collective-permute-start | bytes 172040 | tf_op jit(solution)/shard_map/ppermute | solution.py:222
  56.3 2.3 %copy-start = (f32[4,7,160,160]{3,2,1,0:T(8,128)S(1)}, f32[4,7,160,160]{3,2,1,0:T(8,128)}, u32[]{:S(2)}) copy-start(f32[4,7,160,160]{3,2,1,0:T(8,128)} %hamiltonian_ref.1) | copy-start | bytes 8601604
  60.7 3.2 %collective-permute-start.5 = (f32[256,128]{1,0:T(8,128)S(1)}, f32[256,128]{1,0:T(8,128)S(1)}, u32[]{:S(2)}, u32[]{:S(2)}) collective-permute-start(f32[256,128]{1,0:T(8,128)S(1)} %shard_map.67.mine_ref), channel_id=1, source_target_pairs={{0,32},{32,0},{1,33},{33,1},{2,34},{34,2},{3,35},{35,3},{4,36},{36... | collective-permute-start | bytes 393224 | tf_op jit(solution)/shard_map/ppermute | solution.py:243
  89.1 10.1 %collective-permute-start.6 = (f32[160,128]{1,0:T(8,128)S(1)}, f32[160,128]{1,0:T(8,128)S(1)}, u32[]{:S(2)}, u32[]{:S(2)}) collective-permute-start(f32[160,128]{1,0:T(8,128)S(1)} %shard_map.69.field_ref.start_ref), channel_id=1, source_target_pairs={{0,32},{32,64},{64,96},{96,128},{128,160},{160,192},{192,224},{224... | collective-permute-start | bytes 245768 | tf_op jit(solution)/shard_map/ppermute | solution.py:214
  89.1 10.1 %collective-permute-start.7 = (f32[160,128]{1,0:T(8,128)S(1)}, f32[160,128]{1,0:T(8,128)S(1)}, u32[]{:S(2)}, u32[]{:S(2)}) collective-permute-start(f32[160,128]{1,0:T(8,128)S(1)} %shard_map.69.field_ref.start_ref), channel_id=1, source_target_pairs={{0,224},{32,0},{64,32},{96,64},{128,96},{160,128},{192,160},{224,1... | collective-permute-start | bytes 245768 | tf_op jit(solution)/shard_map/ppermute | solution.py:215
  92.0 8.2 %collective-permute-start.8 = (f32[160,128]{1,0:T(8,128)S(1)}, f32[160,128]{1,0:T(8,128)S(1)}, u32[]{:S(2)}, u32[]{:S(2)}) collective-permute-start(f32[160,128]{1,0:T(8,128)S(1)} %shard_map.69.field_ref.start_ref), channel_id=1, source_target_pairs={{0,256},{256,512},{512,768},{1,257},{257,513},{513,769},{2,258},{2... | collective-permute-start | bytes 245768 | tf_op jit(solution)/shard_map/ppermute | solution.py:216
  94.1 6.3 %collective-permute-start.9 = (f32[160,128]{1,0:T(8,128)S(1)}, f32[160,128]{1,0:T(8,128)S(1)}, u32[]{:S(2)}, u32[]{:S(2)}) collective-permute-start(f32[160,128]{1,0:T(8,128)S(1)} %shard_map.69.field_ref.start_ref), channel_id=1, source_target_pairs={{256,0},{512,256},{768,512},{257,1},{513,257},{769,513},{258,2},{5... | collective-permute-start | bytes 245768 | tf_op jit(solution)/shard_map/ppermute | solution.py:217
  100.9 8.8 %collective-permute-start.10 = (f32[160,128]{1,0:T(8,128)S(1)}, f32[160,128]{1,0:T(8,128)S(1)}, u32[]{:S(2)}, u32[]{:S(2)}) collective-permute-start(f32[160,128]{1,0:T(8,128)S(1)} %shard_map.71.field_ref.middle_ref), channel_id=1, source_target_pairs={{0,32},{32,64},{64,96},{96,128},{128,160},{160,192},{192,224},{224... | collective-permute-start | bytes 245768 | tf_op jit(solution)/shard_map/ppermute | solution.py:214
  101.0 8.8 %collective-permute-start.11 = (f32[160,128]{1,0:T(8,128)S(1)}, f32[160,128]{1,0:T(8,128)S(1)}, u32[]{:S(2)}, u32[]{:S(2)}) collective-permute-start(f32[160,128]{1,0:T(8,128)S(1)} %shard_map.71.field_ref.middle_ref), channel_id=1, source_target_pairs={{0,224},{32,0},{64,32},{96,64},{128,96},{160,128},{192,160},{224,1... | collective-permute-start | bytes 245768 | tf_op jit(solution)/shard_map/ppermute | solution.py:215
  103.9 7.0 %collective-permute-start.12 = (f32[160,128]{1,0:T(8,128)S(1)}, f32[160,128]{1,0:T(8,128)S(1)}, u32[]{:S(2)}, u32[]{:S(2)}) collective-permute-start(f32[160,128]{1,0:T(8,128)S(1)} %shard_map.71.field_ref.middle_ref), channel_id=1, source_target_pairs={{0,256},{256,512},{512,768},{1,257},{257,513},{513,769},{2,258},{2... | collective-permute-start | bytes 245768 | tf_op jit(solution)/shard_map/ppermute | solution.py:216
  107.4 6.3 %collective-permute-start.13 = (f32[160,128]{1,0:T(8,128)S(1)}, f32[160,128]{1,0:T(8,128)S(1)}, u32[]{:S(2)}, u32[]{:S(2)}) collective-permute-start(f32[160,128]{1,0:T(8,128)S(1)} %shard_map.71.field_ref.middle_ref), channel_id=1, source_target_pairs={{256,0},{512,256},{768,512},{257,1},{513,257},{769,513},{258,2},{5... | collective-permute-start | bytes 245768 | tf_op jit(solution)/shard_map/ppermute | solution.py:217

commit v6 on v5

--- a/solution.py
+++ b/solution.py
@@ -71,11 +71,13 @@
     return row < limit
 
 
-def cut_columns(orbitals_ref, rotation_ref, counts_ref, out_ref, mine_ref, live_ref):
+def cut_rotation(rotation_ref, mine_ref):
     for far in range(FAR):
         lanes = pl.ds(pl.multiple_of(256 * far + 128 * lax.axis_index("core"), 128), 128)
         mine_ref[far] = rotation_ref[:, lanes]
-    live_ref[...] = jnp.where(alive(counts_ref), 1.0, 0.0)
+
+
+def cut_columns(orbitals_ref, out_ref):
     first = lax.broadcasted_iota(jnp.int32, (ELEMS, WIDE), 1) < 64
     for i in range(PIECE):
         for low in range(LOW):
@@ -159,10 +161,11 @@
             for low in range(LOW):
                 rows_ref[pl.ds(10 * low + PIECE * share, PIECE), :] = sum_ref[share, pl.ds(20 * by + PIECE * low, PIECE), :]
         at = pl.ds(pl.multiple_of(40 * far_place(by), 8), 40)
-        out_ref[at, :] = jnp.where(live_ref[at, :] > 0.5, rows_ref[...], 0.0)
-
-
-def split_blocks(hamiltonian_ref, high_ref, low_ref):
+        out_ref[at, :] = jnp.where(live_ref[at, :].astype(F32) > 0.5, rows_ref[...], 0.0)
+
+
+def split_blocks(hamiltonian_ref, counts_ref, high_ref, low_ref, live_ref):
+    live_ref[...] = jnp.where(alive(counts_ref), 1.0, 0.0).astype(BF16)
     for e in range(ELEMS):
         for slot in range(7):
             high_ref[e, slot], low_ref[e, slot] = split(hamiltonian_ref[e, slot])
@@ -194,7 +197,7 @@
 
 def applied(own_ref, c_ref, d_ref, high_ref, low_ref, live_ref):
     total = own_ref[...] + blocks_times(high_ref, low_ref, (5, 6), (c_ref[...], d_ref[...]))
-    return jnp.where(live_ref[...] > 0.5, total, 0.0)
+    return jnp.where(live_ref[...].astype(F32) > 0.5, total, 0.0)
 
 
 def first_step(own_ref, c_ref, d_ref, high_ref, low_ref, start_ref, live_ref, center_ref, width_ref, out_ref):
@@ -229,16 +232,17 @@
 
 def shards(orbitals, rotation, counts, hamiltonian, center, width):
     pieces = jnp.transpose(orbitals, (1, 0, 2))
-    shapes = ((LOW, 2 * ELEMS * PIECE, WIDE), (FAR, 32, WIDE), (ROWS, WIDE))
-    cut, mine, live = call(cut_columns, shapes, 0, 4 * FIELD, (V, V, S))(pieces, rotation, counts)
+    mine = call(cut_rotation, (FAR, 32, WIDE), 0, 2 * FIELD, (V,))(rotation)
     other = lax.ppermute(mine, "y_hi", [(0, 1), (1, 0)])
+    cut = call(cut_columns, (LOW, 2 * ELEMS * PIECE, WIDE), 0, 2 * FIELD, (V,))(pieces)
     cut = lax.all_to_all(cut, "z_lo", split_axis=0, concat_axis=0, tiled=True)
     message = (2 * PASS + 32, WIDE)
     up, down, slices = call(pack, (message, message, (64, WIDE)), 0, 6 * FIELD, (V,) * 3)(cut, mine, other)
     above, below = far_step(down, -1), far_step(up, 1)
+    shapes = (hamiltonian.shape, hamiltonian.shape, (ROWS, WIDE))
+    blocks = call(split_blocks, shapes, 0, 2 * BLOCKS, (V, S), (), BF16)(hamiltonian, counts)
+    below, *blocks, live = lax.optimization_barrier((below, *blocks))
     passed_up, passed_down = far_step(below[:PASS], 1), far_step(above[:PASS], -1)
-    blocks = call(split_blocks, (hamiltonian.shape,) * 2, 0, 2 * BLOCKS, (V,), (), BF16)(hamiltonian)
-    slices, *blocks = lax.optimization_barrier((slices, *blocks))
     mine = call(collect, (256, WIDE), 0, 4 * FIELD, (V,) * 5)(slices, below, above, passed_up, passed_down)
     other = lax.ppermute(mine, "core", [(0, 1), (1, 0)])
     scratch = [V((2, HALF, WIDE), F32)]

time: 116 us -> 114 us (0.983)
  starting transfers between devices: 67.3 us -> 64.3 us
  waiting for transfers between devices: 10.4 us -> 12.1 us
    ppermute x4, starting transfers between devices: 33.7 us -> 30.8 us  [far_step(): return lax.ppermute(v, 'z_hi', [(i, (i + by) % FAR) for i in range(FAR)])]
    ppermute x4, waiting for transfers between devices: 2.72 us -> 4.5 us  [far_step(): return lax.ppermute(v, 'z_hi', [(i, (i + by) % FAR) for i in range(FAR)])]
  transfers between devices with their start and end apart: 15 -> 15, of which waited for: 6 -> 5; matrix products, arithmetic and copies ran while one was open for 0% -> 0% of each run, Pallas kernels for 2% -> 3%
where the time goes in v6:
time: 114 us; the launch traced here: 113 us
  starting transfers between devices  64.3 us (56%)
  blocking collectives  24.1 us (21%)
  waiting for transfers between devices  12.1 us (11%)
  Pallas kernels  6.62 us (6%)
  local copies, waits for them, and re-layouts  4.75 us (4%)
  between operations  1.55 us (1%)
    ppermute x4, starting transfers between devices, far_step(): return lax.ppermute(v, 'z_hi', [(i, (i + by) % FAR) for i in range(FAR)])  30.8 us
    all_to_all x1, blocking collectives, shards(): lax.all_to_all(parts, NEARS, split_axis=0, concat_axis=0, tiled=True)  24.1 us
    all_to_all x1, starting transfers between devices, shards(): cut = lax.all_to_all(cut, 'z_lo', split_axis=0, concat_axis=0, tiled=True)  7.26 us
    ppermute x1, starting transfers between devices, shards(): other = lax.ppermute(mine, 'y_hi', [(0, 1), (1, 0)])  6.83 us
    ppermute x2, starting transfers between devices, neighbours(): lax.ppermute(field, 'layer', [(i + 1, i) for i in range(LAYERS - 1)])  6.15 us
    ppermute x2, starting transfers between devices, neighbours(): lax.ppermute(field, RING, [(i, (i - 1) % ring) for i in range(ring)])  5.89 us
    ppermute x2, starting transfers between devices, neighbours(): lax.ppermute(field, 'layer', [(i, i + 1) for i in range(LAYERS - 1)])  5.51 us
    unnamed x8, local copies, waits for them, and re-layouts  4.74 us
  transfers between devices with their start and end apart: 15, of which 5 were waited for; matrix products, arithmetic and copies ran while one was open for 0% of the time, Pallas kernels for 3%

profile of v6, /device:TPU:8, one launch (start us, length us, event | category | flops | bytes accessed | tf_op | source)
XLA Modules:
  0.0 113.4 jit_solution(8783549816063358418)
XLA Ops:
  0.0 0.0 copy-start.2
  0.0 0.9 copy-done.2
  0.9 0.7 shard_map.64
  1.6 7.3 %all-to-all-start = ((f32[4,40,128]{2,1,0:T(8,128)}), f32[4,40,128]{2,1,0:T(8,128)S(1)}, u32[]{:S(2)}, u32[]{:S(2)}) async-start(f32[4,40,128]{2,1,0:T(8,128)} %shard_map.64), calls=%async_computation | async-start | bytes 163840 | tf_op jit(solution)/shard_map/all_to_all | solution.py:238
  8.9 0.0 copy-start.1
  8.9 0.9 copy-done.1
  9.8 6.8 %collective-permute-start = (f32[4,32,128]{2,1,0:T(8,128)S(1)}, f32[4,32,128]{2,1,0:T(8,128)S(1)}, u32[]{:S(2)}, u32[]{:S(2)}) collective-permute-start(f32[4,32,128]{2,1,0:T(8,128)S(1)} %shard_map.65.mine_ref), channel_id=1, source_target_pairs={{0,1},{1,0},{2,3},{3,2},{4,5},{5,4},{6,7},{7,6},{8,9},{9,8},{10,11... | collective-permute-start | bytes 196616 | tf_op jit(solution)/shard_map/ppermute | solution.py:236
  16.6 3.3 %collective-permute-done.other_ref = f32[4,32,128]{2,1,0:T(8,128)S(1)} collective-permute-done((f32[4,32,128]{2,1,0:T(8,128)S(1)}, f32[4,32,128]{2,1,0:T(8,128)S(1)}, u32[]{:S(2)}, u32[]{:S(2)}) %collective-permute-start) | collective-permute-done | bytes 65568 | tf_op jit(solution)/shard_map/ppermute | solution.py:236
  20.0 0.0 all-to-all-done.rows_ref
  20.0 0.1 shard_map.66
  20.1 10.9 %collective-permute-start.1 = (f32[256,128]{1,0:T(8,128)S(1)}, f32[256,128]{1,0:T(8,128)S(1)}, u32[]{:S(2)}, u32[]{:S(2)}) collective-permute-start(f32[256,128]{1,0:T(8,128)S(1)} %get-tuple-element.15.up_ref), channel_id=1, source_target_pairs={{0,8},{8,16},{16,24},{24,0},{1,9},{9,17},{17,25},{25,1},{2,10},{10... | collective-permute-start | bytes 393224 | tf_op jit(solution)/shard_map/ppermute | solution.py:225
  31.0 6.5 %collective-permute-start.2 = (f32[256,128]{1,0:T(8,128)S(1)}, f32[256,128]{1,0:T(8,128)S(1)}, u32[]{:S(2)}, u32[]{:S(2)}) collective-permute-start(f32[256,128]{1,0:T(8,128)S(1)} %get-tuple-element.16.down_ref), channel_id=1, source_target_pairs={{0,24},{8,0},{16,8},{24,16},{1,25},{9,1},{17,9},{25,17},{2,26},{10... | collective-permute-start | bytes 393224 | tf_op jit(solution)/shard_map/ppermute | solution.py:225
  37.5 0.0 copy-start
  37.5 2.3 %copy-done = f32[4,7,160,160]{3,2,1,0:T(8,128)S(1)} copy-done((f32[4,7,160,160]{3,2,1,0:T(8,128)S(1)}, f32[4,7,160,160]{3,2,1,0:T(8,128)}, u32[]{:S(2)}) %copy-start) | copy-done | bytes 2867224
  39.8 0.0 copy-start.3
  39.8 0.7 copy-done.3
  40.5 1.2 %shard_map.67 = (bf16[4,7,160,160]{3,2,1,0:T(8,128)(2,1)S(1)}, bf16[4,7,160,160]{3,2,1,0:T(8,128)(2,1)S(1)}, bf16[160,128]{1,0:T(8,128)(2,1)S(1)}) custom-call(f32[4,7,160,160]{3,2,1,0:T(8,128)S(1)} %copy-done, s32[4]{0:T(128)S(1)} %copy-done.3), custom_call_target="tpu_custom_call" | custom-call | bytes 9175040 | tf_op jit(solution)/shard_map/pallas_call | solution.py:243
  41.7 0.0 collective-permute-done.1.below_ref
  41.7 7.2 %collective-permute-start.3 = (f32[112,128]{1,0:T(8,128)S(1)}, f32[112,128]{1,0:T(8,128)S(1)}, u32[]{:S(2)}, u32[]{:S(2)}) collective-permute-start(f32[112,128]{1,0:T(8,128)S(1)} %slice.6), channel_id=1, source_target_pairs={{0,8},{8,16},{16,24},{24,0},{1,9},{9,17},{17,25},{25,1},{2,10},{10... | collective-permute-start | bytes 172040 | tf_op jit(solution)/shard_map/ppermute | solution.py:225
  48.9 0.0 collective-permute-done.2.above_ref
  48.9 6.2 %collective-permute-start.4 = (f32[112,128]{1,0:T(8,128)S(1)}, f32[112,128]{1,0:T(8,128)S(1)}, u32[]{:S(2)}, u32[]{:S(2)}) collective-permute-start(f32[112,128]{1,0:T(8,128)S(1)} %slice.8), channel_id=1, source_target_pairs={{0,24},{8,0},{16,8},{24,16},{1,25},{9,1},{17,9},{25,17},{2,26},{10... | collective-permute-start | bytes 172040 | tf_op jit(solution)/shard_map/ppermute | solution.py:225
  55.1 0.0 collective-permute-done.3.passed_up_ref
  55.1 4.5 %collective-permute-done.4.passed_down_ref = f32[112,128]{1,0:T(8,128)S(1)} collective-permute-done((f32[112,128]{1,0:T(8,128)S(1)}, f32[112,128]{1,0:T(8,128)S(1)}, u32[]{:S(2)}, u32[]{:S(2)}) %collective-permute-start.4) | collective-permute-done | bytes 57376 | tf_op jit(solution)/shard_map/ppermute | solution.py:225
  59.6 1.9 %collective-permute-start.5 = (f32[256,128]{1,0:T(8,128)S(1)}, f32[256,128]{1,0:T(8,128)S(1)}, u32[]{:S(2)}, u32[]{:S(2)}) collective-permute-start(f32[256,128]{1,0:T(8,128)S(1)} %shard_map.68.mine_ref), channel_id=1, source_target_pairs={{0,32},{32,0},{1,33},{33,1},{2,34},{34,2},{3,35},{35,3},{4,36},{36... | collective-permute-start | bytes 393224 | tf_op jit(solution)/shard_map/ppermute | solution.py:247
  61.5 1.3 %collective-permute-done.5.other_ref = f32[256,128]{1,0:T(8,128)S(1)} collective-permute-done((f32[256,128]{1,0:T(8,128)S(1)}, f32[256,128]{1,0:T(8,128)S(1)}, u32[]{:S(2)}, u32[]{:S(2)}) %collective-permute-start.5) | collective-permute-done | bytes 131104 | tf_op jit(solution)/shard_map/ppermute | solution.py:247
  62.8 0.6 shard_map.69
  63.4 24.1 %all_to_all.10.parts_ref = f32[8,80,128]{2,1,0:T(8,128)S(1)} all-to-all(f32[8,80,128]{2,1,0:T(8,128)S(1)} %shard_map.69), channel_id=1, replica_groups=mesh['layer'=4,'column'=4,'core'=2,'z_hi'=4,'z_lo'=4,'y_hi'=2] {'z_lo','..., dimensions={0} | all-to-all | bytes 655360 | tf_op jit(solution)/shard_map/all_to_all | solution.py:252
  87.5 0.1 shard_map.70.field_ref.start_ref
  87.5 0.0 collective-permute-start.6
  87.6 2.9 %collective-permute-start.7 = (f32[160,128]{1,0:T(8,128)S(1)}, f32[160,128]{1,0:T(8,128)S(1)}, u32[]{:S(2)}, u32[]{:S(2)}) collective-permute-start(f32[160,128]{1,0:T(8,128)S(1)} %shard_map.70.field_ref.start_ref), channel_id=1, source_target_pairs={{0,224},{32,0},{64,32},{96,64},{128,96},{160,128},{192,160},{224,1... | collective-permute-start | bytes 245768 | tf_op jit(solution)/shard_map/ppermute | solution.py:218
  90.5 2.2 %collective-permute-start.8 = (f32[160,128]{1,0:T(8,128)S(1)}, f32[160,128]{1,0:T(8,128)S(1)}, u32[]{:S(2)}, u32[]{:S(2)}) collective-permute-start(f32[160,128]{1,0:T(8,128)S(1)} %shard_map.70.field_ref.start_ref), channel_id=1, source_target_pairs={{0,256},{256,512},{512,768},{1,257},{257,513},{513,769},{2,258},{2... | collective-permute-start | bytes 245768 | tf_op jit(solution)/shard_map/ppermute | solution.py:219
  92.7 3.6 %collective-permute-start.9 = (f32[160,128]{1,0:T(8,128)S(1)}, f32[160,128]{1,0:T(8,128)S(1)}, u32[]{:S(2)}, u32[]{:S(2)}) collective-permute-start(f32[160,128]{1,0:T(8,128)S(1)} %shard_map.70.field_ref.start_ref), channel_id=1, source_target_pairs={{256,0},{512,256},{768,512},{257,1},{513,257},{769,513},{258,2},{5... | collective-permute-start | bytes 245768 | tf_op jit(solution)/shard_map/ppermute | solution.py:220
  97.6 0.0 collective-permute-done.6.a_ref
  97.7 0.0 collective-permute-done.7.b_ref
  97.7 1.1 shard_map.71.own_ref
  98.8 0.0 collective-permute-done.8.c_ref
  98.8 0.3 collective-permute-done.9.d_ref
  99.1 0.5 shard_map.72.field_ref.middle_ref
  99.6 0.0 collective-permute-start.10
  99.6 2.9 %collective-permute-start.11 = (f32[160,128]{1,0:T(8,128)S(1)}, f32[160,128]{1,0:T(8,128)S(1)}, u32[]{:S(2)}, u32[]{:S(2)}) collective-permute-start(f32[160,128]{1,0:T(8,128)S(1)} %shard_map.72.field_ref.middle_ref), channel_id=1, source_target_pairs={{0,224},{32,0},{64,32},{96,64},{128,96},{160,128},{192,160},{224,1... | collective-permute-start | bytes 245768 | tf_op jit(solution)/shard_map/ppermute | solution.py:218
  102.5 3.3 %collective-permute-start.12 = (f32[160,128]{1,0:T(8,128)S(1)}, f32[160,128]{1,0:T(8,128)S(1)}, u32[]{:S(2)}, u32[]{:S(2)}) collective-permute-start(f32[160,128]{1,0:T(8,128)S(1)} %shard_map.72.field_ref.middle_ref), channel_id=1, source_target_pairs={{0,256},{256,512},{512,768},{1,257},{257,513},{513,769},{2,258},{2... | collective-permute-start | bytes 245768 | tf_op jit(solution)/shard_map/ppermute | solution.py:219
  105.8 2.5 %collective-permute-start.13 = (f32[160,128]{1,0:T(8,128)S(1)}, f32[160,128]{1,0:T(8,128)S(1)}, u32[]{:S(2)}, u32[]{:S(2)}) collective-permute-start(f32[160,128]{1,0:T(8,128)S(1)} %shard_map.72.field_ref.middle_ref), channel_id=1, source_target_pairs={{256,0},{512,256},{768,512},{257,1},{513,257},{769,513},{258,2},{5... | collective-permute-start | bytes 245768 | tf_op jit(solution)/shard_map/ppermute | solution.py:220
  108.4 0.0 collective-permute-done.10.a_ref
  108.4 0.0 collective-permute-done.11.b_ref
  108.4 1.1 shard_map.73.own_ref
  109.5 0.0 collective-permute-done.12.c_ref
  109.5 2.6 %collective-permute-done.13.d_ref = f32[160,128]{1,0:T(8,128)S(1)} collective-permute-done((f32[160,128]{1,0:T(8,128)S(1)}, f32[160,128]{1,0:T(8,128)S(1)}, u32[]{:S(2)}, u32[]{:S(2)}) %collective-permute-start.13) | collective-permute-done | bytes 81952 | tf_op jit(solution)/shard_map/ppermute | solution.py:220
  112.2 1.3 %shard_map.74 = f32[128,160]{1,0:T(8,128)} custom-call(f32[160,128]{1,0:T(8,128)S(1)} %shard_map.73.own_ref, f32[160,128]{1,0:T(8,128)S(1)} %collective-permute-done.12.c_ref, f32[160,128]{1,0:T(8,128)S(1)} %collective-permute-done.13.d_ref, bf16[4,7,160,160]{3,2,1,0:T(8,128)(2,1)S(1)} %get-tuple-element.23.high_ref, ...), custom_call_target="tpu_custom_call" | custom-call | flops 157286400 | bytes 1529173 | tf_op jit(solution)/shard_map/pallas_call | solution.py:264
  (4 shorter events, 0.0 us)
Async XLA Ops:
  0.0 0.9 copy-start.2
  1.6 18.3 %all-to-all-start = ((f32[4,40,128]{2,1,0:T(8,128)}), f32[4,40,128]{2,1,0:T(8,128)S(1)}, u32[]{:S(2)}, u32[]{:S(2)}) async-start(f32[4,40,128]{2,1,0:T(8,128)} %shard_map.64), calls=%async_computation | async-start | bytes 163840 | tf_op jit(solution)/shard_map/all_to_all | solution.py:238
  8.9 0.9 copy-start.1
  9.8 10.2 %collective-permute-start = (f32[4,32,128]{2,1,0:T(8,128)S(1)}, f32[4,32,128]{2,1,0:T(8,128)S(1)}, u32[]{:S(2)}, u32[]{:S(2)}) collective-permute-start(f32[4,32,128]{2,1,0:T(8,128)S(1)} %shard_map.65.mine_ref), channel_id=1, source_target_pairs={{0,1},{1,0},{2,3},{3,2},{4,5},{5,4},{6,7},{7,6},{8,9},{9,8},{10,11... | collective-permute-start | bytes 196616 | tf_op jit(solution)/shard_map/ppermute | solution.py:236
  20.1 21.6 %collective-permute-start.1 = (f32[256,128]{1,0:T(8,128)S(1)}, f32[256,128]{1,0:T(8,128)S(1)}, u32[]{:S(2)}, u32[]{:S(2)}) collective-permute-start(f32[256,128]{1,0:T(8,128)S(1)} %get-tuple-element.15.up_ref), channel_id=1, source_target_pairs={{0,8},{8,16},{16,24},{24,0},{1,9},{9,17},{17,25},{25,1},{2,10},{10... | collective-permute-start | bytes 393224 | tf_op jit(solution)/shard_map/ppermute | solution.py:225
  31.0 17.8 %collective-permute-start.2 = (f32[256,128]{1,0:T(8,128)S(1)}, f32[256,128]{1,0:T(8,128)S(1)}, u32[]{:S(2)}, u32[]{:S(2)}) collective-permute-start(f32[256,128]{1,0:T(8,128)S(1)} %get-tuple-element.16.down_ref), channel_id=1, source_target_pairs={{0,24},{8,0},{16,8},{24,16},{1,25},{9,1},{17,9},{25,17},{2,26},{10... | collective-permute-start | bytes 393224 | tf_op jit(solution)/shard_map/ppermute | solution.py:225
  37.5 2.3 %copy-start = (f32[4,7,160,160]{3,2,1,0:T(8,128)S(1)}, f32[4,7,160,160]{3,2,1,0:T(8,128)}, u32[]{:S(2)}) copy-start(f32[4,7,160,160]{3,2,1,0:T(8,128)} %hamiltonian_ref.1) | copy-start | bytes 8601604
  39.8 0.7 copy-start.3
  41.7 13.4 %collective-permute-start.3 = (f32[112,128]{1,0:T(8,128)S(1)}, f32[112,128]{1,0:T(8,128)S(1)}, u32[]{:S(2)}, u32[]{:S(2)}) collective-permute-start(f32[112,128]{1,0:T(8,128)S(1)} %slice.6), channel_id=1, source_target_pairs={{0,8},{8,16},{16,24},{24,0},{1,9},{9,17},{17,25},{25,1},{2,10},{10... | collective-permute-start | bytes 172040 | tf_op jit(solution)/shard_map/ppermute | solution.py:225
  48.9 10.7 %collective-permute-start.4 = (f32[112,128]{1,0:T(8,128)S(1)}, f32[112,128]{1,0:T(8,128)S(1)}, u32[]{:S(2)}, u32[]{:S(2)}) collective-permute-start(f32[112,128]{1,0:T(8,128)S(1)} %slice.8), channel_id=1, source_target_pairs={{0,24},{8,0},{16,8},{24,16},{1,25},{9,1},{17,9},{25,17},{2,26},{10... | collective-permute-start | bytes 172040 | tf_op jit(solution)/shard_map/ppermute | solution.py:225
  59.6 3.2 %collective-permute-start.5 = (f32[256,128]{1,0:T(8,128)S(1)}, f32[256,128]{1,0:T(8,128)S(1)}, u32[]{:S(2)}, u32[]{:S(2)}) collective-permute-start(f32[256,128]{1,0:T(8,128)S(1)} %shard_map.68.mine_ref), channel_id=1, source_target_pairs={{0,32},{32,0},{1,33},{33,1},{2,34},{34,2},{3,35},{35,3},{4,36},{36... | collective-permute-start | bytes 393224 | tf_op jit(solution)/shard_map/ppermute | solution.py:247
  87.5 10.1 %collective-permute-start.6 = (f32[160,128]{1,0:T(8,128)S(1)}, f32[160,128]{1,0:T(8,128)S(1)}, u32[]{:S(2)}, u32[]{:S(2)}) collective-permute-start(f32[160,128]{1,0:T(8,128)S(1)} %shard_map.70.field_ref.start_ref), channel_id=1, source_target_pairs={{0,32},{32,64},{64,96},{96,128},{128,160},{160,192},{192,224},{224... | collective-permute-start | bytes 245768 | tf_op jit(solution)/shard_map/ppermute | solution.py:217
  87.6 10.1 %collective-permute-start.7 = (f32[160,128]{1,0:T(8,128)S(1)}, f32[160,128]{1,0:T(8,128)S(1)}, u32[]{:S(2)}, u32[]{:S(2)}) collective-permute-start(f32[160,128]{1,0:T(8,128)S(1)} %shard_map.70.field_ref.start_ref), channel_id=1, source_target_pairs={{0,224},{32,0},{64,32},{96,64},{128,96},{160,128},{192,160},{224,1... | collective-permute-start | bytes 245768 | tf_op jit(solution)/shard_map/ppermute | solution.py:218
  90.5 8.3 %collective-permute-start.8 = (f32[160,128]{1,0:T(8,128)S(1)}, f32[160,128]{1,0:T(8,128)S(1)}, u32[]{:S(2)}, u32[]{:S(2)}) collective-permute-start(f32[160,128]{1,0:T(8,128)S(1)} %shard_map.70.field_ref.start_ref), channel_id=1, source_target_pairs={{0,256},{256,512},{512,768},{1,257},{257,513},{513,769},{2,258},{2... | collective-permute-start | bytes 245768 | tf_op jit(solution)/shard_map/ppermute | solution.py:219
  92.7 6.3 %collective-permute-start.9 = (f32[160,128]{1,0:T(8,128)S(1)}, f32[160,128]{1,0:T(8,128)S(1)}, u32[]{:S(2)}, u32[]{:S(2)}) collective-permute-start(f32[160,128]{1,0:T(8,128)S(1)} %shard_map.70.field_ref.start_ref), channel_id=1, source_target_pairs={{256,0},{512,256},{768,512},{257,1},{513,257},{769,513},{258,2},{5... | collective-permute-start | bytes 245768 | tf_op jit(solution)/shard_map/ppermute | solution.py:220
  99.6 8.8 %collective-permute-start.10 = (f32[160,128]{1,0:T(8,128)S(1)}, f32[160,128]{1,0:T(8,128)S(1)}, u32[]{:S(2)}, u32[]{:S(2)}) collective-permute-start(f32[160,128]{1,0:T(8,128)S(1)} %shard_map.72.field_ref.middle_ref), channel_id=1, source_target_pairs={{0,32},{32,64},{64,96},{96,128},{128,160},{160,192},{192,224},{224... | collective-permute-start | bytes 245768 | tf_op jit(solution)/shard_map/ppermute | solution.py:217
  99.6 8.8 %collective-permute-start.11 = (f32[160,128]{1,0:T(8,128)S(1)}, f32[160,128]{1,0:T(8,128)S(1)}, u32[]{:S(2)}, u32[]{:S(2)}) collective-permute-start(f32[160,128]{1,0:T(8,128)S(1)} %shard_map.72.field_ref.middle_ref), channel_id=1, source_target_pairs={{0,224},{32,0},{64,32},{96,64},{128,96},{160,128},{192,160},{224,1... | collective-permute-start | bytes 245768 | tf_op jit(solution)/shard_map/ppermute | solution.py:218
  102.5 7.0 %collective-permute-start.12 = (f32[160,128]{1,0:T(8,128)S(1)}, f32[160,128]{1,0:T(8,128)S(1)}, u32[]{:S(2)}, u32[]{:S(2)}) collective-permute-start(f32[160,128]{1,0:T(8,128)S(1)} %shard_map.72.field_ref.middle_ref), channel_id=1, source_target_pairs={{0,256},{256,512},{512,768},{1,257},{257,513},{513,769},{2,258},{2... | collective-permute-start | bytes 245768 | tf_op jit(solution)/shard_map/ppermute | solution.py:219
  105.8 6.3 %collective-permute-start.13 = (f32[160,128]{1,0:T(8,128)S(1)}, f32[160,128]{1,0:T(8,128)S(1)}, u32[]{:S(2)}, u32[]{:S(2)}) collective-permute-start(f32[160,128]{1,0:T(8,128)S(1)} %shard_map.72.field_ref.middle_ref), channel_id=1, source_target_pairs={{256,0},{512,256},{768,512},{257,1},{513,257},{769,513},{258,2},{5... | collective-permute-start | bytes 245768 | tf_op jit(solution)/shard_map/ppermute | solution.py:220

commit v7 on v6

--- a/solution.py
+++ b/solution.py
@@ -96,7 +96,17 @@
 PASS = HALF + 32
 
 
-def pack(rows_ref, mine_ref, other_ref, up_ref, down_ref, own_ref):
+def by_parity(body, first, second, *relayed):
+    even = lax.rem(lax.axis_index("z_hi"), 2) == 0
+    pl.when(even)(lambda: body(first, second, *relayed))
+    pl.when(jnp.logical_not(even))(lambda: body(second, first, *reversed(relayed)))
+
+
+def pack(rows_ref, mine_ref, other_ref, first_ref, second_ref, own_ref):
+    by_parity(lambda up, down: pack_into(rows_ref, mine_ref, other_ref, up, down, own_ref), first_ref, second_ref)
+
+
+def pack_into(rows_ref, mine_ref, other_ref, up_ref, down_ref, own_ref):
     for k in range(2):
         first, second = (down_ref, up_ref) if k else (up_ref, down_ref)
         for e in range(ELEMS):
@@ -119,7 +129,14 @@
     own_ref[:32, :], own_ref[32:, :] = slices(0)
 
 
-def collect(own_ref, below_ref, above_ref, passed_up_ref, passed_down_ref, out_ref):
+def collect(own_ref, near_ref, next_ref, passed_ref, last_ref, out_ref):
+    def body(above, below, passed_up, passed_down):
+        collect_from(own_ref, below, above, passed_up, passed_down, out_ref)
+
+    by_parity(body, near_ref, next_ref, passed_ref, last_ref)
+
+
+def collect_from(own_ref, below_ref, above_ref, passed_up_ref, passed_down_ref, out_ref):
     tail = PASS + HALF
     passed = jnp.concatenate([passed_up_ref[HALF:, :], passed_down_ref[HALF:, :]], axis=0)
     for by, piece in ((0, own_ref[...]), (3, below_ref[tail:, :]), (1, above_ref[tail:, :]), (2, passed)):
@@ -127,6 +144,15 @@
 
 
 def rotate(
+    first_ref, second_ref, mine_ref, other_ref, near_ref, next_ref, passed_ref, last_ref, out_ref, sum_ref
+):
+    def body(up, down, above, passed_up, passed_down, below):
+        rotate_from(up, down, mine_ref, other_ref, below, above, passed_up, passed_down, out_ref, sum_ref)
+
+    by_parity(body, first_ref, second_ref, near_ref, passed_ref, last_ref, next_ref)
+
+
+def rotate_from(
     up_ref, down_ref, mine_ref, other_ref, below_ref, above_ref, passed_up_ref, passed_down_ref, out_ref, sum_ref
 ):
     tail = PASS + HALF
@@ -188,15 +214,15 @@
     return by_owner(totals)
 
 
-def own_and_ring(field_ref, a_ref, b_ref, high_ref, low_ref, out_ref):
+def own_and_layers(field_ref, a_ref, b_ref, high_ref, low_ref, out_ref):
     field = field_ref[...]
     out_ref[...] = blocks_times(
-        high_ref, low_ref, range(5), (field, turned(field, 1), turned(field, -1), a_ref[...], b_ref[...])
+        high_ref, low_ref, (0, 1, 2, 5, 6), (field, turned(field, 1), turned(field, -1), a_ref[...], b_ref[...])
     )
 
 
 def applied(own_ref, c_ref, d_ref, high_ref, low_ref, live_ref):
-    total = own_ref[...] + blocks_times(high_ref, low_ref, (5, 6), (c_ref[...], d_ref[...]))
+    total = own_ref[...] + blocks_times(high_ref, low_ref, (3, 4), (c_ref[...], d_ref[...]))
     return jnp.where(live_ref[...].astype(F32) > 0.5, total, 0.0)
 
 
@@ -221,8 +247,9 @@
     )
 
 
-def far_step(v, by):
-    return lax.ppermute(v, "z_hi", [(i, (i + by) % FAR) for i in range(FAR)])
+def swapped(v, start):
+    pairs = [(i % FAR, (i + 1) % FAR) for i in range(start, FAR, 2)]
+    return lax.ppermute(v, "z_hi", pairs + [(b, a) for a, b in pairs])
 
 
 V, S = pltpu.VMEM, pltpu.SMEM
@@ -237,29 +264,29 @@
     cut = call(cut_columns, (LOW, 2 * ELEMS * PIECE, WIDE), 0, 2 * FIELD, (V,))(pieces)
     cut = lax.all_to_all(cut, "z_lo", split_axis=0, concat_axis=0, tiled=True)
     message = (2 * PASS + 32, WIDE)
-    up, down, slices = call(pack, (message, message, (64, WIDE)), 0, 6 * FIELD, (V,) * 3)(cut, mine, other)
-    above, below = far_step(down, -1), far_step(up, 1)
+    first, second, slices = call(pack, (message, message, (64, WIDE)), 0, 6 * FIELD, (V,) * 3)(cut, mine, other)
+    near, after = swapped(first, 0), swapped(second, 1)
     shapes = (hamiltonian.shape, hamiltonian.shape, (ROWS, WIDE))
     blocks = call(split_blocks, shapes, 0, 2 * BLOCKS, (V, S), (), BF16)(hamiltonian, counts)
-    below, *blocks, live = lax.optimization_barrier((below, *blocks))
-    passed_up, passed_down = far_step(below[:PASS], 1), far_step(above[:PASS], -1)
-    mine = call(collect, (256, WIDE), 0, 4 * FIELD, (V,) * 5)(slices, below, above, passed_up, passed_down)
+    near, *blocks, live = lax.optimization_barrier((near, *blocks))
+    passed, last = swapped(near[:PASS], 1), swapped(after[:PASS], 0)
+    mine = call(collect, (256, WIDE), 0, 4 * FIELD, (V,) * 5)(slices, near, after, passed, last)
     other = lax.ppermute(mine, "core", [(0, 1), (1, 0)])
     scratch = [V((2, HALF, WIDE), F32)]
     parts = call(rotate, (NEAR, HALF, WIDE), 6 * 320 * 256 * 256, 11 * FIELD, (V,) * 8, scratch)(
-        up, down, mine, other, below, above, passed_up, passed_down
+        first, second, mine, other, near, after, passed, last
     )
     parts = lax.all_to_all(parts, NEARS, split_axis=0, concat_axis=0, tiled=True)
     scratch = [V((2, HALF, WIDE), F32), V((40, WIDE), F32)]
     start = call(add_up, (ROWS, WIDE), 0, 5 * FIELD, (V, V), scratch)(parts, live)
 
-    own = call(own_and_ring, (ROWS, WIDE), 6 * 20 * ROWS * ROWS * WIDE, BLOCKS, (V,) * 5)
+    own = call(own_and_layers, (ROWS, WIDE), 6 * 20 * ROWS * ROWS * WIDE, BLOCKS, (V,) * 5)
     first = call(first_step, (ROWS, WIDE), 6 * 8 * ROWS * ROWS * WIDE, BLOCKS // 3, (V,) * 7 + (S,) * 2)
     second = call(second_step, (WIDE, ROWS), 6 * 8 * ROWS * ROWS * WIDE, BLOCKS // 3, (V,) * 8 + (S,) * 2)
-    a, b, c, d = neighbours(start)
+    c, d, a, b = neighbours(start)
     own_part = own(start, a, b, *blocks)
     middle = first(own_part, c, d, *blocks, start, live, center, width)
-    a, b, c, d = neighbours(middle)
+    c, d, a, b = neighbours(middle)
     own_part = own(middle, a, b, *blocks)
     filtered = second(own_part, c, d, *blocks, middle, start, live, center, width)
     return jnp.transpose(filtered.reshape(ELEMS, BANDS, ROWS), (0, 2, 1))

time: 114 us -> 117 us (1.026)
  the two profiles are of different devices: /device:TPU:8 before, /device:TPU:15 now
where the time goes in v7:
time: 117 us
  starting transfers between devices  66.8 us (57%)
  blocking collectives  23.8 us (20%)
  waiting for transfers between devices  13 us (11%)
  Pallas kernels  6.63 us (6%)
  local copies, waits for them, and re-layouts  4.75 us (4%)
  between operations  1.53 us (1%)
    ppermute x4, starting transfers between devices, swapped(): return lax.ppermute(v, 'z_hi', pairs + [(b, a) for a, b in pairs])  30.5 us
    all_to_all x1, blocking collectives, shards(): lax.all_to_all(parts, NEARS, split_axis=0, concat_axis=0, tiled=True)  23.8 us
    ppermute x1, starting transfers between devices, shards(): other = lax.ppermute(mine, 'core', [(0, 1), (1, 0)])  8.41 us
    all_to_all x1, starting transfers between devices, shards(): cut = lax.all_to_all(cut, 'z_lo', split_axis=0, concat_axis=0, tiled=True)  6.98 us
    ppermute x2, starting transfers between devices, neighbours(): lax.ppermute(field, 'layer', [(i + 1, i) for i in range(LAYERS - 1)])  6.72 us
    ppermute x1, starting transfers between devices, shards(): other = lax.ppermute(mine, 'y_hi', [(0, 1), (1, 0)])  6.55 us
    ppermute x2, waiting for transfers between devices, neighbours(): lax.ppermute(field, RING, [(i, (i - 1) % ring) for i in range(ring)])  4.95 us
    unnamed x8, local copies, waits for them, and re-layouts  4.74 us
  transfers between devices with their start and end apart: 15, of which 6 were waited for; matrix products, arithmetic and copies ran while one was open for 0% of the time, Pallas kernels for 3%

profile of v7, /device:TPU:15, one launch (start us, length us, event | category | flops | bytes accessed | tf_op | source)
XLA Modules:
  0.0 116.6 jit_solution(8717064300048756708)
XLA Ops:
  0.0 0.0 copy-start.2
  0.0 0.9 copy-done.2
  0.9 0.7 shard_map.64
  1.6 7.0 %all-to-all-start = ((f32[4,40,128]{2,1,0:T(8,128)}), f32[4,40,128]{2,1,0:T(8,128)S(1)}, u32[]{:S(2)}, u32[]{:S(2)}) async-start(f32[4,40,128]{2,1,0:T(8,128)} %shard_map.64), calls=%async_computation | async-start | bytes 163840 | tf_op jit(solution)/shard_map/all_to_all | solution.py:265
  8.6 0.0 copy-start.1
  8.6 0.9 copy-done.1
  9.5 6.6 %collective-permute-start = (f32[4,32,128]{2,1,0:T(8,128)S(1)}, f32[4,32,128]{2,1,0:T(8,128)S(1)}, u32[]{:S(2)}, u32[]{:S(2)}) collective-permute-start(f32[4,32,128]{2,1,0:T(8,128)S(1)} %shard_map.65.mine_ref), channel_id=1, source_target_pairs={{0,1},{1,0},{2,3},{3,2},{4,5},{5,4},{6,7},{7,6},{8,9},{9,8},{10,11... | collective-permute-start | bytes 196616 | tf_op jit(solution)/shard_map/ppermute | solution.py:263
  16.1 2.5 %collective-permute-done.other_ref = f32[4,32,128]{2,1,0:T(8,128)S(1)} collective-permute-done((f32[4,32,128]{2,1,0:T(8,128)S(1)}, f32[4,32,128]{2,1,0:T(8,128)S(1)}, u32[]{:S(2)}, u32[]{:S(2)}) %collective-permute-start) | collective-permute-done | bytes 65568 | tf_op jit(solution)/shard_map/ppermute | solution.py:263
  18.5 0.0 all-to-all-done.rows_ref
  18.6 0.1 shard_map.66
  18.7 10.6 %collective-permute-start.1 = (f32[256,128]{1,0:T(8,128)S(1)}, f32[256,128]{1,0:T(8,128)S(1)}, u32[]{:S(2)}, u32[]{:S(2)}) collective-permute-start(f32[256,128]{1,0:T(8,128)S(1)} %get-tuple-element.15.first_ref), channel_id=1, source_target_pairs={{0,8},{16,24},{8,0},{24,16},{1,9},{17,25},{9,1},{25,17},{2,10},{18... | collective-permute-start | bytes 393224 | tf_op jit(solution)/shard_map/ppermute | solution.py:252
  29.3 7.9 %collective-permute-start.2 = (f32[256,128]{1,0:T(8,128)S(1)}, f32[256,128]{1,0:T(8,128)S(1)}, u32[]{:S(2)}, u32[]{:S(2)}) collective-permute-start(f32[256,128]{1,0:T(8,128)S(1)} %get-tuple-element.16.second_ref), channel_id=1, source_target_pairs={{8,16},{24,0},{16,8},{0,24},{9,17},{25,1},{17,9},{1,25},{10,18},{2... | collective-permute-start | bytes 393224 | tf_op jit(solution)/shard_map/ppermute | solution.py:252
  37.3 0.0 copy-start
  37.3 2.3 %copy-done = f32[4,7,160,160]{3,2,1,0:T(8,128)S(1)} copy-done((f32[4,7,160,160]{3,2,1,0:T(8,128)S(1)}, f32[4,7,160,160]{3,2,1,0:T(8,128)}, u32[]{:S(2)}) %copy-start) | copy-done | bytes 2867224
  39.6 0.0 copy-start.3
  39.6 0.7 copy-done.3
  40.2 1.2 %shard_map.67 = (bf16[4,7,160,160]{3,2,1,0:T(8,128)(2,1)S(1)}, bf16[4,7,160,160]{3,2,1,0:T(8,128)(2,1)S(1)}, bf16[160,128]{1,0:T(8,128)(2,1)S(1)}) custom-call(f32[4,7,160,160]{3,2,1,0:T(8,128)S(1)} %copy-done, s32[4]{0:T(128)S(1)} %copy-done.3), custom_call_target="tpu_custom_call" | custom-call | bytes 9175040 | tf_op jit(solution)/shard_map/pallas_call | solution.py:270
  41.4 0.0 collective-permute-done.1.near_ref
  41.4 2.4 %collective-permute-start.3 = (f32[112,128]{1,0:T(8,128)S(1)}, f32[112,128]{1,0:T(8,128)S(1)}, u32[]{:S(2)}, u32[]{:S(2)}) collective-permute-start(f32[112,128]{1,0:T(8,128)S(1)} %slice.6), channel_id=1, source_target_pairs={{8,16},{24,0},{16,8},{0,24},{9,17},{25,1},{17,9},{1,25},{10,18},{2... | collective-permute-start | bytes 172040 | tf_op jit(solution)/shard_map/ppermute | solution.py:252
  43.8 0.0 collective-permute-done.2.next_ref
  43.8 9.5 %collective-permute-start.4 = (f32[112,128]{1,0:T(8,128)S(1)}, f32[112,128]{1,0:T(8,128)S(1)}, u32[]{:S(2)}, u32[]{:S(2)}) collective-permute-start(f32[112,128]{1,0:T(8,128)S(1)} %slice.8), channel_id=1, source_target_pairs={{0,8},{16,24},{8,0},{24,16},{1,9},{17,25},{9,1},{25,17},{2,10},{18... | collective-permute-start | bytes 172040 | tf_op jit(solution)/shard_map/ppermute | solution.py:252
  53.3 0.0 collective-permute-done.3.passed_ref
  53.3 3.0 %collective-permute-done.4.last_ref = f32[112,128]{1,0:T(8,128)S(1)} collective-permute-done((f32[112,128]{1,0:T(8,128)S(1)}, f32[112,128]{1,0:T(8,128)S(1)}, u32[]{:S(2)}, u32[]{:S(2)}) %collective-permute-start.4) | collective-permute-done | bytes 57376 | tf_op jit(solution)/shard_map/ppermute | solution.py:252
  56.3 8.4 %collective-permute-start.5 = (f32[256,128]{1,0:T(8,128)S(1)}, f32[256,128]{1,0:T(8,128)S(1)}, u32[]{:S(2)}, u32[]{:S(2)}) collective-permute-start(f32[256,128]{1,0:T(8,128)S(1)} %shard_map.68.mine_ref), channel_id=1, source_target_pairs={{0,32},{32,0},{1,33},{33,1},{2,34},{34,2},{3,35},{35,3},{4,36},{36... | collective-permute-start | bytes 393224 | tf_op jit(solution)/shard_map/ppermute | solution.py:274
  64.7 1.0 collective-permute-done.5.other_ref
  65.7 0.6 shard_map.69
  66.3 23.8 %all_to_all.10.parts_ref = f32[8,80,128]{2,1,0:T(8,128)S(1)} all-to-all(f32[8,80,128]{2,1,0:T(8,128)S(1)} %shard_map.69), channel_id=1, replica_groups=mesh['layer'=4,'column'=4,'core'=2,'z_hi'=4,'z_lo'=4,'y_hi'=2] {'z_lo','..., dimensions={0} | all-to-all | bytes 655360 | tf_op jit(solution)/shard_map/all_to_all | solution.py:279
  90.1 0.1 shard_map.70.field_ref.start_ref
  90.2 1.9 %collective-permute-start.6 = (f32[160,128]{1,0:T(8,128)S(1)}, f32[160,128]{1,0:T(8,128)S(1)}, u32[]{:S(2)}, u32[]{:S(2)}) collective-permute-start(f32[160,128]{1,0:T(8,128)S(1)} %shard_map.70.field_ref.start_ref), channel_id=1, source_target_pairs={{0,256},{256,512},{512,768},{1,257},{257,513},{513,769},{2,258},{2... | collective-permute-start | bytes 245768 | tf_op jit(solution)/shard_map/ppermute | solution.py:245
  92.1 3.4 %collective-permute-start.7 = (f32[160,128]{1,0:T(8,128)S(1)}, f32[160,128]{1,0:T(8,128)S(1)}, u32[]{:S(2)}, u32[]{:S(2)}) collective-permute-start(f32[160,128]{1,0:T(8,128)S(1)} %shard_map.70.field_ref.start_ref), channel_id=1, source_target_pairs={{256,0},{512,256},{768,512},{257,1},{513,257},{769,513},{258,2},{5... | collective-permute-start | bytes 245768 | tf_op jit(solution)/shard_map/ppermute | solution.py:246
  95.5 3.0 %collective-permute-start.8 = (f32[160,128]{1,0:T(8,128)S(1)}, f32[160,128]{1,0:T(8,128)S(1)}, u32[]{:S(2)}, u32[]{:S(2)}) collective-permute-start(f32[160,128]{1,0:T(8,128)S(1)} %shard_map.70.field_ref.start_ref), channel_id=1, source_target_pairs={{0,32},{32,64},{64,96},{96,128},{128,160},{160,192},{192,224},{224... | collective-permute-start | bytes 245768 | tf_op jit(solution)/shard_map/ppermute | solution.py:243
  98.4 0.0 collective-permute-start.9
  99.7 0.0 collective-permute-done.6.a_ref
  99.7 0.0 collective-permute-done.7.b_ref
  99.8 1.1 shard_map.71.own_ref
  100.9 0.0 collective-permute-done.8.c_ref
  100.9 2.6 %collective-permute-done.9.d_ref = f32[160,128]{1,0:T(8,128)S(1)} collective-permute-done((f32[160,128]{1,0:T(8,128)S(1)}, f32[160,128]{1,0:T(8,128)S(1)}, u32[]{:S(2)}, u32[]{:S(2)}) %collective-permute-start.9) | collective-permute-done | bytes 81952 | tf_op jit(solution)/shard_map/ppermute | solution.py:244
  103.5 0.5 shard_map.72.field_ref.middle_ref
  104.0 1.9 %collective-permute-start.10 = (f32[160,128]{1,0:T(8,128)S(1)}, f32[160,128]{1,0:T(8,128)S(1)}, u32[]{:S(2)}, u32[]{:S(2)}) collective-permute-start(f32[160,128]{1,0:T(8,128)S(1)} %shard_map.72.field_ref.middle_ref), channel_id=1, source_target_pairs={{0,256},{256,512},{512,768},{1,257},{257,513},{513,769},{2,258},{2... | collective-permute-start | bytes 245768 | tf_op jit(solution)/shard_map/ppermute | solution.py:245
  106.0 3.4 %collective-permute-start.11 = (f32[160,128]{1,0:T(8,128)S(1)}, f32[160,128]{1,0:T(8,128)S(1)}, u32[]{:S(2)}, u32[]{:S(2)}) collective-permute-start(f32[160,128]{1,0:T(8,128)S(1)} %shard_map.72.field_ref.middle_ref), channel_id=1, source_target_pairs={{256,0},{512,256},{768,512},{257,1},{513,257},{769,513},{258,2},{5... | collective-permute-start | bytes 245768 | tf_op jit(solution)/shard_map/ppermute | solution.py:246
  109.3 0.9 collective-permute-start.12
  110.2 0.0 collective-permute-start.13
  110.2 0.0 collective-permute-done.10.a_ref
  110.2 1.6 %collective-permute-done.11.b_ref = f32[160,128]{1,0:T(8,128)S(1)} collective-permute-done((f32[160,128]{1,0:T(8,128)S(1)}, f32[160,128]{1,0:T(8,128)S(1)}, u32[]{:S(2)}, u32[]{:S(2)}) %collective-permute-start.11) | collective-permute-done | bytes 81952 | tf_op jit(solution)/shard_map/ppermute | solution.py:246
  111.9 1.1 shard_map.73.own_ref
  113.0 0.0 collective-permute-done.12.c_ref
  113.0 2.3 %collective-permute-done.13.d_ref = f32[160,128]{1,0:T(8,128)S(1)} collective-permute-done((f32[160,128]{1,0:T(8,128)S(1)}, f32[160,128]{1,0:T(8,128)S(1)}, u32[]{:S(2)}, u32[]{:S(2)}) %collective-permute-start.13) | collective-permute-done | bytes 81952 | tf_op jit(solution)/shard_map/ppermute | solution.py:244
  115.3 1.3 %shard_map.74 = f32[128,160]{1,0:T(8,128)} custom-call(f32[160,128]{1,0:T(8,128)S(1)} %shard_map.73.own_ref, f32[160,128]{1,0:T(8,128)S(1)} %collective-permute-done.12.c_ref, f32[160,128]{1,0:T(8,128)S(1)} %collective-permute-done.13.d_ref, bf16[4,7,160,160]{3,2,1,0:T(8,128)(2,1)S(1)} %get-tuple-element.23.high_ref, ...), custom_call_target="tpu_custom_call" | custom-call | flops 157286400 | bytes 1529173 | tf_op jit(solution)/shard_map/pallas_call | solution.py:291
  (4 shorter events, 0.0 us)
Async XLA Ops:
  0.0 0.9 copy-start.2
  1.6 16.9 %all-to-all-start = ((f32[4,40,128]{2,1,0:T(8,128)}), f32[4,40,128]{2,1,0:T(8,128)S(1)}, u32[]{:S(2)}, u32[]{:S(2)}) async-start(f32[4,40,128]{2,1,0:T(8,128)} %shard_map.64), calls=%async_computation | async-start | bytes 163840 | tf_op jit(solution)/shard_map/all_to_all | solution.py:265
  8.6 0.9 copy-start.1
  9.5 9.0 %collective-permute-start = (f32[4,32,128]{2,1,0:T(8,128)S(1)}, f32[4,32,128]{2,1,0:T(8,128)S(1)}, u32[]{:S(2)}, u32[]{:S(2)}) collective-permute-start(f32[4,32,128]{2,1,0:T(8,128)S(1)} %shard_map.65.mine_ref), channel_id=1, source_target_pairs={{0,1},{1,0},{2,3},{3,2},{4,5},{5,4},{6,7},{7,6},{8,9},{9,8},{10,11... | collective-permute-start | bytes 196616 | tf_op jit(solution)/shard_map/ppermute | solution.py:263
  18.7 22.7 %collective-permute-start.1 = (f32[256,128]{1,0:T(8,128)S(1)}, f32[256,128]{1,0:T(8,128)S(1)}, u32[]{:S(2)}, u32[]{:S(2)}) collective-permute-start(f32[256,128]{1,0:T(8,128)S(1)} %get-tuple-element.15.first_ref), channel_id=1, source_target_pairs={{0,8},{16,24},{8,0},{24,16},{1,9},{17,25},{9,1},{25,17},{2,10},{18... | collective-permute-start | bytes 393224 | tf_op jit(solution)/shard_map/ppermute | solution.py:252
  29.3 14.5 %collective-permute-start.2 = (f32[256,128]{1,0:T(8,128)S(1)}, f32[256,128]{1,0:T(8,128)S(1)}, u32[]{:S(2)}, u32[]{:S(2)}) collective-permute-start(f32[256,128]{1,0:T(8,128)S(1)} %get-tuple-element.16.second_ref), channel_id=1, source_target_pairs={{8,16},{24,0},{16,8},{0,24},{9,17},{25,1},{17,9},{1,25},{10,18},{2... | collective-permute-start | bytes 393224 | tf_op jit(solution)/shard_map/ppermute | solution.py:252
  37.3 2.3 %copy-start = (f32[4,7,160,160]{3,2,1,0:T(8,128)S(1)}, f32[4,7,160,160]{3,2,1,0:T(8,128)}, u32[]{:S(2)}) copy-start(f32[4,7,160,160]{3,2,1,0:T(8,128)} %hamiltonian_ref.1) | copy-start | bytes 8601604
  39.6 0.7 copy-start.3
  41.4 11.9 %collective-permute-start.3 = (f32[112,128]{1,0:T(8,128)S(1)}, f32[112,128]{1,0:T(8,128)S(1)}, u32[]{:S(2)}, u32[]{:S(2)}) collective-permute-start(f32[112,128]{1,0:T(8,128)S(1)} %slice.6), channel_id=1, source_target_pairs={{8,16},{24,0},{16,8},{0,24},{9,17},{25,1},{17,9},{1,25},{10,18},{2... | collective-permute-start | bytes 172040 | tf_op jit(solution)/shard_map/ppermute | solution.py:252
  43.8 12.5 %collective-permute-start.4 = (f32[112,128]{1,0:T(8,128)S(1)}, f32[112,128]{1,0:T(8,128)S(1)}, u32[]{:S(2)}, u32[]{:S(2)}) collective-permute-start(f32[112,128]{1,0:T(8,128)S(1)} %slice.8), channel_id=1, source_target_pairs={{0,8},{16,24},{8,0},{24,16},{1,9},{17,25},{9,1},{25,17},{2,10},{18... | collective-permute-start | bytes 172040 | tf_op jit(solution)/shard_map/ppermute | solution.py:252
  56.3 9.4 %collective-permute-start.5 = (f32[256,128]{1,0:T(8,128)S(1)}, f32[256,128]{1,0:T(8,128)S(1)}, u32[]{:S(2)}, u32[]{:S(2)}) collective-permute-start(f32[256,128]{1,0:T(8,128)S(1)} %shard_map.68.mine_ref), channel_id=1, source_target_pairs={{0,32},{32,0},{1,33},{33,1},{2,34},{34,2},{3,35},{35,3},{4,36},{36... | collective-permute-start | bytes 393224 | tf_op jit(solution)/shard_map/ppermute | solution.py:274
  90.2 9.6 %collective-permute-start.6 = (f32[160,128]{1,0:T(8,128)S(1)}, f32[160,128]{1,0:T(8,128)S(1)}, u32[]{:S(2)}, u32[]{:S(2)}) collective-permute-start(f32[160,128]{1,0:T(8,128)S(1)} %shard_map.70.field_ref.start_ref), channel_id=1, source_target_pairs={{0,256},{256,512},{512,768},{1,257},{257,513},{513,769},{2,258},{2... | collective-permute-start | bytes 245768 | tf_op jit(solution)/shard_map/ppermute | solution.py:245
  92.1 7.7 %collective-permute-start.7 = (f32[160,128]{1,0:T(8,128)S(1)}, f32[160,128]{1,0:T(8,128)S(1)}, u32[]{:S(2)}, u32[]{:S(2)}) collective-permute-start(f32[160,128]{1,0:T(8,128)S(1)} %shard_map.70.field_ref.start_ref), channel_id=1, source_target_pairs={{256,0},{512,256},{768,512},{257,1},{513,257},{769,513},{258,2},{5... | collective-permute-start | bytes 245768 | tf_op jit(solution)/shard_map/ppermute | solution.py:246
  95.5 5.4 %collective-permute-start.8 = (f32[160,128]{1,0:T(8,128)S(1)}, f32[160,128]{1,0:T(8,128)S(1)}, u32[]{:S(2)}, u32[]{:S(2)}) collective-permute-start(f32[160,128]{1,0:T(8,128)S(1)} %shard_map.70.field_ref.start_ref), channel_id=1, source_target_pairs={{0,32},{32,64},{64,96},{96,128},{128,160},{160,192},{192,224},{224... | collective-permute-start | bytes 245768 | tf_op jit(solution)/shard_map/ppermute | solution.py:243
  98.4 5.1 %collective-permute-start.9 = (f32[160,128]{1,0:T(8,128)S(1)}, f32[160,128]{1,0:T(8,128)S(1)}, u32[]{:S(2)}, u32[]{:S(2)}) collective-permute-start(f32[160,128]{1,0:T(8,128)S(1)} %shard_map.70.field_ref.start_ref), channel_id=1, source_target_pairs={{0,224},{32,0},{64,32},{96,64},{128,96},{160,128},{192,160},{224,1... | collective-permute-start | bytes 245768 | tf_op jit(solution)/shard_map/ppermute | solution.py:244
  104.0 6.2 %collective-permute-start.10 = (f32[160,128]{1,0:T(8,128)S(1)}, f32[160,128]{1,0:T(8,128)S(1)}, u32[]{:S(2)}, u32[]{:S(2)}) collective-permute-start(f32[160,128]{1,0:T(8,128)S(1)} %shard_map.72.field_ref.middle_ref), channel_id=1, source_target_pairs={{0,256},{256,512},{512,768},{1,257},{257,513},{513,769},{2,258},{2... | collective-permute-start | bytes 245768 | tf_op jit(solution)/shard_map/ppermute | solution.py:245
  106.0 5.9 %collective-permute-start.11 = (f32[160,128]{1,0:T(8,128)S(1)}, f32[160,128]{1,0:T(8,128)S(1)}, u32[]{:S(2)}, u32[]{:S(2)}) collective-permute-start(f32[160,128]{1,0:T(8,128)S(1)} %shard_map.72.field_ref.middle_ref), channel_id=1, source_target_pairs={{256,0},{512,256},{768,512},{257,1},{513,257},{769,513},{258,2},{5... | collective-permute-start | bytes 245768 | tf_op jit(solution)/shard_map/ppermute | solution.py:246
  109.3 3.7 %collective-permute-start.12 = (f32[160,128]{1,0:T(8,128)S(1)}, f32[160,128]{1,0:T(8,128)S(1)}, u32[]{:S(2)}, u32[]{:S(2)}) collective-permute-start(f32[160,128]{1,0:T(8,128)S(1)} %shard_map.72.field_ref.middle_ref), channel_id=1, source_target_pairs={{0,32},{32,64},{64,96},{96,128},{128,160},{160,192},{192,224},{224... | collective-permute-start | bytes 245768 | tf_op jit(solution)/shard_map/ppermute | solution.py:243
  110.2 5.1 %collective-permute-start.13 = (f32[160,128]{1,0:T(8,128)S(1)}, f32[160,128]{1,0:T(8,128)S(1)}, u32[]{:S(2)}, u32[]{:S(2)}) collective-permute-start(f32[160,128]{1,0:T(8,128)S(1)} %shard_map.72.field_ref.middle_ref), channel_id=1, source_target_pairs={{0,224},{32,0},{64,32},{96,64},{128,96},{160,128},{192,160},{224,1... | collective-permute-start | bytes 245768 | tf_op jit(solution)/shard_map/ppermute | solution.py:244

commit v8 on v6

--- a/solution.py
+++ b/solution.py
@@ -74,18 +74,27 @@
 def cut_rotation(rotation_ref, mine_ref):
     for far in range(FAR):
         lanes = pl.ds(pl.multiple_of(256 * far + 128 * lax.axis_index("core"), 128), 128)
-        mine_ref[far] = rotation_ref[:, lanes]
-
-
-def cut_columns(orbitals_ref, out_ref):
+        mine_ref[0, far] = mine_ref[1, far] = rotation_ref[:, lanes]
+
+
+def low_place(by):
+    return lax.rem(lax.axis_index("z_lo") + by, LOW)
+
+
+def cut_columns(orbitals_ref, *out_refs):
     first = lax.broadcasted_iota(jnp.int32, (ELEMS, WIDE), 1) < 64
-    for i in range(PIECE):
-        for low in range(LOW):
-            half, odd = divmod(low, 2)
+    for by, out_ref in enumerate(out_refs):
+        low = low_place(by)
+        odd = jnp.full((ELEMS, WIDE), lax.rem(low, 2), jnp.int32) == 1
+        for i in range(PIECE):
             for k in range(2):
-                parts = [orbitals_ref[i, :, pl.ds(256 * far + 128 * half, 128)] for far in (2 * k, 2 * k + 1)]
-                parts[1 - odd] = turned(parts[1 - odd], 2)
-                out_ref[low, pl.ds(20 * k + ELEMS * i, ELEMS), :] = jnp.where(first, parts[0], parts[1])
+                parts = []
+                for far in (2 * k, 2 * k + 1):
+                    lanes = pl.ds(pl.multiple_of(256 * far + 128 * lax.div(low, 2), 128), 128)
+                    parts.append(orbitals_ref[i, :, lanes])
+                even_form = jnp.where(first, parts[0], turned(parts[1], 2))
+                odd_form = jnp.where(first, turned(parts[0], 2), parts[1])
+                out_ref[pl.ds(20 * k + ELEMS * i, ELEMS), :] = jnp.where(odd, odd_form, even_form)
 
 
 def far_place(by):
@@ -96,21 +105,18 @@
 PASS = HALF + 32
 
 
-def pack(rows_ref, mine_ref, other_ref, up_ref, down_ref, own_ref):
+def pack(rows_0, rows_1, rows_2, rows_3, both_ref, up_ref, down_ref, own_ref):
     for k in range(2):
         first, second = (down_ref, up_ref) if k else (up_ref, down_ref)
         for e in range(ELEMS):
-            for low in range(LOW):
+            for by, rows_ref in enumerate((rows_0, rows_1, rows_2, rows_3)):
                 for i in range(PIECE):
-                    at = 20 * e + PIECE * low + i
-                    row = rows_ref[low, pl.ds(20 * k + ELEMS * i + e, 1), :]
+                    at = 20 * e + PIECE * low_place(LOW - by) + i
+                    row = rows_ref[pl.ds(20 * k + ELEMS * i + e, 1), :]
                     first[pl.ds(at, 1), :] = row
                     second[pl.ds(PASS + at, 1), :] = row
-    lower = lax.axis_index("y_hi") == 0
-
     def slices(by):
-        mine, other = mine_ref[far_place(by)], other_ref[far_place(by)]
-        return jnp.where(lower, mine, other), jnp.where(lower, other, mine)
+        return both_ref[0, far_place(by)], both_ref[1, far_place(by)]
 
     up_ref[HALF:PASS, :], down_ref[HALF:PASS, :] = slices(2)
     tail = PASS + HALF
@@ -232,12 +238,14 @@
 
 def shards(orbitals, rotation, counts, hamiltonian, center, width):
     pieces = jnp.transpose(orbitals, (1, 0, 2))
-    mine = call(cut_rotation, (FAR, 32, WIDE), 0, 2 * FIELD, (V,))(rotation)
-    other = lax.ppermute(mine, "y_hi", [(0, 1), (1, 0)])
-    cut = call(cut_columns, (LOW, 2 * ELEMS * PIECE, WIDE), 0, 2 * FIELD, (V,))(pieces)
-    cut = lax.all_to_all(cut, "z_lo", split_axis=0, concat_axis=0, tiled=True)
+    both = call(cut_rotation, (2, FAR, 32, WIDE), 0, 3 * FIELD, (V,))(rotation)
+    both = lax.all_to_all(both, "y_hi", split_axis=0, concat_axis=0, tiled=True)
+    cut = call(cut_columns, ((2 * ELEMS * PIECE, WIDE),) * LOW, 0, 2 * FIELD, (V,))(pieces)
+    rows = [cut[0]] + [
+        lax.ppermute(cut[by], "z_lo", [(i, (i + by) % LOW) for i in range(LOW)]) for by in range(1, LOW)
+    ]
     message = (2 * PASS + 32, WIDE)
-    up, down, slices = call(pack, (message, message, (64, WIDE)), 0, 6 * FIELD, (V,) * 3)(cut, mine, other)
+    up, down, slices = call(pack, (message, message, (64, WIDE)), 0, 6 * FIELD, (V,) * 5)(*rows, both)
     above, below = far_step(down, -1), far_step(up, 1)
     shapes = (hamiltonian.shape, hamiltonian.shape, (ROWS, WIDE))
     blocks = call(split_blocks, shapes, 0, 2 * BLOCKS, (V, S), (), BF16)(hamiltonian, counts)

time: 114 us -> 118 us (1.035)
  starting transfers between devices: 64.3 us -> 66.6 us
  waiting for transfers between devices: 12.1 us -> 14.3 us
    ppermute x1 -> x3, starting transfers between devices: 6.83 us -> 12.8 us  [shards(): lax.ppermute(cut[by], 'z_lo', [(i, (i + by) % LOW) for i in range(LOW)])]
    ppermute x4, starting transfers between devices: 30.8 us -> 28 us  [far_step(): return lax.ppermute(v, 'z_hi', [(i, (i + by) % FAR) for i in range(FAR)])]
    ppermute x4, waiting for transfers between devices: 4.5 us -> 7.17 us  [far_step(): return lax.ppermute(v, 'z_hi', [(i, (i + by) % FAR) for i in range(FAR)])]
    ppermute x1 -> x3, waiting for transfers between devices: 3.33 us -> 3.19 us  [shards(): lax.ppermute(cut[by], 'z_lo', [(i, (i + by) % LOW) for i in range(LOW)])]
  transfers between devices with their start and end apart: 15 -> 17, of which waited for: 5 -> 6; matrix products, arithmetic and copies ran while one was open for 0% -> 0% of each run, Pallas kernels for 3% -> 3%
where the time goes in v8:
time: 118 us; the launch traced here: 117 us
  starting transfers between devices  66.6 us (56%)
  blocking collectives  23.1 us (20%)
  waiting for transfers between devices  14.3 us (12%)
  Pallas kernels  6.69 us (6%)
  local copies, waits for them, and re-layouts  4.75 us (4%)
  between operations  1.56 us (1%)
    ppermute x4, starting transfers between devices, far_step(): return lax.ppermute(v, 'z_hi', [(i, (i + by) % FAR) for i in range(FAR)])  28 us
    all_to_all x1, blocking collectives, shards(): lax.all_to_all(parts, NEARS, split_axis=0, concat_axis=0, tiled=True)  23.1 us
    ppermute x3, starting transfers between devices, shards(): lax.ppermute(cut[by], 'z_lo', [(i, (i + by) % LOW) for i in range(LOW)])  12.8 us
    ppermute x4, waiting for transfers between devices, far_step(): return lax.ppermute(v, 'z_hi', [(i, (i + by) % FAR) for i in range(FAR)])  7.17 us
    ppermute x2, starting transfers between devices, neighbours(): lax.ppermute(field, 'layer', [(i + 1, i) for i in range(LAYERS - 1)])  6.48 us
    all_to_all x1, starting transfers between devices, shards(): both = lax.all_to_all(both, 'y_hi', split_axis=0, concat_axis=0, tiled=True)  6.19 us
    ppermute x2, starting transfers between devices, neighbours(): lax.ppermute(field, RING, [(i, (i - 1) % ring) for i in range(ring)])  5.89 us
    ppermute x2, starting transfers between devices, neighbours(): lax.ppermute(field, 'layer', [(i, i + 1) for i in range(LAYERS - 1)])  5.18 us
  transfers between devices with their start and end apart: 17, of which 6 were waited for; matrix products, arithmetic and copies ran while one was open for 0% of the time, Pallas kernels for 3%

profile of v8, /device:TPU:8, one launch (start us, length us, event | category | flops | bytes accessed | tf_op | source)
XLA Modules:
  0.0 116.9 jit_solution(2497112248686366912)
XLA Ops:
  0.0 0.0 copy-start.1
  0.0 0.9 copy-done.1
  0.9 0.7 shard_map.65
  1.6 6.2 %all-to-all-start = ((f32[2,4,32,128]{3,2,1,0:T(8,128)}), f32[2,4,32,128]{3,2,1,0:T(8,128)S(1)}, u32[]{:S(2)}, u32[]{:S(2)}) async-start(f32[2,4,32,128]{3,2,1,0:T(8,128)} %shard_map.65), calls=%async_computation | async-start | bytes 262144 | tf_op jit(solution)/shard_map/all_to_all | solution.py:242
  7.8 0.0 copy-start.2
  7.8 0.9 copy-done.2
  8.7 0.1 shard_map.64
  8.8 4.3 %collective-permute-start = (f32[40,128]{1,0:T(8,128)S(1)}, f32[40,128]{1,0:T(8,128)S(1)}, u32[]{:S(2)}, u32[]{:S(2)}) collective-permute-start(f32[40,128]{1,0:T(8,128)S(1)} %get-tuple-element.20), channel_id=1, source_target_pairs={{0,2},{2,4},{4,6},{6,0},{1,3},{3,5},{5,7},{7,1},{8,10},{10,12},{12... | collective-permute-start | bytes 61448 | tf_op jit(solution)/shard_map/ppermute | solution.py:245
  13.1 6.1 %collective-permute-start.1 = (f32[40,128]{1,0:T(8,128)S(1)}, f32[40,128]{1,0:T(8,128)S(1)}, u32[]{:S(2)}, u32[]{:S(2)}) collective-permute-start(f32[40,128]{1,0:T(8,128)S(1)} %get-tuple-element.21), channel_id=1, source_target_pairs={{0,4},{2,6},{4,0},{6,2},{1,5},{3,7},{5,1},{7,3},{8,12},{10,14},{12... | collective-permute-start | bytes 61448 | tf_op jit(solution)/shard_map/ppermute | solution.py:245
  19.2 2.5 %collective-permute-start.2 = (f32[40,128]{1,0:T(8,128)S(1)}, f32[40,128]{1,0:T(8,128)S(1)}, u32[]{:S(2)}, u32[]{:S(2)}) collective-permute-start(f32[40,128]{1,0:T(8,128)S(1)} %get-tuple-element.22), channel_id=1, source_target_pairs={{0,6},{2,0},{4,2},{6,4},{1,7},{3,1},{5,3},{7,5},{8,14},{10,8},{12,... | collective-permute-start | bytes 61448 | tf_op jit(solution)/shard_map/ppermute | solution.py:245
  21.7 0.0 collective-permute-done.rows_1
  21.7 0.0 collective-permute-done.1.rows_2
  21.7 3.2 %collective-permute-done.2.rows_3 = f32[40,128]{1,0:T(8,128)S(1)} collective-permute-done((f32[40,128]{1,0:T(8,128)S(1)}, f32[40,128]{1,0:T(8,128)S(1)}, u32[]{:S(2)}, u32[]{:S(2)}) %collective-permute-start.2) | collective-permute-done | bytes 20512 | tf_op jit(solution)/shard_map/ppermute | solution.py:245
  24.9 0.0 all-to-all-done.both_ref
  24.9 0.1 shard_map.66
  25.0 10.9 %collective-permute-start.3 = (f32[256,128]{1,0:T(8,128)S(1)}, f32[256,128]{1,0:T(8,128)S(1)}, u32[]{:S(2)}, u32[]{:S(2)}) collective-permute-start(f32[256,128]{1,0:T(8,128)S(1)} %get-tuple-element.23.up_ref), channel_id=1, source_target_pairs={{0,8},{8,16},{16,24},{24,0},{1,9},{9,17},{17,25},{25,1},{2,10},{10... | collective-permute-start | bytes 393224 | tf_op jit(solution)/shard_map/ppermute | solution.py:231
  35.9 6.5 %collective-permute-start.4 = (f32[256,128]{1,0:T(8,128)S(1)}, f32[256,128]{1,0:T(8,128)S(1)}, u32[]{:S(2)}, u32[]{:S(2)}) collective-permute-start(f32[256,128]{1,0:T(8,128)S(1)} %get-tuple-element.24.down_ref), channel_id=1, source_target_pairs={{0,24},{8,0},{16,8},{24,16},{1,25},{9,1},{17,9},{25,17},{2,26},{10... | collective-permute-start | bytes 393224 | tf_op jit(solution)/shard_map/ppermute | solution.py:231
  42.4 0.0 copy-start
  42.4 2.3 %copy-done = f32[4,7,160,160]{3,2,1,0:T(8,128)S(1)} copy-done((f32[4,7,160,160]{3,2,1,0:T(8,128)S(1)}, f32[4,7,160,160]{3,2,1,0:T(8,128)}, u32[]{:S(2)}) %copy-start) | copy-done | bytes 2867224
  44.7 0.0 copy-start.3
  44.7 0.7 copy-done.3
  45.4 1.2 shard_map.67
  46.5 0.0 collective-permute-done.3.below_ref
  46.6 4.4 %collective-permute-start.5 = (f32[112,128]{1,0:T(8,128)S(1)}, f32[112,128]{1,0:T(8,128)S(1)}, u32[]{:S(2)}, u32[]{:S(2)}) collective-permute-start(f32[112,128]{1,0:T(8,128)S(1)} %slice.6), channel_id=1, source_target_pairs={{0,8},{8,16},{16,24},{24,0},{1,9},{9,17},{17,25},{25,1},{2,10},{10... | collective-permute-start | bytes 172040 | tf_op jit(solution)/shard_map/ppermute | solution.py:231
  51.0 2.4 %collective-permute-done.4.above_ref = f32[256,128]{1,0:T(8,128)S(1)} collective-permute-done((f32[256,128]{1,0:T(8,128)S(1)}, f32[256,128]{1,0:T(8,128)S(1)}, u32[]{:S(2)}, u32[]{:S(2)}) %collective-permute-start.4) | collective-permute-done | bytes 131104 | tf_op jit(solution)/shard_map/ppermute | solution.py:231
  53.4 6.2 %collective-permute-start.6 = (f32[112,128]{1,0:T(8,128)S(1)}, f32[112,128]{1,0:T(8,128)S(1)}, u32[]{:S(2)}, u32[]{:S(2)}) collective-permute-start(f32[112,128]{1,0:T(8,128)S(1)} %slice.8), channel_id=1, source_target_pairs={{0,24},{8,0},{16,8},{24,16},{1,25},{9,1},{17,9},{25,17},{2,26},{10... | collective-permute-start | bytes 172040 | tf_op jit(solution)/shard_map/ppermute | solution.py:231
  59.6 0.0 collective-permute-done.5.passed_up_ref
  59.7 4.7 %collective-permute-done.6.passed_down_ref = f32[112,128]{1,0:T(8,128)S(1)} collective-permute-done((f32[112,128]{1,0:T(8,128)S(1)}, f32[112,128]{1,0:T(8,128)S(1)}, u32[]{:S(2)}, u32[]{:S(2)}) %collective-permute-start.6) | collective-permute-done | bytes 57376 | tf_op jit(solution)/shard_map/ppermute | solution.py:231
  64.4 1.9 %collective-permute-start.7 = (f32[256,128]{1,0:T(8,128)S(1)}, f32[256,128]{1,0:T(8,128)S(1)}, u32[]{:S(2)}, u32[]{:S(2)}) collective-permute-start(f32[256,128]{1,0:T(8,128)S(1)} %shard_map.68.mine_ref), channel_id=1, source_target_pairs={{0,32},{32,0},{1,33},{33,1},{2,34},{34,2},{3,35},{35,3},{4,36},{36... | collective-permute-start | bytes 393224 | tf_op jit(solution)/shard_map/ppermute | solution.py:255
  66.3 1.3 %collective-permute-done.7.other_ref = f32[256,128]{1,0:T(8,128)S(1)} collective-permute-done((f32[256,128]{1,0:T(8,128)S(1)}, f32[256,128]{1,0:T(8,128)S(1)}, u32[]{:S(2)}, u32[]{:S(2)}) %collective-permute-start.7) | collective-permute-done | bytes 131104 | tf_op jit(solution)/shard_map/ppermute | solution.py:255
  67.7 0.6 shard_map.69
  68.2 23.1 %all_to_all.10.parts_ref = f32[8,80,128]{2,1,0:T(8,128)S(1)} all-to-all(f32[8,80,128]{2,1,0:T(8,128)S(1)} %shard_map.69), channel_id=1, replica_groups=mesh['layer'=4,'column'=4,'core'=2,'z_hi'=4,'z_lo'=4,'y_hi'=2] {'z_lo','..., dimensions={0} | all-to-all | bytes 655360 | tf_op jit(solution)/shard_map/all_to_all | solution.py:260
  91.3 0.1 shard_map.70.field_ref.start_ref
  91.4 0.0 collective-permute-start.8
  91.4 2.9 %collective-permute-start.9 = (f32[160,128]{1,0:T(8,128)S(1)}, f32[160,128]{1,0:T(8,128)S(1)}, u32[]{:S(2)}, u32[]{:S(2)}) collective-permute-start(f32[160,128]{1,0:T(8,128)S(1)} %shard_map.70.field_ref.start_ref), channel_id=1, source_target_pairs={{0,224},{32,0},{64,32},{96,64},{128,96},{160,128},{192,160},{224,1... | collective-permute-start | bytes 245768 | tf_op jit(solution)/shard_map/ppermute | solution.py:224
  94.3 2.7 %collective-permute-start.10 = (f32[160,128]{1,0:T(8,128)S(1)}, f32[160,128]{1,0:T(8,128)S(1)}, u32[]{:S(2)}, u32[]{:S(2)}) collective-permute-start(f32[160,128]{1,0:T(8,128)S(1)} %shard_map.70.field_ref.start_ref), channel_id=1, source_target_pairs={{0,256},{256,512},{512,768},{1,257},{257,513},{513,769},{2,258},{2... | collective-permute-start | bytes 245768 | tf_op jit(solution)/shard_map/ppermute | solution.py:225
  97.0 3.2 %collective-permute-start.11 = (f32[160,128]{1,0:T(8,128)S(1)}, f32[160,128]{1,0:T(8,128)S(1)}, u32[]{:S(2)}, u32[]{:S(2)}) collective-permute-start(f32[160,128]{1,0:T(8,128)S(1)} %shard_map.70.field_ref.start_ref), channel_id=1, source_target_pairs={{256,0},{512,256},{768,512},{257,1},{513,257},{769,513},{258,2},{5... | collective-permute-start | bytes 245768 | tf_op jit(solution)/shard_map/ppermute | solution.py:226
  101.5 0.0 collective-permute-done.8.a_ref
  101.5 0.0 collective-permute-done.9.b_ref
  101.5 1.1 shard_map.71.own_ref
  102.6 0.0 collective-permute-done.10.c_ref
  102.6 0.7 collective-permute-done.11.d_ref
  103.3 0.5 shard_map.72.field_ref.middle_ref
  103.8 0.0 collective-permute-start.12
  103.9 2.9 %collective-permute-start.13 = (f32[160,128]{1,0:T(8,128)S(1)}, f32[160,128]{1,0:T(8,128)S(1)}, u32[]{:S(2)}, u32[]{:S(2)}) collective-permute-start(f32[160,128]{1,0:T(8,128)S(1)} %shard_map.72.field_ref.middle_ref), channel_id=1, source_target_pairs={{0,224},{32,0},{64,32},{96,64},{128,96},{160,128},{192,160},{224,1... | collective-permute-start | bytes 245768 | tf_op jit(solution)/shard_map/ppermute | solution.py:224
  106.8 2.5 %collective-permute-start.14 = (f32[160,128]{1,0:T(8,128)S(1)}, f32[160,128]{1,0:T(8,128)S(1)}, u32[]{:S(2)}, u32[]{:S(2)}) collective-permute-start(f32[160,128]{1,0:T(8,128)S(1)} %shard_map.72.field_ref.middle_ref), channel_id=1, source_target_pairs={{0,256},{256,512},{512,768},{1,257},{257,513},{513,769},{2,258},{2... | collective-permute-start | bytes 245768 | tf_op jit(solution)/shard_map/ppermute | solution.py:225
  109.3 3.3 %collective-permute-start.15 = (f32[160,128]{1,0:T(8,128)S(1)}, f32[160,128]{1,0:T(8,128)S(1)}, u32[]{:S(2)}, u32[]{:S(2)}) collective-permute-start(f32[160,128]{1,0:T(8,128)S(1)} %shard_map.72.field_ref.middle_ref), channel_id=1, source_target_pairs={{256,0},{512,256},{768,512},{257,1},{513,257},{769,513},{258,2},{5... | collective-permute-start | bytes 245768 | tf_op jit(solution)/shard_map/ppermute | solution.py:226
  112.7 0.0 collective-permute-done.12.a_ref
  112.7 0.0 collective-permute-done.13.b_ref
  112.7 1.1 shard_map.73.own_ref
  113.8 0.0 collective-permute-done.14.c_ref
  113.8 1.9 %collective-permute-done.15.d_ref = f32[160,128]{1,0:T(8,128)S(1)} collective-permute-done((f32[160,128]{1,0:T(8,128)S(1)}, f32[160,128]{1,0:T(8,128)S(1)}, u32[]{:S(2)}, u32[]{:S(2)}) %collective-permute-start.15) | collective-permute-done | bytes 81952 | tf_op jit(solution)/shard_map/ppermute | solution.py:226
  115.7 1.3 %shard_map.74 = f32[128,160]{1,0:T(8,128)} custom-call(f32[160,128]{1,0:T(8,128)S(1)} %shard_map.73.own_ref, f32[160,128]{1,0:T(8,128)S(1)} %collective-permute-done.14.c_ref, f32[160,128]{1,0:T(8,128)S(1)} %collective-permute-done.15.d_ref, bf16[4,7,160,160]{3,2,1,0:T(8,128)(2,1)S(1)} %get-tuple-element.31.high_ref, ...), custom_call_target="tpu_custom_call" | custom-call | flops 157286400 | bytes 1529173 | tf_op jit(solution)/shard_map/pallas_call | solution.py:272
  (3 shorter events, 0.0 us)
Async XLA Ops:
  0.0 0.9 copy-start.1
  1.6 23.3 %all-to-all-start = ((f32[2,4,32,128]{3,2,1,0:T(8,128)}), f32[2,4,32,128]{3,2,1,0:T(8,128)S(1)}, u32[]{:S(2)}, u32[]{:S(2)}) async-start(f32[2,4,32,128]{3,2,1,0:T(8,128)} %shard_map.65), calls=%async_computation | async-start | bytes 262144 | tf_op jit(solution)/shard_map/all_to_all | solution.py:242
  7.8 0.9 copy-start.2
  8.8 12.9 %collective-permute-start = (f32[40,128]{1,0:T(8,128)S(1)}, f32[40,128]{1,0:T(8,128)S(1)}, u32[]{:S(2)}, u32[]{:S(2)}) collective-permute-start(f32[40,128]{1,0:T(8,128)S(1)} %get-tuple-element.20), channel_id=1, source_target_pairs={{0,2},{2,4},{4,6},{6,0},{1,3},{3,5},{5,7},{7,1},{8,10},{10,12},{12... | collective-permute-start | bytes 61448 | tf_op jit(solution)/shard_map/ppermute | solution.py:245
  13.1 8.6 %collective-permute-start.1 = (f32[40,128]{1,0:T(8,128)S(1)}, f32[40,128]{1,0:T(8,128)S(1)}, u32[]{:S(2)}, u32[]{:S(2)}) collective-permute-start(f32[40,128]{1,0:T(8,128)S(1)} %get-tuple-element.21), channel_id=1, source_target_pairs={{0,4},{2,6},{4,0},{6,2},{1,5},{3,7},{5,1},{7,3},{8,12},{10,14},{12... | collective-permute-start | bytes 61448 | tf_op jit(solution)/shard_map/ppermute | solution.py:245
  19.2 5.7 %collective-permute-start.2 = (f32[40,128]{1,0:T(8,128)S(1)}, f32[40,128]{1,0:T(8,128)S(1)}, u32[]{:S(2)}, u32[]{:S(2)}) collective-permute-start(f32[40,128]{1,0:T(8,128)S(1)} %get-tuple-element.22), channel_id=1, source_target_pairs={{0,6},{2,0},{4,2},{6,4},{1,7},{3,1},{5,3},{7,5},{8,14},{10,8},{12,... | collective-permute-start | bytes 61448 | tf_op jit(solution)/shard_map/ppermute | solution.py:245
  25.0 21.6 %collective-permute-start.3 = (f32[256,128]{1,0:T(8,128)S(1)}, f32[256,128]{1,0:T(8,128)S(1)}, u32[]{:S(2)}, u32[]{:S(2)}) collective-permute-start(f32[256,128]{1,0:T(8,128)S(1)} %get-tuple-element.23.up_ref), channel_id=1, source_target_pairs={{0,8},{8,16},{16,24},{24,0},{1,9},{9,17},{17,25},{25,1},{2,10},{10... | collective-permute-start | bytes 393224 | tf_op jit(solution)/shard_map/ppermute | solution.py:231
  35.9 17.5 %collective-permute-start.4 = (f32[256,128]{1,0:T(8,128)S(1)}, f32[256,128]{1,0:T(8,128)S(1)}, u32[]{:S(2)}, u32[]{:S(2)}) collective-permute-start(f32[256,128]{1,0:T(8,128)S(1)} %get-tuple-element.24.down_ref), channel_id=1, source_target_pairs={{0,24},{8,0},{16,8},{24,16},{1,25},{9,1},{17,9},{25,17},{2,26},{10... | collective-permute-start | bytes 393224 | tf_op jit(solution)/shard_map/ppermute | solution.py:231
  42.4 2.3 %copy-start = (f32[4,7,160,160]{3,2,1,0:T(8,128)S(1)}, f32[4,7,160,160]{3,2,1,0:T(8,128)}, u32[]{:S(2)}) copy-start(f32[4,7,160,160]{3,2,1,0:T(8,128)} %hamiltonian_ref.1) | copy-start | bytes 8601604
  44.7 0.7 copy-start.3
  46.6 13.1 %collective-permute-start.5 = (f32[112,128]{1,0:T(8,128)S(1)}, f32[112,128]{1,0:T(8,128)S(1)}, u32[]{:S(2)}, u32[]{:S(2)}) collective-permute-start(f32[112,128]{1,0:T(8,128)S(1)} %slice.6), channel_id=1, source_target_pairs={{0,8},{8,16},{16,24},{24,0},{1,9},{9,17},{17,25},{25,1},{2,10},{10... | collective-permute-start | bytes 172040 | tf_op jit(solution)/shard_map/ppermute | solution.py:231
  53.4 11.0 %collective-permute-start.6 = (f32[112,128]{1,0:T(8,128)S(1)}, f32[112,128]{1,0:T(8,128)S(1)}, u32[]{:S(2)}, u32[]{:S(2)}) collective-permute-start(f32[112,128]{1,0:T(8,128)S(1)} %slice.8), channel_id=1, source_target_pairs={{0,24},{8,0},{16,8},{24,16},{1,25},{9,1},{17,9},{25,17},{2,26},{10... | collective-permute-start | bytes 172040 | tf_op jit(solution)/shard_map/ppermute | solution.py:231
  64.4 3.2 %collective-permute-start.7 = (f32[256,128]{1,0:T(8,128)S(1)}, f32[256,128]{1,0:T(8,128)S(1)}, u32[]{:S(2)}, u32[]{:S(2)}) collective-permute-start(f32[256,128]{1,0:T(8,128)S(1)} %shard_map.68.mine_ref), channel_id=1, source_target_pairs={{0,32},{32,0},{1,33},{33,1},{2,34},{34,2},{3,35},{35,3},{4,36},{36... | collective-permute-start | bytes 393224 | tf_op jit(solution)/shard_map/ppermute | solution.py:255
  91.4 10.1 %collective-permute-start.8 = (f32[160,128]{1,0:T(8,128)S(1)}, f32[160,128]{1,0:T(8,128)S(1)}, u32[]{:S(2)}, u32[]{:S(2)}) collective-permute-start(f32[160,128]{1,0:T(8,128)S(1)} %shard_map.70.field_ref.start_ref), channel_id=1, source_target_pairs={{0,32},{32,64},{64,96},{96,128},{128,160},{160,192},{192,224},{224... | collective-permute-start | bytes 245768 | tf_op jit(solution)/shard_map/ppermute | solution.py:223
  91.4 10.1 %collective-permute-start.9 = (f32[160,128]{1,0:T(8,128)S(1)}, f32[160,128]{1,0:T(8,128)S(1)}, u32[]{:S(2)}, u32[]{:S(2)}) collective-permute-start(f32[160,128]{1,0:T(8,128)S(1)} %shard_map.70.field_ref.start_ref), channel_id=1, source_target_pairs={{0,224},{32,0},{64,32},{96,64},{128,96},{160,128},{192,160},{224,1... | collective-permute-start | bytes 245768 | tf_op jit(solution)/shard_map/ppermute | solution.py:224
  94.3 8.3 %collective-permute-start.10 = (f32[160,128]{1,0:T(8,128)S(1)}, f32[160,128]{1,0:T(8,128)S(1)}, u32[]{:S(2)}, u32[]{:S(2)}) collective-permute-start(f32[160,128]{1,0:T(8,128)S(1)} %shard_map.70.field_ref.start_ref), channel_id=1, source_target_pairs={{0,256},{256,512},{512,768},{1,257},{257,513},{513,769},{2,258},{2... | collective-permute-start | bytes 245768 | tf_op jit(solution)/shard_map/ppermute | solution.py:225
  97.0 6.3 %collective-permute-start.11 = (f32[160,128]{1,0:T(8,128)S(1)}, f32[160,128]{1,0:T(8,128)S(1)}, u32[]{:S(2)}, u32[]{:S(2)}) collective-permute-start(f32[160,128]{1,0:T(8,128)S(1)} %shard_map.70.field_ref.start_ref), channel_id=1, source_target_pairs={{256,0},{512,256},{768,512},{257,1},{513,257},{769,513},{258,2},{5... | collective-permute-start | bytes 245768 | tf_op jit(solution)/shard_map/ppermute | solution.py:226
  103.8 8.8 %collective-permute-start.12 = (f32[160,128]{1,0:T(8,128)S(1)}, f32[160,128]{1,0:T(8,128)S(1)}, u32[]{:S(2)}, u32[]{:S(2)}) collective-permute-start(f32[160,128]{1,0:T(8,128)S(1)} %shard_map.72.field_ref.middle_ref), channel_id=1, source_target_pairs={{0,32},{32,64},{64,96},{96,128},{128,160},{160,192},{192,224},{224... | collective-permute-start | bytes 245768 | tf_op jit(solution)/shard_map/ppermute | solution.py:223
  103.9 8.8 %collective-permute-start.13 = (f32[160,128]{1,0:T(8,128)S(1)}, f32[160,128]{1,0:T(8,128)S(1)}, u32[]{:S(2)}, u32[]{:S(2)}) collective-permute-start(f32[160,128]{1,0:T(8,128)S(1)} %shard_map.72.field_ref.middle_ref), channel_id=1, source_target_pairs={{0,224},{32,0},{64,32},{96,64},{128,96},{160,128},{192,160},{224,1... | collective-permute-start | bytes 245768 | tf_op jit(solution)/shard_map/ppermute | solution.py:224
  106.8 7.0 %collective-permute-start.14 = (f32[160,128]{1,0:T(8,128)S(1)}, f32[160,128]{1,0:T(8,128)S(1)}, u32[]{:S(2)}, u32[]{:S(2)}) collective-permute-start(f32[160,128]{1,0:T(8,128)S(1)} %shard_map.72.field_ref.middle_ref), channel_id=1, source_target_pairs={{0,256},{256,512},{512,768},{1,257},{257,513},{513,769},{2,258},{2... | collective-permute-start | bytes 245768 | tf_op jit(solution)/shard_map/ppermute | solution.py:225
  109.3 6.3 %collective-permute-start.15 = (f32[160,128]{1,0:T(8,128)S(1)}, f32[160,128]{1,0:T(8,128)S(1)}, u32[]{:S(2)}, u32[]{:S(2)}) collective-permute-start(f32[160,128]{1,0:T(8,128)S(1)} %shard_map.72.field_ref.middle_ref), channel_id=1, source_target_pairs={{256,0},{512,256},{768,512},{257,1},{513,257},{769,513},{258,2},{5... | collective-permute-start | bytes 245768 | tf_op jit(solution)/shard_map/ppermute | solution.py:226

commit v9 on v3

--- a/solution.py
+++ b/solution.py
@@ -71,8 +71,7 @@
     return row < limit
 
 
-def cut_columns(orbitals_ref, rotation_ref, counts_ref, out_ref, slices_ref, live_ref):
-    live_ref[...] = jnp.where(alive(counts_ref), 1.0, 0.0)
+def cut_columns(orbitals_ref, rotation_ref, out_ref, slices_ref):
     for far in range(FAR):
         for half in range(2):
             slices_ref[far, pl.ds(32 * half, 32), :] = rotation_ref[:, pl.ds(256 * far + 128 * half, 128)]
@@ -141,10 +140,11 @@
     total = parts_ref[0]
     for near in range(1, NEAR):
         total = total + parts_ref[near]
-    out_ref[...] = jnp.where(live_ref[...] > 0.5, total, 0.0)
-
-
-def split_blocks(hamiltonian_ref, high_ref, low_ref):
+    out_ref[...] = jnp.where(live_ref[...].astype(F32) > 0.5, total, 0.0)
+
+
+def split_blocks(hamiltonian_ref, counts_ref, high_ref, low_ref, live_ref):
+    live_ref[...] = jnp.where(alive(counts_ref), 1.0, 0.0).astype(BF16)
     for e in range(ELEMS):
         for slot in range(7):
             high_ref[e, slot], low_ref[e, slot] = split(hamiltonian_ref[e, slot])
@@ -176,7 +176,7 @@
 
 def applied(own_ref, c_ref, d_ref, high_ref, low_ref, live_ref):
     total = own_ref[...] + blocks_times(high_ref, low_ref, (5, 6), (c_ref[...], d_ref[...]))
-    return jnp.where(live_ref[...] > 0.5, total, 0.0)
+    return jnp.where(live_ref[...].astype(F32) > 0.5, total, 0.0)
 
 
 def first_step(own_ref, c_ref, d_ref, high_ref, low_ref, start_ref, live_ref, center_ref, width_ref, out_ref):
@@ -211,15 +211,16 @@
 
 def shards(orbitals, rotation, counts, hamiltonian, center, width):
     pieces = jnp.transpose(orbitals, (1, 0, 2))
-    shapes = ((NEAR, ELEMS * PIECE, WIDE), (FAR, 64, WIDE), (ROWS, WIDE))
-    cut, slices, live = call(cut_columns, shapes, 0, 6 * FIELD, (V, V, S))(pieces, rotation, counts)
+    shapes = ((NEAR, ELEMS * PIECE, WIDE), (FAR, 64, WIDE))
+    cut, slices = call(cut_columns, shapes, 0, 5 * FIELD, (V, V))(pieces, rotation)
     cut = lax.all_to_all(cut, NEARS, split_axis=0, concat_axis=0, tiled=True)
     message = (2 * PASS + 32, WIDE)
     up, down = call(pack, (message, message), 0, 6 * FIELD, (V, V))(cut, slices)
     above, below = far_step(down, -1), far_step(up, 1)
+    shapes = (hamiltonian.shape, hamiltonian.shape, (ROWS, WIDE))
+    blocks = call(split_blocks, shapes, 0, 2 * BLOCKS, (V, S), (), BF16)(hamiltonian, counts)
+    below, *blocks, live = lax.optimization_barrier((below, *blocks))
     passed_up, passed_down = far_step(below[:PASS], 1), far_step(above[:PASS], -1)
-    blocks = call(split_blocks, (hamiltonian.shape,) * 2, 0, 2 * BLOCKS, (V,), (), BF16)(hamiltonian)
-    slices, *blocks = lax.optimization_barrier((slices, *blocks))
     scratch = [V((WIDE, WIDE), F32)] * 2
     parts = call(rotate, (NEAR, ROWS, WIDE), 6 * 640 * 128 * 256, 13 * FIELD, (V,) * 7, scratch)(
         up, down, slices, below, above, passed_up, passed_down

time: 116 us -> 116 us (level)
  transfers between devices with their start and end apart: 12 -> 12, of which waited for: 5 -> 5; matrix products, arithmetic and copies ran while one was open for 0% -> 0% of each run, Pallas kernels for 2% -> 3%
where the time goes in v9:
time: 116 us
  blocking collectives  46.7 us (40%)
  starting transfers between devices  43.1 us (37%)
  waiting for transfers between devices  13.2 us (11%)
  Pallas kernels  6.28 us (5%)
  local copies, waits for them, and re-layouts  4.75 us (4%)
  between operations  1.5 us (1%)
    ppermute x4, starting transfers between devices, far_step(): return lax.ppermute(v, 'z_hi', [(i, (i + by) % FAR) for i in range(FAR)])  25.5 us
    all_to_all x1, blocking collectives, shards(): lax.all_to_all(parts, NEARS, split_axis=0, concat_axis=0, tiled=True)  24.2 us
    all_to_all x1, blocking collectives, shards(): cut = lax.all_to_all(cut, NEARS, split_axis=0, concat_axis=0, tiled=True)  22.5 us
    ppermute x4, waiting for transfers between devices, far_step(): return lax.ppermute(v, 'z_hi', [(i, (i + by) % FAR) for i in range(FAR)])  10.6 us
    ppermute x2, starting transfers between devices, neighbours(): lax.ppermute(field, 'layer', [(i + 1, i) for i in range(LAYERS - 1)])  6.47 us
    ppermute x2, starting transfers between devices, neighbours(): lax.ppermute(field, RING, [(i, (i - 1) % ring) for i in range(ring)])  5.89 us
    ppermute x2, starting transfers between devices, neighbours(): lax.ppermute(field, 'layer', [(i, i + 1) for i in range(LAYERS - 1)])  5.19 us
    unnamed x8, local copies, waits for them, and re-layouts  4.74 us
  transfers between devices with their start and end apart: 12, of which 5 were waited for; matrix products, arithmetic and copies ran while one was open for 0% of the time, Pallas kernels for 3%

profile of v9, /device:TPU:8, one launch (start us, length us, event | category | flops | bytes accessed | tf_op | source)
XLA Modules:
  0.0 115.6 jit_solution(10038313104208654835)
XLA Ops:
  0.0 0.0 copy-start.1
  0.0 0.9 copy-done.1
  0.9 0.0 copy-start.2
  0.9 0.9 copy-done.2
  1.8 0.2 shard_map.64
  2.0 22.5 %all_to_all.10.rows_ref = f32[8,20,128]{2,1,0:T(8,128)S(1)} all-to-all(f32[8,20,128]{2,1,0:T(8,128)S(1)} %get-tuple-element.16), channel_id=1, replica_groups=mesh['layer'=4,'column'=4,'core'=2,'z_hi'=4,'z_lo'=4,'y_hi'=2] {'z_lo','..., dimensions={0} | all-to-all | bytes 163840 | tf_op jit(solution)/shard_map/all_to_all | solution.py:216
  24.4 0.1 shard_map.65
  24.5 10.9 %collective-permute-start = (f32[256,128]{1,0:T(8,128)S(1)}, f32[256,128]{1,0:T(8,128)S(1)}, u32[]{:S(2)}, u32[]{:S(2)}) collective-permute-start(f32[256,128]{1,0:T(8,128)S(1)} %get-tuple-element.18.up_ref), channel_id=1, source_target_pairs={{0,8},{8,16},{16,24},{24,0},{1,9},{9,17},{17,25},{25,1},{2,10},{10... | collective-permute-start | bytes 393224 | tf_op jit(solution)/shard_map/ppermute | solution.py:204
  35.5 6.5 %collective-permute-start.1 = (f32[256,128]{1,0:T(8,128)S(1)}, f32[256,128]{1,0:T(8,128)S(1)}, u32[]{:S(2)}, u32[]{:S(2)}) collective-permute-start(f32[256,128]{1,0:T(8,128)S(1)} %get-tuple-element.19.down_ref), channel_id=1, source_target_pairs={{0,24},{8,0},{16,8},{24,16},{1,25},{9,1},{17,9},{25,17},{2,26},{10... | collective-permute-start | bytes 393224 | tf_op jit(solution)/shard_map/ppermute | solution.py:204
  42.0 0.0 copy-start
  42.0 2.3 %copy-done = f32[4,7,160,160]{3,2,1,0:T(8,128)S(1)} copy-done((f32[4,7,160,160]{3,2,1,0:T(8,128)S(1)}, f32[4,7,160,160]{3,2,1,0:T(8,128)}, u32[]{:S(2)}) %copy-start) | copy-done | bytes 2867224
  44.3 0.0 copy-start.3
  44.3 0.7 copy-done.3
  44.9 1.2 %shard_map.66 = (bf16[4,7,160,160]{3,2,1,0:T(8,128)(2,1)S(1)}, bf16[4,7,160,160]{3,2,1,0:T(8,128)(2,1)S(1)}, bf16[160,128]{1,0:T(8,128)(2,1)S(1)}) custom-call(f32[4,7,160,160]{3,2,1,0:T(8,128)S(1)} %copy-done, s32[4]{0:T(128)S(1)} %copy-done.3), custom_call_target="tpu_custom_call" | custom-call | bytes 9175040 | tf_op jit(solution)/shard_map/pallas_call | solution.py:221
  46.1 3.4 %collective-permute-done.below_ref = f32[256,128]{1,0:T(8,128)S(1)} collective-permute-done((f32[256,128]{1,0:T(8,128)S(1)}, f32[256,128]{1,0:T(8,128)S(1)}, u32[]{:S(2)}, u32[]{:S(2)}) %collective-permute-start) | collective-permute-done | bytes 131104 | tf_op jit(solution)/shard_map/ppermute | solution.py:204
  49.5 1.9 %collective-permute-start.2 = (f32[112,128]{1,0:T(8,128)S(1)}, f32[112,128]{1,0:T(8,128)S(1)}, u32[]{:S(2)}, u32[]{:S(2)}) collective-permute-start(f32[112,128]{1,0:T(8,128)S(1)} %slice.6), channel_id=1, source_target_pairs={{0,8},{8,16},{16,24},{24,0},{1,9},{9,17},{17,25},{25,1},{2,10},{10... | collective-permute-start | bytes 172040 | tf_op jit(solution)/shard_map/ppermute | solution.py:204
  51.4 2.0 %collective-permute-done.1.above_ref = f32[256,128]{1,0:T(8,128)S(1)} collective-permute-done((f32[256,128]{1,0:T(8,128)S(1)}, f32[256,128]{1,0:T(8,128)S(1)}, u32[]{:S(2)}, u32[]{:S(2)}) %collective-permute-start.1) | collective-permute-done | bytes 131104 | tf_op jit(solution)/shard_map/ppermute | solution.py:204
  53.4 6.2 %collective-permute-start.3 = (f32[112,128]{1,0:T(8,128)S(1)}, f32[112,128]{1,0:T(8,128)S(1)}, u32[]{:S(2)}, u32[]{:S(2)}) collective-permute-start(f32[112,128]{1,0:T(8,128)S(1)} %slice.8), channel_id=1, source_target_pairs={{0,24},{8,0},{16,8},{24,16},{1,25},{9,1},{17,9},{25,17},{2,26},{10... | collective-permute-start | bytes 172040 | tf_op jit(solution)/shard_map/ppermute | solution.py:204
  59.6 0.0 collective-permute-done.2.passed_up_ref
  59.6 5.3 %collective-permute-done.3.passed_down_ref = f32[112,128]{1,0:T(8,128)S(1)} collective-permute-done((f32[112,128]{1,0:T(8,128)S(1)}, f32[112,128]{1,0:T(8,128)S(1)}, u32[]{:S(2)}, u32[]{:S(2)}) %collective-permute-start.3) | collective-permute-done | bytes 57376 | tf_op jit(solution)/shard_map/ppermute | solution.py:204
  64.8 0.8 shard_map.67
  65.7 24.2 %all_to_all.11.parts_ref = f32[8,160,128]{2,1,0:T(8,128)S(1)} all-to-all(f32[8,160,128]{2,1,0:T(8,128)S(1)} %shard_map.67), channel_id=1, replica_groups=mesh['layer'=4,'column'=4,'core'=2,'z_hi'=4,'z_lo'=4,'y_hi'=2] {'z_lo','..., dimensions={0} | all-to-all | bytes 1310720 | tf_op jit(solution)/shard_map/all_to_all | solution.py:228
  90.0 0.0 collective-permute-start.4
  90.0 2.9 %collective-permute-start.5 = (f32[160,128]{1,0:T(8,128)S(1)}, f32[160,128]{1,0:T(8,128)S(1)}, u32[]{:S(2)}, u32[]{:S(2)}) collective-permute-start(f32[160,128]{1,0:T(8,128)S(1)} %shard_map.68.field_ref.start_ref), channel_id=1, source_target_pairs={{0,224},{32,0},{64,32},{96,64},{128,96},{160,128},{192,160},{224,1... | collective-permute-start | bytes 245768 | tf_op jit(solution)/shard_map/ppermute | solution.py:197
  92.9 2.1 %collective-permute-start.6 = (f32[160,128]{1,0:T(8,128)S(1)}, f32[160,128]{1,0:T(8,128)S(1)}, u32[]{:S(2)}, u32[]{:S(2)}) collective-permute-start(f32[160,128]{1,0:T(8,128)S(1)} %shard_map.68.field_ref.start_ref), channel_id=1, source_target_pairs={{0,256},{256,512},{512,768},{1,257},{257,513},{513,769},{2,258},{2... | collective-permute-start | bytes 245768 | tf_op jit(solution)/shard_map/ppermute | solution.py:198
  95.0 3.8 %collective-permute-start.7 = (f32[160,128]{1,0:T(8,128)S(1)}, f32[160,128]{1,0:T(8,128)S(1)}, u32[]{:S(2)}, u32[]{:S(2)}) collective-permute-start(f32[160,128]{1,0:T(8,128)S(1)} %shard_map.68.field_ref.start_ref), channel_id=1, source_target_pairs={{256,0},{512,256},{768,512},{257,1},{513,257},{769,513},{258,2},{5... | collective-permute-start | bytes 245768 | tf_op jit(solution)/shard_map/ppermute | solution.py:199
  100.1 0.0 collective-permute-done.4.a_ref
  100.1 0.0 collective-permute-done.5.b_ref
  100.1 1.1 shard_map.69.own_ref
  101.2 0.0 collective-permute-done.6.c_ref
  101.2 0.1 collective-permute-done.7.d_ref
  101.3 0.5 shard_map.70.field_ref.middle_ref
  101.8 0.0 collective-permute-start.8
  101.9 2.9 %collective-permute-start.9 = (f32[160,128]{1,0:T(8,128)S(1)}, f32[160,128]{1,0:T(8,128)S(1)}, u32[]{:S(2)}, u32[]{:S(2)}) collective-permute-start(f32[160,128]{1,0:T(8,128)S(1)} %shard_map.70.field_ref.middle_ref), channel_id=1, source_target_pairs={{0,224},{32,0},{64,32},{96,64},{128,96},{160,128},{192,160},{224,1... | collective-permute-start | bytes 245768 | tf_op jit(solution)/shard_map/ppermute | solution.py:197
  104.8 3.1 %collective-permute-start.10 = (f32[160,128]{1,0:T(8,128)S(1)}, f32[160,128]{1,0:T(8,128)S(1)}, u32[]{:S(2)}, u32[]{:S(2)}) collective-permute-start(f32[160,128]{1,0:T(8,128)S(1)} %shard_map.70.field_ref.middle_ref), channel_id=1, source_target_pairs={{0,256},{256,512},{512,768},{1,257},{257,513},{513,769},{2,258},{2... | collective-permute-start | bytes 245768 | tf_op jit(solution)/shard_map/ppermute | solution.py:198
  108.0 2.7 %collective-permute-start.11 = (f32[160,128]{1,0:T(8,128)S(1)}, f32[160,128]{1,0:T(8,128)S(1)}, u32[]{:S(2)}, u32[]{:S(2)}) collective-permute-start(f32[160,128]{1,0:T(8,128)S(1)} %shard_map.70.field_ref.middle_ref), channel_id=1, source_target_pairs={{256,0},{512,256},{768,512},{257,1},{513,257},{769,513},{258,2},{5... | collective-permute-start | bytes 245768 | tf_op jit(solution)/shard_map/ppermute | solution.py:199
  110.7 0.0 collective-permute-done.8.a_ref
  110.7 0.0 collective-permute-done.9.b_ref
  110.7 1.1 shard_map.71.own_ref
  111.8 0.0 collective-permute-done.10.c_ref
  111.8 2.5 %collective-permute-done.11.d_ref = f32[160,128]{1,0:T(8,128)S(1)} collective-permute-done((f32[160,128]{1,0:T(8,128)S(1)}, f32[160,128]{1,0:T(8,128)S(1)}, u32[]{:S(2)}, u32[]{:S(2)}) %collective-permute-start.11) | collective-permute-done | bytes 81952 | tf_op jit(solution)/shard_map/ppermute | solution.py:199
  114.3 1.3 %shard_map.72 = f32[128,160]{1,0:T(8,128)} custom-call(f32[160,128]{1,0:T(8,128)S(1)} %shard_map.71.own_ref, f32[160,128]{1,0:T(8,128)S(1)} %collective-permute-done.10.c_ref, f32[160,128]{1,0:T(8,128)S(1)} %collective-permute-done.11.d_ref, bf16[4,7,160,160]{3,2,1,0:T(8,128)(2,1)S(1)} %get-tuple-element.25.high_ref, ...), custom_call_target="tpu_custom_call" | custom-call | flops 157286400 | bytes 1529173 | tf_op jit(solution)/shard_map/pallas_call | solution.py:239
  (3 shorter events, 0.0 us)
Async XLA Ops:
  0.0 0.9 copy-start.1
  0.9 0.9 copy-start.2
  24.5 24.9 %collective-permute-start = (f32[256,128]{1,0:T(8,128)S(1)}, f32[256,128]{1,0:T(8,128)S(1)}, u32[]{:S(2)}, u32[]{:S(2)}) collective-permute-start(f32[256,128]{1,0:T(8,128)S(1)} %get-tuple-element.18.up_ref), channel_id=1, source_target_pairs={{0,8},{8,16},{16,24},{24,0},{1,9},{9,17},{17,25},{25,1},{2,10},{10... | collective-permute-start | bytes 393224 | tf_op jit(solution)/shard_map/ppermute | solution.py:204
  35.5 17.9 %collective-permute-start.1 = (f32[256,128]{1,0:T(8,128)S(1)}, f32[256,128]{1,0:T(8,128)S(1)}, u32[]{:S(2)}, u32[]{:S(2)}) collective-permute-start(f32[256,128]{1,0:T(8,128)S(1)} %get-tuple-element.19.down_ref), channel_id=1, source_target_pairs={{0,24},{8,0},{16,8},{24,16},{1,25},{9,1},{17,9},{25,17},{2,26},{10... | collective-permute-start | bytes 393224 | tf_op jit(solution)/shard_map/ppermute | solution.py:204
  42.0 2.3 %copy-start = (f32[4,7,160,160]{3,2,1,0:T(8,128)S(1)}, f32[4,7,160,160]{3,2,1,0:T(8,128)}, u32[]{:S(2)}) copy-start(f32[4,7,160,160]{3,2,1,0:T(8,128)} %hamiltonian_ref.1) | copy-start | bytes 8601604
  44.3 0.7 copy-start.3
  49.5 10.1 %collective-permute-start.2 = (f32[112,128]{1,0:T(8,128)S(1)}, f32[112,128]{1,0:T(8,128)S(1)}, u32[]{:S(2)}, u32[]{:S(2)}) collective-permute-start(f32[112,128]{1,0:T(8,128)S(1)} %slice.6), channel_id=1, source_target_pairs={{0,8},{8,16},{16,24},{24,0},{1,9},{9,17},{17,25},{25,1},{2,10},{10... | collective-permute-start | bytes 172040 | tf_op jit(solution)/shard_map/ppermute | solution.py:204
  53.4 11.5 %collective-permute-start.3 = (f32[112,128]{1,0:T(8,128)S(1)}, f32[112,128]{1,0:T(8,128)S(1)}, u32[]{:S(2)}, u32[]{:S(2)}) collective-permute-start(f32[112,128]{1,0:T(8,128)S(1)} %slice.8), channel_id=1, source_target_pairs={{0,24},{8,0},{16,8},{24,16},{1,25},{9,1},{17,9},{25,17},{2,26},{10... | collective-permute-start | bytes 172040 | tf_op jit(solution)/shard_map/ppermute | solution.py:204
  90.0 10.1 %collective-permute-start.4 = (f32[160,128]{1,0:T(8,128)S(1)}, f32[160,128]{1,0:T(8,128)S(1)}, u32[]{:S(2)}, u32[]{:S(2)}) collective-permute-start(f32[160,128]{1,0:T(8,128)S(1)} %shard_map.68.field_ref.start_ref), channel_id=1, source_target_pairs={{0,32},{32,64},{64,96},{96,128},{128,160},{160,192},{192,224},{224... | collective-permute-start | bytes 245768 | tf_op jit(solution)/shard_map/ppermute | solution.py:196
  90.0 10.1 %collective-permute-start.5 = (f32[160,128]{1,0:T(8,128)S(1)}, f32[160,128]{1,0:T(8,128)S(1)}, u32[]{:S(2)}, u32[]{:S(2)}) collective-permute-start(f32[160,128]{1,0:T(8,128)S(1)} %shard_map.68.field_ref.start_ref), channel_id=1, source_target_pairs={{0,224},{32,0},{64,32},{96,64},{128,96},{160,128},{192,160},{224,1... | collective-permute-start | bytes 245768 | tf_op jit(solution)/shard_map/ppermute | solution.py:197
  92.9 8.3 %collective-permute-start.6 = (f32[160,128]{1,0:T(8,128)S(1)}, f32[160,128]{1,0:T(8,128)S(1)}, u32[]{:S(2)}, u32[]{:S(2)}) collective-permute-start(f32[160,128]{1,0:T(8,128)S(1)} %shard_map.68.field_ref.start_ref), channel_id=1, source_target_pairs={{0,256},{256,512},{512,768},{1,257},{257,513},{513,769},{2,258},{2... | collective-permute-start | bytes 245768 | tf_op jit(solution)/shard_map/ppermute | solution.py:198
  95.0 6.3 %collective-permute-start.7 = (f32[160,128]{1,0:T(8,128)S(1)}, f32[160,128]{1,0:T(8,128)S(1)}, u32[]{:S(2)}, u32[]{:S(2)}) collective-permute-start(f32[160,128]{1,0:T(8,128)S(1)} %shard_map.68.field_ref.start_ref), channel_id=1, source_target_pairs={{256,0},{512,256},{768,512},{257,1},{513,257},{769,513},{258,2},{5... | collective-permute-start | bytes 245768 | tf_op jit(solution)/shard_map/ppermute | solution.py:199
  101.8 8.8 %collective-permute-start.8 = (f32[160,128]{1,0:T(8,128)S(1)}, f32[160,128]{1,0:T(8,128)S(1)}, u32[]{:S(2)}, u32[]{:S(2)}) collective-permute-start(f32[160,128]{1,0:T(8,128)S(1)} %shard_map.70.field_ref.middle_ref), channel_id=1, source_target_pairs={{0,32},{32,64},{64,96},{96,128},{128,160},{160,192},{192,224},{224... | collective-permute-start | bytes 245768 | tf_op jit(solution)/shard_map/ppermute | solution.py:196
  101.9 8.8 %collective-permute-start.9 = (f32[160,128]{1,0:T(8,128)S(1)}, f32[160,128]{1,0:T(8,128)S(1)}, u32[]{:S(2)}, u32[]{:S(2)}) collective-permute-start(f32[160,128]{1,0:T(8,128)S(1)} %shard_map.70.field_ref.middle_ref), channel_id=1, source_target_pairs={{0,224},{32,0},{64,32},{96,64},{128,96},{160,128},{192,160},{224,1... | collective-permute-start | bytes 245768 | tf_op jit(solution)/shard_map/ppermute | solution.py:197
  104.8 7.0 %collective-permute-start.10 = (f32[160,128]{1,0:T(8,128)S(1)}, f32[160,128]{1,0:T(8,128)S(1)}, u32[]{:S(2)}, u32[]{:S(2)}) collective-permute-start(f32[160,128]{1,0:T(8,128)S(1)} %shard_map.70.field_ref.middle_ref), channel_id=1, source_target_pairs={{0,256},{256,512},{512,768},{1,257},{257,513},{513,769},{2,258},{2... | collective-permute-start | bytes 245768 | tf_op jit(solution)/shard_map/ppermute | solution.py:198
  108.0 6.3 %collective-permute-start.11 = (f32[160,128]{1,0:T(8,128)S(1)}, f32[160,128]{1,0:T(8,128)S(1)}, u32[]{:S(2)}, u32[]{:S(2)}) collective-permute-start(f32[160,128]{1,0:T(8,128)S(1)} %shard_map.70.field_ref.middle_ref), channel_id=1, source_target_pairs={{256,0},{512,256},{768,512},{257,1},{513,257},{769,513},{258,2},{5... | collective-permute-start | bytes 245768 | tf_op jit(solution)/shard_map/ppermute | solution.py:199

commit v10 on v6

--- a/solution.py
+++ b/solution.py
@@ -196,7 +196,8 @@
 
 
 def applied(own_ref, c_ref, d_ref, high_ref, low_ref, live_ref):
-    total = own_ref[...] + blocks_times(high_ref, low_ref, (5, 6), (c_ref[...], d_ref[...]))
+    odd = lax.rem(lax.axis_index("layer"), 2)
+    total = own_ref[...] + blocks_times(high_ref, low_ref, (6 - odd, 5 + odd), (c_ref[...], d_ref[...]))
     return jnp.where(live_ref[...].astype(F32) > 0.5, total, 0.0)
 
 
@@ -216,8 +217,8 @@
     return (
         lax.ppermute(field, RING, [(i, (i + 1) % ring) for i in range(ring)]),
         lax.ppermute(field, RING, [(i, (i - 1) % ring) for i in range(ring)]),
-        lax.ppermute(field, "layer", [(i, i + 1) for i in range(LAYERS - 1)]),
-        lax.ppermute(field, "layer", [(i + 1, i) for i in range(LAYERS - 1)]),
+        lax.ppermute(field, "layer", [(i, i ^ 1) for i in range(LAYERS)]),
+        lax.ppermute(field, "layer", [(i, LAYERS - 1 - i) for i in range(1, LAYERS - 1)]),
     )
 
 

time: 114 us -> 114 us (level)
  waiting for transfers between devices: 12.1 us -> 14.3 us
  starting transfers between devices: 64.3 us -> 62.1 us
    ppermute x4, starting transfers between devices: 11.7 us -> 9.38 us  [the longest x2 5.47 us: neighbours(): lax.ppermute(field, 'layer', [(i, i ^ 1) for i in range(LAYERS)])]
    ppermute x4, waiting for transfers between devices: 2.93 us -> 5.18 us  [the longest x2 3.87 us: neighbours(): lax.ppermute(field, 'layer', [(i, LAYERS - 1 - i) for i in range(1, LAYER...]
  transfers between devices with their start and end apart: 15 -> 15, of which waited for: 5 -> 6; matrix products, arithmetic and copies ran while one was open for 0% -> 0% of each run, Pallas kernels for 3% -> 3%
where the time goes in v10:
time: 114 us; the launch traced here: 113 us
  starting transfers between devices  62.1 us (54%)
  blocking collectives  24.1 us (21%)
  waiting for transfers between devices  14.3 us (13%)
  Pallas kernels  6.63 us (6%)
  local copies, waits for them, and re-layouts  4.75 us (4%)
  between operations  1.54 us (1%)
    ppermute x4, starting transfers between devices, far_step(): return lax.ppermute(v, 'z_hi', [(i, (i + by) % FAR) for i in range(FAR)])  30.8 us
    all_to_all x1, blocking collectives, shards(): lax.all_to_all(parts, NEARS, split_axis=0, concat_axis=0, tiled=True)  24.1 us
    all_to_all x1, starting transfers between devices, shards(): cut = lax.all_to_all(cut, 'z_lo', split_axis=0, concat_axis=0, tiled=True)  7.26 us
    ppermute x1, starting transfers between devices, shards(): other = lax.ppermute(mine, 'y_hi', [(0, 1), (1, 0)])  6.83 us
    ppermute x2, starting transfers between devices, neighbours(): lax.ppermute(field, RING, [(i, (i - 1) % ring) for i in range(ring)])  5.89 us
    ppermute x2, starting transfers between devices, neighbours(): lax.ppermute(field, 'layer', [(i, i ^ 1) for i in range(LAYERS)])  5.47 us
    unnamed x8, local copies, waits for them, and re-layouts  4.74 us
    ppermute x4, waiting for transfers between devices, far_step(): return lax.ppermute(v, 'z_hi', [(i, (i + by) % FAR) for i in range(FAR)])  4.5 us
  transfers between devices with their start and end apart: 15, of which 6 were waited for; matrix products, arithmetic and copies ran while one was open for 0% of the time, Pallas kernels for 3%

profile of v10, /device:TPU:8, one launch (start us, length us, event | category | flops | bytes accessed | tf_op | source)
XLA Modules:
  0.0 113.4 jit_solution(6291892323078476273)
XLA Ops:
  0.0 0.0 copy-start.2
  0.0 0.9 copy-done.2
  0.9 0.7 shard_map.64
  1.6 7.3 %all-to-all-start = ((f32[4,40,128]{2,1,0:T(8,128)}), f32[4,40,128]{2,1,0:T(8,128)S(1)}, u32[]{:S(2)}, u32[]{:S(2)}) async-start(f32[4,40,128]{2,1,0:T(8,128)} %shard_map.64), calls=%async_computation | async-start | bytes 163840 | tf_op jit(solution)/shard_map/all_to_all | solution.py:239
  8.9 0.0 copy-start.1
  8.9 0.9 copy-done.1
  9.8 6.8 %collective-permute-start = (f32[4,32,128]{2,1,0:T(8,128)S(1)}, f32[4,32,128]{2,1,0:T(8,128)S(1)}, u32[]{:S(2)}, u32[]{:S(2)}) collective-permute-start(f32[4,32,128]{2,1,0:T(8,128)S(1)} %shard_map.65.mine_ref), channel_id=1, source_target_pairs={{0,1},{1,0},{2,3},{3,2},{4,5},{5,4},{6,7},{7,6},{8,9},{9,8},{10,11... | collective-permute-start | bytes 196616 | tf_op jit(solution)/shard_map/ppermute | solution.py:237
  16.6 3.3 %collective-permute-done.other_ref = f32[4,32,128]{2,1,0:T(8,128)S(1)} collective-permute-done((f32[4,32,128]{2,1,0:T(8,128)S(1)}, f32[4,32,128]{2,1,0:T(8,128)S(1)}, u32[]{:S(2)}, u32[]{:S(2)}) %collective-permute-start) | collective-permute-done | bytes 65568 | tf_op jit(solution)/shard_map/ppermute | solution.py:237
  20.0 0.0 all-to-all-done.rows_ref
  20.0 0.1 shard_map.66
  20.1 10.9 %collective-permute-start.1 = (f32[256,128]{1,0:T(8,128)S(1)}, f32[256,128]{1,0:T(8,128)S(1)}, u32[]{:S(2)}, u32[]{:S(2)}) collective-permute-start(f32[256,128]{1,0:T(8,128)S(1)} %get-tuple-element.15.up_ref), channel_id=1, source_target_pairs={{0,8},{8,16},{16,24},{24,0},{1,9},{9,17},{17,25},{25,1},{2,10},{10... | collective-permute-start | bytes 393224 | tf_op jit(solution)/shard_map/ppermute | solution.py:226
  31.0 6.5 %collective-permute-start.2 = (f32[256,128]{1,0:T(8,128)S(1)}, f32[256,128]{1,0:T(8,128)S(1)}, u32[]{:S(2)}, u32[]{:S(2)}) collective-permute-start(f32[256,128]{1,0:T(8,128)S(1)} %get-tuple-element.16.down_ref), channel_id=1, source_target_pairs={{0,24},{8,0},{16,8},{24,16},{1,25},{9,1},{17,9},{25,17},{2,26},{10... | collective-permute-start | bytes 393224 | tf_op jit(solution)/shard_map/ppermute | solution.py:226
  37.5 0.0 copy-start
  37.5 2.3 %copy-done = f32[4,7,160,160]{3,2,1,0:T(8,128)S(1)} copy-done((f32[4,7,160,160]{3,2,1,0:T(8,128)S(1)}, f32[4,7,160,160]{3,2,1,0:T(8,128)}, u32[]{:S(2)}) %copy-start) | copy-done | bytes 2867224
  39.8 0.0 copy-start.3
  39.8 0.7 copy-done.3
  40.5 1.2 %shard_map.67 = (bf16[4,7,160,160]{3,2,1,0:T(8,128)(2,1)S(1)}, bf16[4,7,160,160]{3,2,1,0:T(8,128)(2,1)S(1)}, bf16[160,128]{1,0:T(8,128)(2,1)S(1)}) custom-call(f32[4,7,160,160]{3,2,1,0:T(8,128)S(1)} %copy-done, s32[4]{0:T(128)S(1)} %copy-done.3), custom_call_target="tpu_custom_call" | custom-call | bytes 9175040 | tf_op jit(solution)/shard_map/pallas_call | solution.py:244
  41.7 0.0 collective-permute-done.1.below_ref
  41.7 7.2 %collective-permute-start.3 = (f32[112,128]{1,0:T(8,128)S(1)}, f32[112,128]{1,0:T(8,128)S(1)}, u32[]{:S(2)}, u32[]{:S(2)}) collective-permute-start(f32[112,128]{1,0:T(8,128)S(1)} %slice.6), channel_id=1, source_target_pairs={{0,8},{8,16},{16,24},{24,0},{1,9},{9,17},{17,25},{25,1},{2,10},{10... | collective-permute-start | bytes 172040 | tf_op jit(solution)/shard_map/ppermute | solution.py:226
  48.9 0.0 collective-permute-done.2.above_ref
  48.9 6.2 %collective-permute-start.4 = (f32[112,128]{1,0:T(8,128)S(1)}, f32[112,128]{1,0:T(8,128)S(1)}, u32[]{:S(2)}, u32[]{:S(2)}) collective-permute-start(f32[112,128]{1,0:T(8,128)S(1)} %slice.8), channel_id=1, source_target_pairs={{0,24},{8,0},{16,8},{24,16},{1,25},{9,1},{17,9},{25,17},{2,26},{10... | collective-permute-start | bytes 172040 | tf_op jit(solution)/shard_map/ppermute | solution.py:226
  55.1 0.0 collective-permute-done.3.passed_up_ref
  55.1 4.5 %collective-permute-done.4.passed_down_ref = f32[112,128]{1,0:T(8,128)S(1)} collective-permute-done((f32[112,128]{1,0:T(8,128)S(1)}, f32[112,128]{1,0:T(8,128)S(1)}, u32[]{:S(2)}, u32[]{:S(2)}) %collective-permute-start.4) | collective-permute-done | bytes 57376 | tf_op jit(solution)/shard_map/ppermute | solution.py:226
  59.6 1.9 %collective-permute-start.5 = (f32[256,128]{1,0:T(8,128)S(1)}, f32[256,128]{1,0:T(8,128)S(1)}, u32[]{:S(2)}, u32[]{:S(2)}) collective-permute-start(f32[256,128]{1,0:T(8,128)S(1)} %shard_map.68.mine_ref), channel_id=1, source_target_pairs={{0,32},{32,0},{1,33},{33,1},{2,34},{34,2},{3,35},{35,3},{4,36},{36... | collective-permute-start | bytes 393224 | tf_op jit(solution)/shard_map/ppermute | solution.py:248
  61.5 1.3 %collective-permute-done.5.other_ref = f32[256,128]{1,0:T(8,128)S(1)} collective-permute-done((f32[256,128]{1,0:T(8,128)S(1)}, f32[256,128]{1,0:T(8,128)S(1)}, u32[]{:S(2)}, u32[]{:S(2)}) %collective-permute-start.5) | collective-permute-done | bytes 131104 | tf_op jit(solution)/shard_map/ppermute | solution.py:248
  62.8 0.6 shard_map.69
  63.4 24.1 %all_to_all.10.parts_ref = f32[8,80,128]{2,1,0:T(8,128)S(1)} all-to-all(f32[8,80,128]{2,1,0:T(8,128)S(1)} %shard_map.69), channel_id=1, replica_groups=mesh['layer'=4,'column'=4,'core'=2,'z_hi'=4,'z_lo'=4,'y_hi'=2] {'z_lo','..., dimensions={0} | all-to-all | bytes 655360 | tf_op jit(solution)/shard_map/all_to_all | solution.py:253
  87.5 0.1 shard_map.70.field_ref.start_ref
  87.5 0.0 collective-permute-start.6
  87.6 2.9 %collective-permute-start.7 = (f32[160,128]{1,0:T(8,128)S(1)}, f32[160,128]{1,0:T(8,128)S(1)}, u32[]{:S(2)}, u32[]{:S(2)}) collective-permute-start(f32[160,128]{1,0:T(8,128)S(1)} %shard_map.70.field_ref.start_ref), channel_id=1, source_target_pairs={{0,224},{32,0},{64,32},{96,64},{128,96},{160,128},{192,160},{224,1... | collective-permute-start | bytes 245768 | tf_op jit(solution)/shard_map/ppermute | solution.py:219
  90.5 3.6 %collective-permute-start.8 = (f32[160,128]{1,0:T(8,128)S(1)}, f32[160,128]{1,0:T(8,128)S(1)}, u32[]{:S(2)}, u32[]{:S(2)}) collective-permute-start(f32[160,128]{1,0:T(8,128)S(1)} %shard_map.70.field_ref.start_ref), channel_id=1, source_target_pairs={{0,256},{256,0},{512,768},{768,512},{1,257},{257,1},{513,769},{769... | collective-permute-start | bytes 245768 | tf_op jit(solution)/shard_map/ppermute | solution.py:220
  94.1 2.0 %collective-permute-start.9 = (f32[160,128]{1,0:T(8,128)S(1)}, f32[160,128]{1,0:T(8,128)S(1)}, u32[]{:S(2)}, u32[]{:S(2)}) collective-permute-start(f32[160,128]{1,0:T(8,128)S(1)} %shard_map.70.field_ref.start_ref), channel_id=1, source_target_pairs={{256,512},{512,256},{257,513},{513,257},{258,514},{514,258},{259,5... | collective-permute-start | bytes 245768 | tf_op jit(solution)/shard_map/ppermute | solution.py:221
  97.3 0.0 collective-permute-done.6.a_ref
  97.3 0.0 collective-permute-done.7.b_ref
  97.4 1.1 shard_map.71.own_ref
  98.5 0.0 collective-permute-done.8.c_ref
  98.5 1.9 %collective-permute-done.9.d_ref = f32[160,128]{1,0:T(8,128)S(1)} collective-permute-done((f32[160,128]{1,0:T(8,128)S(1)}, f32[160,128]{1,0:T(8,128)S(1)}, u32[]{:S(2)}, u32[]{:S(2)}) %collective-permute-start.9) | collective-permute-done | bytes 81952 | tf_op jit(solution)/shard_map/ppermute | solution.py:221
  100.4 0.5 shard_map.72.field_ref.middle_ref
  100.9 0.0 collective-permute-start.10
  101.0 2.9 %collective-permute-start.11 = (f32[160,128]{1,0:T(8,128)S(1)}, f32[160,128]{1,0:T(8,128)S(1)}, u32[]{:S(2)}, u32[]{:S(2)}) collective-permute-start(f32[160,128]{1,0:T(8,128)S(1)} %shard_map.72.field_ref.middle_ref), channel_id=1, source_target_pairs={{0,224},{32,0},{64,32},{96,64},{128,96},{160,128},{192,160},{224,1... | collective-permute-start | bytes 245768 | tf_op jit(solution)/shard_map/ppermute | solution.py:219
  103.9 1.9 %collective-permute-start.12 = (f32[160,128]{1,0:T(8,128)S(1)}, f32[160,128]{1,0:T(8,128)S(1)}, u32[]{:S(2)}, u32[]{:S(2)}) collective-permute-start(f32[160,128]{1,0:T(8,128)S(1)} %shard_map.72.field_ref.middle_ref), channel_id=1, source_target_pairs={{0,256},{256,0},{512,768},{768,512},{1,257},{257,1},{513,769},{769... | collective-permute-start | bytes 245768 | tf_op jit(solution)/shard_map/ppermute | solution.py:220
  105.8 2.0 %collective-permute-start.13 = (f32[160,128]{1,0:T(8,128)S(1)}, f32[160,128]{1,0:T(8,128)S(1)}, u32[]{:S(2)}, u32[]{:S(2)}) collective-permute-start(f32[160,128]{1,0:T(8,128)S(1)} %shard_map.72.field_ref.middle_ref), channel_id=1, source_target_pairs={{256,512},{512,256},{257,513},{513,257},{258,514},{514,258},{259,5... | collective-permute-start | bytes 245768 | tf_op jit(solution)/shard_map/ppermute | solution.py:221
  107.8 0.0 collective-permute-done.10.a_ref
  107.8 0.0 collective-permute-done.11.b_ref
  107.8 1.1 shard_map.73.own_ref
  108.9 1.3 %collective-permute-done.12.c_ref = f32[160,128]{1,0:T(8,128)S(1)} collective-permute-done((f32[160,128]{1,0:T(8,128)S(1)}, f32[160,128]{1,0:T(8,128)S(1)}, u32[]{:S(2)}, u32[]{:S(2)}) %collective-permute-start.12) | collective-permute-done | bytes 81952 | tf_op jit(solution)/shard_map/ppermute | solution.py:220
  110.2 1.9 %collective-permute-done.13.d_ref = f32[160,128]{1,0:T(8,128)S(1)} collective-permute-done((f32[160,128]{1,0:T(8,128)S(1)}, f32[160,128]{1,0:T(8,128)S(1)}, u32[]{:S(2)}, u32[]{:S(2)}) %collective-permute-start.13) | collective-permute-done | bytes 81952 | tf_op jit(solution)/shard_map/ppermute | solution.py:221
  112.2 1.3 %shard_map.74 = f32[128,160]{1,0:T(8,128)} custom-call(f32[160,128]{1,0:T(8,128)S(1)} %shard_map.73.own_ref, f32[160,128]{1,0:T(8,128)S(1)} %collective-permute-done.12.c_ref, f32[160,128]{1,0:T(8,128)S(1)} %collective-permute-done.13.d_ref, bf16[4,7,160,160]{3,2,1,0:T(8,128)(2,1)S(1)} %get-tuple-element.23.high_ref, ...), custom_call_target="tpu_custom_call" | custom-call | flops 157286400 | bytes 1529173 | tf_op jit(solution)/shard_map/pallas_call | solution.py:265
  (4 shorter events, 0.0 us)
Async XLA Ops:
  0.0 0.9 copy-start.2
  1.6 18.3 %all-to-all-start = ((f32[4,40,128]{2,1,0:T(8,128)}), f32[4,40,128]{2,1,0:T(8,128)S(1)}, u32[]{:S(2)}, u32[]{:S(2)}) async-start(f32[4,40,128]{2,1,0:T(8,128)} %shard_map.64), calls=%async_computation | async-start | bytes 163840 | tf_op jit(solution)/shard_map/all_to_all | solution.py:239
  8.9 0.9 copy-start.1
  9.8 10.2 %collective-permute-start = (f32[4,32,128]{2,1,0:T(8,128)S(1)}, f32[4,32,128]{2,1,0:T(8,128)S(1)}, u32[]{:S(2)}, u32[]{:S(2)}) collective-permute-start(f32[4,32,128]{2,1,0:T(8,128)S(1)} %shard_map.65.mine_ref), channel_id=1, source_target_pairs={{0,1},{1,0},{2,3},{3,2},{4,5},{5,4},{6,7},{7,6},{8,9},{9,8},{10,11... | collective-permute-start | bytes 196616 | tf_op jit(solution)/shard_map/ppermute | solution.py:237
  20.1 21.6 %collective-permute-start.1 = (f32[256,128]{1,0:T(8,128)S(1)}, f32[256,128]{1,0:T(8,128)S(1)}, u32[]{:S(2)}, u32[]{:S(2)}) collective-permute-start(f32[256,128]{1,0:T(8,128)S(1)} %get-tuple-element.15.up_ref), channel_id=1, source_target_pairs={{0,8},{8,16},{16,24},{24,0},{1,9},{9,17},{17,25},{25,1},{2,10},{10... | collective-permute-start | bytes 393224 | tf_op jit(solution)/shard_map/ppermute | solution.py:226
  31.0 17.8 %collective-permute-start.2 = (f32[256,128]{1,0:T(8,128)S(1)}, f32[256,128]{1,0:T(8,128)S(1)}, u32[]{:S(2)}, u32[]{:S(2)}) collective-permute-start(f32[256,128]{1,0:T(8,128)S(1)} %get-tuple-element.16.down_ref), channel_id=1, source_target_pairs={{0,24},{8,0},{16,8},{24,16},{1,25},{9,1},{17,9},{25,17},{2,26},{10... | collective-permute-start | bytes 393224 | tf_op jit(solution)/shard_map/ppermute | solution.py:226
  37.5 2.3 %copy-start = (f32[4,7,160,160]{3,2,1,0:T(8,128)S(1)}, f32[4,7,160,160]{3,2,1,0:T(8,128)}, u32[]{:S(2)}) copy-start(f32[4,7,160,160]{3,2,1,0:T(8,128)} %hamiltonian_ref.1) | copy-start | bytes 8601604
  39.8 0.7 copy-start.3
  41.7 13.4 %collective-permute-start.3 = (f32[112,128]{1,0:T(8,128)S(1)}, f32[112,128]{1,0:T(8,128)S(1)}, u32[]{:S(2)}, u32[]{:S(2)}) collective-permute-start(f32[112,128]{1,0:T(8,128)S(1)} %slice.6), channel_id=1, source_target_pairs={{0,8},{8,16},{16,24},{24,0},{1,9},{9,17},{17,25},{25,1},{2,10},{10... | collective-permute-start | bytes 172040 | tf_op jit(solution)/shard_map/ppermute | solution.py:226
  48.9 10.7 %collective-permute-start.4 = (f32[112,128]{1,0:T(8,128)S(1)}, f32[112,128]{1,0:T(8,128)S(1)}, u32[]{:S(2)}, u32[]{:S(2)}) collective-permute-start(f32[112,128]{1,0:T(8,128)S(1)} %slice.8), channel_id=1, source_target_pairs={{0,24},{8,0},{16,8},{24,16},{1,25},{9,1},{17,9},{25,17},{2,26},{10... | collective-permute-start | bytes 172040 | tf_op jit(solution)/shard_map/ppermute | solution.py:226
  59.6 3.2 %collective-permute-start.5 = (f32[256,128]{1,0:T(8,128)S(1)}, f32[256,128]{1,0:T(8,128)S(1)}, u32[]{:S(2)}, u32[]{:S(2)}) collective-permute-start(f32[256,128]{1,0:T(8,128)S(1)} %shard_map.68.mine_ref), channel_id=1, source_target_pairs={{0,32},{32,0},{1,33},{33,1},{2,34},{34,2},{3,35},{35,3},{4,36},{36... | collective-permute-start | bytes 393224 | tf_op jit(solution)/shard_map/ppermute | solution.py:248
  87.5 9.8 %collective-permute-start.6 = (f32[160,128]{1,0:T(8,128)S(1)}, f32[160,128]{1,0:T(8,128)S(1)}, u32[]{:S(2)}, u32[]{:S(2)}) collective-permute-start(f32[160,128]{1,0:T(8,128)S(1)} %shard_map.70.field_ref.start_ref), channel_id=1, source_target_pairs={{0,32},{32,64},{64,96},{96,128},{128,160},{160,192},{192,224},{224... | collective-permute-start | bytes 245768 | tf_op jit(solution)/shard_map/ppermute | solution.py:218
  87.6 9.8 %collective-permute-start.7 = (f32[160,128]{1,0:T(8,128)S(1)}, f32[160,128]{1,0:T(8,128)S(1)}, u32[]{:S(2)}, u32[]{:S(2)}) collective-permute-start(f32[160,128]{1,0:T(8,128)S(1)} %shard_map.70.field_ref.start_ref), channel_id=1, source_target_pairs={{0,224},{32,0},{64,32},{96,64},{128,96},{160,128},{192,160},{224,1... | collective-permute-start | bytes 245768 | tf_op jit(solution)/shard_map/ppermute | solution.py:219
  90.5 8.0 %collective-permute-start.8 = (f32[160,128]{1,0:T(8,128)S(1)}, f32[160,128]{1,0:T(8,128)S(1)}, u32[]{:S(2)}, u32[]{:S(2)}) collective-permute-start(f32[160,128]{1,0:T(8,128)S(1)} %shard_map.70.field_ref.start_ref), channel_id=1, source_target_pairs={{0,256},{256,0},{512,768},{768,512},{1,257},{257,1},{513,769},{769... | collective-permute-start | bytes 245768 | tf_op jit(solution)/shard_map/ppermute | solution.py:220
  94.1 6.3 %collective-permute-start.9 = (f32[160,128]{1,0:T(8,128)S(1)}, f32[160,128]{1,0:T(8,128)S(1)}, u32[]{:S(2)}, u32[]{:S(2)}) collective-permute-start(f32[160,128]{1,0:T(8,128)S(1)} %shard_map.70.field_ref.start_ref), channel_id=1, source_target_pairs={{256,512},{512,256},{257,513},{513,257},{258,514},{514,258},{259,5... | collective-permute-start | bytes 245768 | tf_op jit(solution)/shard_map/ppermute | solution.py:221
  100.9 6.8 %collective-permute-start.10 = (f32[160,128]{1,0:T(8,128)S(1)}, f32[160,128]{1,0:T(8,128)S(1)}, u32[]{:S(2)}, u32[]{:S(2)}) collective-permute-start(f32[160,128]{1,0:T(8,128)S(1)} %shard_map.72.field_ref.middle_ref), channel_id=1, source_target_pairs={{0,32},{32,64},{64,96},{96,128},{128,160},{160,192},{192,224},{224... | collective-permute-start | bytes 245768 | tf_op jit(solution)/shard_map/ppermute | solution.py:218
  101.0 6.8 %collective-permute-start.11 = (f32[160,128]{1,0:T(8,128)S(1)}, f32[160,128]{1,0:T(8,128)S(1)}, u32[]{:S(2)}, u32[]{:S(2)}) collective-permute-start(f32[160,128]{1,0:T(8,128)S(1)} %shard_map.72.field_ref.middle_ref), channel_id=1, source_target_pairs={{0,224},{32,0},{64,32},{96,64},{128,96},{160,128},{192,160},{224,1... | collective-permute-start | bytes 245768 | tf_op jit(solution)/shard_map/ppermute | solution.py:219
  103.9 6.3 %collective-permute-start.12 = (f32[160,128]{1,0:T(8,128)S(1)}, f32[160,128]{1,0:T(8,128)S(1)}, u32[]{:S(2)}, u32[]{:S(2)}) collective-permute-start(f32[160,128]{1,0:T(8,128)S(1)} %shard_map.72.field_ref.middle_ref), channel_id=1, source_target_pairs={{0,256},{256,0},{512,768},{768,512},{1,257},{257,1},{513,769},{769... | collective-permute-start | bytes 245768 | tf_op jit(solution)/shard_map/ppermute | solution.py:220
  105.8 6.3 %collective-permute-start.13 = (f32[160,128]{1,0:T(8,128)S(1)}, f32[160,128]{1,0:T(8,128)S(1)}, u32[]{:S(2)}, u32[]{:S(2)}) collective-permute-start(f32[160,128]{1,0:T(8,128)S(1)} %shard_map.72.field_ref.middle_ref), channel_id=1, source_target_pairs={{256,512},{512,256},{257,513},{513,257},{258,514},{514,258},{259,5... | collective-permute-start | bytes 245768 | tf_op jit(solution)/shard_map/ppermute | solution.py:221
